TPU v7x, 32 devices: a whole 2x2x4 slice. The times are simulated.
32 devices in a mesh: row: 8 (over z, y), col: 4 (over x, core).
Axes of the slice: x: 2, y: 2, z: 4, core: 2. Of those that a mesh axis runs over, the one named last changes fastest.
Arguments:
- three_index: bfloat16 [8, 4, 8, 2, 128, 128], P('row', 'col'), may hold values from -6 to 6
- slot_pair: int32 [8, 4, 8], P('row', 'col'), may hold values from -1 to 31, as said below
- coeff: bfloat16 [4096, 256], P(('col', 'row')), may hold values from -0.125 to 0.125
- occ_mask: int32 [32, 2], P('col'), may hold values 0 or 1
Outputs:
- exchange_block: bfloat16 [4096, 4096], P('row', 'col')
Inputs may be any that keep to these rules, and one draw needn't show every extreme that they name: `slot_pair`: on each device (first two dimensions) the 8 slots name distinct local pair blocks mb * 8 + nb, the live ones first and -1 after them; in every draw some device fills all 8 slots.
All inputs are finite; a program needn't handle non-finite values. No bound on the sum of `occ_mask` on one device may be relied on, other than what follows from the above.
Results may differ from a plain program's by a relative error of at most 0.0057.
Values may be sent and summed in bfloat16 or wider, within the bound.
No kernel may reach another device: no remote copies, remote signals or barrier semaphores. Data moves between devices by JAX's collectives and lax.ppermute only.
A program may use at most 64 MiB of HBM per device.

v0:
```python
import functools
import math

import jax
import jax.numpy as jnp
from jax import lax
from jax.experimental import pallas as pl
from jax.experimental.pallas import tpu as pltpu
from jax.sharding import PartitionSpec as P


VMEM = pl.BlockSpec(memory_space=pltpu.VMEM)
SMEM = pl.BlockSpec(memory_space=pltpu.SMEM)
PARAMS = pltpu.CompilerParams(vmem_limit_bytes=16 << 20)


class Layout:
    def __init__(self, n_row, n_col):
        self.n_row, self.n_col = n_row, n_col
        self.ratio = n_row // n_col
        self.groups = n_col // 4

    def permute(self, value, target):
        pairs = []
        for row in range(self.n_row):
            for col in range(self.n_col):
                plane, side, place = target(row // self.ratio, row % self.ratio, col)
                pairs.append((row * self.n_col + col, (plane * self.ratio + side) * self.n_col + place))
        return lax.ppermute(value, ("row", "col"), pairs)

    def shift(self, value, plane_bits=0, side_bits=0, col_bits=0):
        return self.permute(value, lambda z, y, w: (z ^ plane_bits, y ^ side_bits, w ^ col_bits))


def share_kernel(own_ref, next_ref, out_ref):
    part = out_ref.shape[2]
    chip = lax.axis_index("col") >> 1 & 1
    columns = pl.ds(pl.multiple_of(chip * part, part), part)
    out_ref[0] = own_ref[:, columns]
    out_ref[1] = next_ref[:, columns]


def half_kernel(kept_slots, nu_blocks, block, place_ref, own_table, next_table, own_ref, next_ref, *refs):
    pieces, (out_ref, rows_ref, held_ref, sem) = refs[:-4], refs[-4:]
    rows, part = pieces[0].shape[1:]
    aux = own_ref.shape[1]
    copy = pltpu.make_async_copy(own_ref, held_ref, sem)
    copy.start()
    occ_blocks = 2 * part // block
    for index, piece in enumerate(pieces):
        start = pl.multiple_of(place_ref[1 + index] * rows, rows)
        for inner in range(0, rows, block):
            count = min(rows, block)
            mask_row = kept_slots + (start + inner) // block * occ_blocks + place_ref[0]
            for first in range(0, part, block):
                columns = slice(first, first + min(block, part))
                for side, table in enumerate((own_table, next_table)):
                    value = piece[side, inner : inner + count, columns]
                    kept = jnp.where(table[mask_row + first // block] != 0, value, jnp.zeros_like(value))
                    rows_ref[side, pl.ds(start + inner, count), columns] = kept
    out_ref[...] = jnp.zeros_like(out_ref)

    def add(table, block_ref, side, slot):
        pair = table[slot]

        @pl.when(pair >= 0)
        def _():
            out_rows = pl.ds(pl.multiple_of(pair // nu_blocks * block, block), block)
            nu_rows = rows_ref[side, pl.ds(pl.multiple_of(pair % nu_blocks * block, block), block), :]
            for p in range(aux):
                columns = slice(p * part, (p + 1) * part)
                out_ref[out_rows, columns] += jnp.dot(
                    block_ref[slot, p], nu_rows, preferred_element_type=jnp.float32
                )

    @pl.loop(0, kept_slots)
    def _(slot):
        add(next_table, next_ref, 1, slot)

    copy.wait()

    @pl.loop(0, kept_slots)
    def _(slot):
        add(own_table, held_ref, 0, slot)


def product_kernel(n_left, scale, place_ref, *refs):
    left, right, (out_ref, left_rows, right_rows) = refs[:n_left], refs[n_left:-3], refs[-3:]
    rows = left[0].shape[0]
    for index, piece in enumerate(left + right):
        target = left_rows if index < n_left else right_rows
        start = pl.multiple_of(place_ref[2 * index + 1], rows)
        target[place_ref[2 * index], pl.ds(start, rows), :] = piece[...]
    step = math.gcd(right_rows.shape[1], 256)
    for start in range(0, right_rows.shape[1], step):
        value = sum(
            lax.dot_general(
                left_rows[chip],
                right_rows[chip, start : start + step, :],
                (((1,), (1,)), ((), ())),
                preferred_element_type=jnp.float32,
            )
            for chip in range(2)
        )
        out_ref[:, start : start + step] = (value * scale).astype(out_ref.dtype)


def exchange(three_index, slot_pair, coeff, occ_mask):
    kept_slots, aux, block = three_index.shape[2:5]
    nu_rows, occ = coeff.shape
    n_row, n_col = lax.axis_size("row"), lax.axis_size("col")
    lay = Layout(n_row, n_col)
    ratio, groups = lay.ratio, lay.groups
    mu_rows, width, part = nu_rows * n_col, aux * occ, occ // 2
    nu_blocks = nu_rows * n_row // block
    row, col = lax.axis_index("row"), lax.axis_index("col")
    plane, side, group, chip = row // ratio, row % ratio, col // 4, col // 2 % 2

    blocks = three_index.reshape(kept_slots, aux, block, block)
    table = jnp.concatenate([slot_pair.reshape(kept_slots), occ_mask.reshape(-1)])
    next_coeff = lay.shift(coeff, col_bits=2)
    next_table = lay.shift(table, col_bits=2)
    next_blocks = lay.shift(blocks, col_bits=2)
    shared = pl.pallas_call(
        share_kernel,
        out_shape=jax.ShapeDtypeStruct((2, nu_rows, part), coeff.dtype),
        in_specs=[VMEM, VMEM],
        out_specs=VMEM,
        compiler_params=PARAMS,
    )(coeff, next_coeff)

    pieces, places = [], []
    for d in range(n_col):
        here = lay.shift(shared, plane_bits=d) if d else shared
        for t in range(ratio):
            pieces.append(lay.shift(here, side_bits=t) if t else here)
            places.append((plane ^ d) * ratio + (side ^ t))
    partial = pl.pallas_call(
        functools.partial(half_kernel, kept_slots, nu_blocks, block),
        out_shape=jax.ShapeDtypeStruct((mu_rows, width // 2), jnp.float32),
        in_specs=[SMEM] * 3 + [pl.BlockSpec(memory_space=pl.ANY)] + [VMEM] * (1 + len(pieces)),
        out_specs=VMEM,
        scratch_shapes=[
            pltpu.VMEM((2, nu_blocks * block, part), coeff.dtype),
            pltpu.VMEM(blocks.shape, blocks.dtype),
            pltpu.SemaphoreType.DMA,
        ],
        compiler_params=PARAMS,
    )(jnp.stack([chip * part // block] + places), table, next_table, blocks, next_blocks, *pieces)

    total = partial + lay.shift(partial, col_bits=1)
    rows = mu_rows // groups
    if groups > 1:
        mine = [lax.dynamic_slice_in_dim(total, (group ^ e) * rows, rows, 0) for e in range(groups)]
        total = mine[0]
        for e in range(1, groups):
            total = total + lay.shift(mine[e], col_bits=4 * e)
    final = total.astype(jnp.bfloat16)

    left, right, places = [], [], []
    for e in range(2 * groups):
        left.append(lay.shift(final, col_bits=2 * e) if e else final)
        places += [(col // 2 ^ e) % 2, (col // 2 ^ e) // 2 * rows]
    for j in range(2 * groups):
        here = lay.permute(final, lambda z, y, w: (w % 2 * 2 * groups + (w // 2 ^ j), y, z))
        for t in range(ratio):
            right.append(lay.shift(here, side_bits=t) if t else here)
            source = plane % (2 * groups) ^ j
            places += [source % 2, (side ^ t) * mu_rows + source // 2 * rows]
    return pl.pallas_call(
        functools.partial(product_kernel, len(left), 1.0 / math.sqrt(width)),
        out_shape=jax.ShapeDtypeStruct((mu_rows, ratio * mu_rows), jnp.bfloat16),
        in_specs=[SMEM] + [VMEM] * (len(left) + len(right)),
        out_specs=VMEM,
        scratch_shapes=[
            pltpu.VMEM((2, mu_rows, width // 2), jnp.bfloat16),
            pltpu.VMEM((2, ratio * mu_rows, width // 2), jnp.bfloat16),
        ],
        compiler_params=PARAMS,
    )(jnp.stack(places), *left, *right)


def solution(mesh):
    return jax.shard_map(
        exchange,
        mesh=mesh,
        in_specs=(
            P("row", "col", None, None, None, None),
            P("row", "col", None),
            P(("col", "row"), None),
            P("col", None),
        ),
        out_specs=P("row", "col"),
        check_vma=False,
    )
```

profile of v0, /device:TPU:2, one launch (start us, length us, event | category | flops | bytes accessed | tf_op | source)
XLA Modules:
  0.0 64.3 jit_solution(11716760551271147772)
XLA Ops:
  0.0 0.0 copy-start.2
  0.0 0.0 collective-permute-start.1
  0.0 2.0 %collective-permute-start.2 = (bf16[128,256]{1,0:T(8,128)(2,1)}, bf16[128,256]{1,0:T(8,128)(2,1)S(1)}, u32[]{:S(2)}, u32[]{:S(2)}) collective-permute-start(bf16[128,256]{1,0:T(8,128)(2,1)} %own_ref.1), channel_id=1, source_target_pairs={{0,2},{1,3},{2,0},{3,1},{4,6},{5,7},{6,4},{7,5},{8,10},{9,11},{10,... | collective-permute-start | bytes 196616 | tf_op jit(solution)/shard_map/ppermute | solution.py:29
  2.0 0.0 copy-done.2
  2.0 0.1 copy.6
  2.1 0.1 reshape.10
  2.2 13.1 %collective-permute-done.2.next_ref = bf16[128,256]{1,0:T(8,128)(2,1)S(1)} collective-permute-done((bf16[128,256]{1,0:T(8,128)(2,1)}, bf16[128,256]{1,0:T(8,128)(2,1)S(1)}, u32[]{:S(2)}, u32[]{:S(2)}) %collective-permute-start.2) | collective-permute-done | bytes 65568 | tf_op jit(solution)/shard_map/ppermute | solution.py:29
  15.3 0.0 copy-start.1
  15.3 0.8 %copy-done.1 = bf16[128,256]{1,0:T(8,128)(2,1)S(1)} copy-done((bf16[128,256]{1,0:T(8,128)(2,1)S(1)}, bf16[128,256]{1,0:T(8,128)(2,1)}, u32[]{:S(2)}) %copy-start.1) | copy-done | bytes 65560
  16.1 0.0 copy-start.3
  16.1 3.7 %collective-permute-start.8 = (bf16[2,128,128]{2,1,0:T(8,128)(2,1)S(1)}, bf16[2,128,128]{2,1,0:T(8,128)(2,1)S(1)}, u32[]{:S(2)}, u32[]{:S(2)}) collective-permute-start(bf16[2,128,128]{2,1,0:T(8,128)(2,1)S(1)} %shard_map.46.refs_0_), channel_id=1, source_target_pairs={{0,24},{1,25},{2,26},{3,27},{4,28},{5,29},{6,30},{7,31},{8,16},{9,... | collective-permute-start | bytes 196616 | tf_op jit(solution)/shard_map/ppermute | solution.py:29
  19.8 0.0 collective-permute-start.6
  19.8 0.8 %collective-permute-start.4 = (bf16[2,128,128]{2,1,0:T(8,128)(2,1)S(1)}, bf16[2,128,128]{2,1,0:T(8,128)(2,1)S(1)}, u32[]{:S(2)}, u32[]{:S(2)}) collective-permute-start(bf16[2,128,128]{2,1,0:T(8,128)(2,1)S(1)} %shard_map.46.refs_0_), channel_id=1, source_target_pairs={{0,8},{1,9},{2,10},{3,11},{4,12},{5,13},{6,14},{7,15},{8,0},{9,1},... | collective-permute-start | bytes 196616 | tf_op jit(solution)/shard_map/ppermute | solution.py:29
  20.6 0.0 copy-done.3
  20.6 0.1 pad_add_fusion.own_table
  20.7 0.4 collective-permute-start
  21.1 3.2 %collective-permute-done.next_table = s32[24]{0:T(128)S(1)} collective-permute-done((s32[24]{0:T(128)S(1)}, s32[24]{0:T(128)S(1)}, u32[]{:S(2)}, u32[]{:S(2)}) %collective-permute-start) | collective-permute-done | bytes 128 | tf_op jit(solution)/shard_map/ppermute | solution.py:29
  24.3 1.5 %collective-permute-start.3 = (bf16[2,128,128]{2,1,0:T(8,128)(2,1)S(1)}, bf16[2,128,128]{2,1,0:T(8,128)(2,1)S(1)}, u32[]{:S(2)}, u32[]{:S(2)}) collective-permute-start(bf16[2,128,128]{2,1,0:T(8,128)(2,1)S(1)} %shard_map.46.refs_0_), channel_id=1, source_target_pairs={{0,4},{1,5},{2,6},{3,7},{4,0},{5,1},{6,2},{7,3},{8,12},{9,13},{10,... | collective-permute-start | bytes 196616 | tf_op jit(solution)/shard_map/ppermute | solution.py:29
  25.8 0.0 collective-permute-done.8.refs_6_
  25.8 0.5 collective-permute-start.9
  26.3 0.0 collective-permute-done.6.refs_4_
  26.3 1.5 %collective-permute-start.7 = (bf16[2,128,128]{2,1,0:T(8,128)(2,1)S(1)}, bf16[2,128,128]{2,1,0:T(8,128)(2,1)S(1)}, u32[]{:S(2)}, u32[]{:S(2)}) collective-permute-start(bf16[2,128,128]{2,1,0:T(8,128)(2,1)S(1)} %collective-permute-done.6.refs_4_), channel_id=1, source_target_pairs={{0,4},{1,5},{2,6},{3,7},{4,0},{5,1},{6,2},{7,3},{8,12},{9,13},{10,... | collective-permute-start | bytes 196616 | tf_op jit(solution)/shard_map/ppermute | solution.py:29
  27.8 0.0 collective-permute-done.4.refs_2_
  27.8 0.5 collective-permute-start.5
  28.3 0.1 stack.85.place_ref
  28.4 0.6 collective-permute-done.3.refs_1_
  29.0 1.0 %collective-permute-done.9.refs_7_ = bf16[2,128,128]{2,1,0:T(8,128)(2,1)S(1)} collective-permute-done((bf16[2,128,128]{2,1,0:T(8,128)(2,1)S(1)}, bf16[2,128,128]{2,1,0:T(8,128)(2,1)S(1)}, u32[]{:S(2)}, u32[]{:S(2)}) %collective-permute-start.9) | collective-permute-done | bytes 65568 | tf_op jit(solution)/shard_map/ppermute | solution.py:29
  30.0 0.7 %collective-permute-done.7.refs_5_ = bf16[2,128,128]{2,1,0:T(8,128)(2,1)S(1)} collective-permute-done((bf16[2,128,128]{2,1,0:T(8,128)(2,1)S(1)}, bf16[2,128,128]{2,1,0:T(8,128)(2,1)S(1)}, u32[]{:S(2)}, u32[]{:S(2)}) %collective-permute-start.7) | collective-permute-done | bytes 65568 | tf_op jit(solution)/shard_map/ppermute | solution.py:29
  30.7 1.3 %collective-permute-done.5.refs_3_ = bf16[2,128,128]{2,1,0:T(8,128)(2,1)S(1)} collective-permute-done((bf16[2,128,128]{2,1,0:T(8,128)(2,1)S(1)}, bf16[2,128,128]{2,1,0:T(8,128)(2,1)S(1)}, u32[]{:S(2)}, u32[]{:S(2)}) %collective-permute-start.5) | collective-permute-done | bytes 65568 | tf_op jit(solution)/shard_map/ppermute | solution.py:29
  32.1 0.0 collective-permute-done.1.next_ref
  32.1 0.0 copy-start
  32.1 1.0 %copy-done = bf16[1,1,8,2,128,128]{5,4,3,2,1,0:T(8,128)(2,1)S(1)} copy-done((bf16[1,1,8,2,128,128]{5,4,3,2,1,0:T(8,128)(2,1)S(1)}, bf16[1,1,8,2,128,128]{5,4,3,2,1,0:T(8,128)(2,1)}, u32[]{:S(2)}) %copy-start) | copy-done | bytes 524312
  33.1 2.6 %shard_map.47 = f32[512,256]{1,0:T(8,128)S(1)} custom-call(s32[9]{0:T(128)S(1)} %stack.85.place_ref, s32[24]{0:T(128)S(1)} %pad_add_fusion.own_table, s32[24]{0:T(128)S(1)} %collective-permute-done.next_table, bf16[8,2,128,128]{3,2,1,0:T(8,128)(2,1)S(1)} %bitcast.22, bf16[8,2,128,128]{3,2,1,0:T(8,128)(2,1)S(1)} %collective-permute-done.1.next_ref, ...), custom_call_target="tpu_custom_call" | custom-call | tf_op jit(solution)/shard_map/pallas_call | solution.py:138
  35.7 0.1 collective-permute-start.10
  35.8 1.9 %collective-permute-done.10 = f32[512,256]{1,0:T(8,128)S(1)} collective-permute-done((f32[512,256]{1,0:T(8,128)S(1)}, f32[512,256]{1,0:T(8,128)S(1)}, u32[]{:S(2)}, u32[]{:S(2)}) %collective-permute-start.10) | collective-permute-done | bytes 524320 | tf_op jit(solution)/shard_map/ppermute | solution.py:29
  37.7 0.1 add_convert_fusion.refs_0_
  37.8 0.6 collective-permute-start.14
  38.4 1.9 %collective-permute-start.12 = (bf16[512,256]{1,0:T(8,128)(2,1)S(1)}, bf16[512,256]{1,0:T(8,128)(2,1)S(1)}, u32[]{:S(2)}, u32[]{:S(2)}) collective-permute-start(bf16[512,256]{1,0:T(8,128)(2,1)S(1)} %add_convert_fusion.refs_0_), channel_id=1, source_target_pairs={{0,0},{1,16},{2,8},{3,24},{4,4},{5,20},{6,12},{7,28},{8,1},{9,17},... | collective-permute-start | bytes 786440 | tf_op jit(solution)/shard_map/ppermute | solution.py:29
  40.3 0.1 collective-permute-start.11
  40.4 10.4 %collective-permute-done.14.refs_4_ = bf16[512,256]{1,0:T(8,128)(2,1)S(1)} collective-permute-done((bf16[512,256]{1,0:T(8,128)(2,1)S(1)}, bf16[512,256]{1,0:T(8,128)(2,1)S(1)}, u32[]{:S(2)}, u32[]{:S(2)}) %collective-permute-start.14) | collective-permute-done | bytes 262176 | tf_op jit(solution)/shard_map/ppermute | solution.py:29
  50.8 0.0 collective-permute-start.15
  50.8 2.5 %collective-permute-done.12.refs_2_ = bf16[512,256]{1,0:T(8,128)(2,1)S(1)} collective-permute-done((bf16[512,256]{1,0:T(8,128)(2,1)S(1)}, bf16[512,256]{1,0:T(8,128)(2,1)S(1)}, u32[]{:S(2)}, u32[]{:S(2)}) %collective-permute-start.12) | collective-permute-done | bytes 262176 | tf_op jit(solution)/shard_map/ppermute | solution.py:29
  53.3 0.7 %collective-permute-start.13 = (bf16[512,256]{1,0:T(8,128)(2,1)S(1)}, bf16[512,256]{1,0:T(8,128)(2,1)S(1)}, u32[]{:S(2)}, u32[]{:S(2)}) collective-permute-start(bf16[512,256]{1,0:T(8,128)(2,1)S(1)} %collective-permute-done.12.refs_2_), channel_id=1, source_target_pairs={{0,4},{1,5},{2,6},{3,7},{4,0},{5,1},{6,2},{7,3},{8,12},{9,13},{10,... | collective-permute-start | bytes 786440 | tf_op jit(solution)/shard_map/ppermute | solution.py:29
  54.0 0.1 stack.75.place_ref
  54.1 0.0 collective-permute-done.11.refs_1_
  54.1 5.1 %collective-permute-done.15.refs_5_ = bf16[512,256]{1,0:T(8,128)(2,1)S(1)} collective-permute-done((bf16[512,256]{1,0:T(8,128)(2,1)S(1)}, bf16[512,256]{1,0:T(8,128)(2,1)S(1)}, u32[]{:S(2)}, u32[]{:S(2)}) %collective-permute-start.15) | collective-permute-done | bytes 262176 | tf_op jit(solution)/shard_map/ppermute | solution.py:29
  59.2 2.8 %collective-permute-done.13.refs_3_ = bf16[512,256]{1,0:T(8,128)(2,1)S(1)} collective-permute-done((bf16[512,256]{1,0:T(8,128)(2,1)S(1)}, bf16[512,256]{1,0:T(8,128)(2,1)S(1)}, u32[]{:S(2)}, u32[]{:S(2)}) %collective-permute-start.13) | collective-permute-done | bytes 262176 | tf_op jit(solution)/shard_map/ppermute | solution.py:29
  62.0 2.3 %shard_map.48 = bf16[512,1024]{1,0:T(8,128)(2,1)} custom-call(s32[12]{0:T(128)S(1)} %stack.75.place_ref, bf16[512,256]{1,0:T(8,128)(2,1)S(1)} %add_convert_fusion.refs_0_, bf16[512,256]{1,0:T(8,128)(2,1)S(1)} %collective-permute-done.11.refs_1_, bf16[512,256]{1,0:T(8,128)(2,1)S(1)} %collective-permute-done.12.refs_2_, ...), custom_call_target="tpu_custom_call" | custom-call | tf_op jit(solution)/shard_map/pallas_call | solution.py:170
  (1 shorter events, 0.0 us)
Async XLA Ops:
  0.0 2.0 %copy-start.2 = (s32[8,2]{0,1:T(2,128)S(1)}, s32[8,2]{0,1:T(2,128)}, u32[]{:S(2)}) copy-start(s32[8,2]{0,1:T(2,128)} %param.7) | copy-start | bytes 196
  0.0 32.1 %collective-permute-start.1 = (bf16[8,2,128,128]{3,2,1,0:T(8,128)(2,1)}, bf16[8,2,128,128]{3,2,1,0:T(8,128)(2,1)S(1)}, u32[]{:S(2)}, u32[]{:S(2)}) collective-permute-start(bf16[8,2,128,128]{3,2,1,0:T(8,128)(2,1)} %bitcast.21), channel_id=1, source_target_pairs={{0,2},{1,3},{2,0},{3,1},{4,6},{5,7},{6,4},{7,5},{8,10},{9,11},{10,... | collective-permute-start | bytes 1572872 | tf_op jit(solution)/shard_map/ppermute | solution.py:29
  0.0 15.3 %collective-permute-start.2 = (bf16[128,256]{1,0:T(8,128)(2,1)}, bf16[128,256]{1,0:T(8,128)(2,1)S(1)}, u32[]{:S(2)}, u32[]{:S(2)}) collective-permute-start(bf16[128,256]{1,0:T(8,128)(2,1)} %own_ref.1), channel_id=1, source_target_pairs={{0,2},{1,3},{2,0},{3,1},{4,6},{5,7},{6,4},{7,5},{8,10},{9,11},{10,... | collective-permute-start | bytes 196616 | tf_op jit(solution)/shard_map/ppermute | solution.py:29
  15.3 0.8 %copy-start.1 = (bf16[128,256]{1,0:T(8,128)(2,1)S(1)}, bf16[128,256]{1,0:T(8,128)(2,1)}, u32[]{:S(2)}) copy-start(bf16[128,256]{1,0:T(8,128)(2,1)} %own_ref.1) | copy-start | bytes 196612
  16.1 4.5 %copy-start.3 = (s32[1,1,8]{2,1,0:T(1,128)S(1)}, s32[1,1,8]{2,1,0:T(1,128)}, u32[]{:S(2)}) copy-start(s32[1,1,8]{2,1,0:T(1,128)} %param.5) | copy-start | bytes 100
  16.1 9.6 %collective-permute-start.8 = (bf16[2,128,128]{2,1,0:T(8,128)(2,1)S(1)}, bf16[2,128,128]{2,1,0:T(8,128)(2,1)S(1)}, u32[]{:S(2)}, u32[]{:S(2)}) collective-permute-start(bf16[2,128,128]{2,1,0:T(8,128)(2,1)S(1)} %shard_map.46.refs_0_), channel_id=1, source_target_pairs={{0,24},{1,25},{2,26},{3,27},{4,28},{5,29},{6,30},{7,31},{8,16},{9,... | collective-permute-start | bytes 196616 | tf_op jit(solution)/shard_map/ppermute | solution.py:29
  19.8 6.5 %collective-permute-start.6 = (bf16[2,128,128]{2,1,0:T(8,128)(2,1)S(1)}, bf16[2,128,128]{2,1,0:T(8,128)(2,1)S(1)}, u32[]{:S(2)}, u32[]{:S(2)}) collective-permute-start(bf16[2,128,128]{2,1,0:T(8,128)(2,1)S(1)} %shard_map.46.refs_0_), channel_id=1, source_target_pairs={{0,16},{1,17},{2,18},{3,19},{4,20},{5,21},{6,22},{7,23},{8,24},{9,... | collective-permute-start | bytes 196616 | tf_op jit(solution)/shard_map/ppermute | solution.py:29
  19.8 8.0 %collective-permute-start.4 = (bf16[2,128,128]{2,1,0:T(8,128)(2,1)S(1)}, bf16[2,128,128]{2,1,0:T(8,128)(2,1)S(1)}, u32[]{:S(2)}, u32[]{:S(2)}) collective-permute-start(bf16[2,128,128]{2,1,0:T(8,128)(2,1)S(1)} %shard_map.46.refs_0_), channel_id=1, source_target_pairs={{0,8},{1,9},{2,10},{3,11},{4,12},{5,13},{6,14},{7,15},{8,0},{9,1},... | collective-permute-start | bytes 196616 | tf_op jit(solution)/shard_map/ppermute | solution.py:29
  20.7 3.6 %collective-permute-start = (s32[24]{0:T(128)S(1)}, s32[24]{0:T(128)S(1)}, u32[]{:S(2)}, u32[]{:S(2)}) collective-permute-start(s32[24]{0:T(128)S(1)} %pad_add_fusion.own_table), channel_id=1, source_target_pairs={{0,2},{1,3},{2,0},{3,1},{4,6},{5,7},{6,4},{7,5},{8,10},{9,11},{10,... | collective-permute-start | bytes 296 | tf_op jit(solution)/shard_map/ppermute | solution.py:29
  24.3 4.7 %collective-permute-start.3 = (bf16[2,128,128]{2,1,0:T(8,128)(2,1)S(1)}, bf16[2,128,128]{2,1,0:T(8,128)(2,1)S(1)}, u32[]{:S(2)}, u32[]{:S(2)}) collective-permute-start(bf16[2,128,128]{2,1,0:T(8,128)(2,1)S(1)} %shard_map.46.refs_0_), channel_id=1, source_target_pairs={{0,4},{1,5},{2,6},{3,7},{4,0},{5,1},{6,2},{7,3},{8,12},{9,13},{10,... | collective-permute-start | bytes 196616 | tf_op jit(solution)/shard_map/ppermute | solution.py:29
  25.8 4.3 %collective-permute-start.9 = (bf16[2,128,128]{2,1,0:T(8,128)(2,1)S(1)}, bf16[2,128,128]{2,1,0:T(8,128)(2,1)S(1)}, u32[]{:S(2)}, u32[]{:S(2)}) collective-permute-start(bf16[2,128,128]{2,1,0:T(8,128)(2,1)S(1)} %collective-permute-done.8.refs_6_), channel_id=1, source_target_pairs={{0,4},{1,5},{2,6},{3,7},{4,0},{5,1},{6,2},{7,3},{8,12},{9,13},{10,... | collective-permute-start | bytes 196616 | tf_op jit(solution)/shard_map/ppermute | solution.py:29
  26.3 4.5 %collective-permute-start.7 = (bf16[2,128,128]{2,1,0:T(8,128)(2,1)S(1)}, bf16[2,128,128]{2,1,0:T(8,128)(2,1)S(1)}, u32[]{:S(2)}, u32[]{:S(2)}) collective-permute-start(bf16[2,128,128]{2,1,0:T(8,128)(2,1)S(1)} %collective-permute-done.6.refs_4_), channel_id=1, source_target_pairs={{0,4},{1,5},{2,6},{3,7},{4,0},{5,1},{6,2},{7,3},{8,12},{9,13},{10,... | collective-permute-start | bytes 196616 | tf_op jit(solution)/shard_map/ppermute | solution.py:29
  27.8 4.3 %collective-permute-start.5 = (bf16[2,128,128]{2,1,0:T(8,128)(2,1)S(1)}, bf16[2,128,128]{2,1,0:T(8,128)(2,1)S(1)}, u32[]{:S(2)}, u32[]{:S(2)}) collective-permute-start(bf16[2,128,128]{2,1,0:T(8,128)(2,1)S(1)} %collective-permute-done.4.refs_2_), channel_id=1, source_target_pairs={{0,4},{1,5},{2,6},{3,7},{4,0},{5,1},{6,2},{7,3},{8,12},{9,13},{10,... | collective-permute-start | bytes 196616 | tf_op jit(solution)/shard_map/ppermute | solution.py:29
  32.1 1.0 %copy-start = (bf16[1,1,8,2,128,128]{5,4,3,2,1,0:T(8,128)(2,1)S(1)}, bf16[1,1,8,2,128,128]{5,4,3,2,1,0:T(8,128)(2,1)}, u32[]{:S(2)}) copy-start(bf16[1,1,8,2,128,128]{5,4,3,2,1,0:T(8,128)(2,1)} %param.4) | copy-start | bytes 1572868
  35.7 2.0 %collective-permute-start.10 = (f32[512,256]{1,0:T(8,128)S(1)}, f32[512,256]{1,0:T(8,128)S(1)}, u32[]{:S(2)}, u32[]{:S(2)}) collective-permute-start(f32[512,256]{1,0:T(8,128)S(1)} %shard_map.47), channel_id=1, source_target_pairs={{0,1},{1,0},{2,3},{3,2},{4,5},{5,4},{6,7},{7,6},{8,9},{9,8},{10,11... | collective-permute-start | bytes 1572872 | tf_op jit(solution)/shard_map/ppermute | solution.py:29
  37.8 13.0 %collective-permute-start.14 = (bf16[512,256]{1,0:T(8,128)(2,1)S(1)}, bf16[512,256]{1,0:T(8,128)(2,1)S(1)}, u32[]{:S(2)}, u32[]{:S(2)}) collective-permute-start(bf16[512,256]{1,0:T(8,128)(2,1)S(1)} %add_convert_fusion.refs_0_), channel_id=1, source_target_pairs={{0,8},{1,24},{2,0},{3,16},{4,12},{5,28},{6,4},{7,20},{8,9},{9,25},... | collective-permute-start | bytes 786440 | tf_op jit(solution)/shard_map/ppermute | solution.py:29
  38.4 14.9 %collective-permute-start.12 = (bf16[512,256]{1,0:T(8,128)(2,1)S(1)}, bf16[512,256]{1,0:T(8,128)(2,1)S(1)}, u32[]{:S(2)}, u32[]{:S(2)}) collective-permute-start(bf16[512,256]{1,0:T(8,128)(2,1)S(1)} %add_convert_fusion.refs_0_), channel_id=1, source_target_pairs={{0,0},{1,16},{2,8},{3,24},{4,4},{5,20},{6,12},{7,28},{8,1},{9,17},... | collective-permute-start | bytes 786440 | tf_op jit(solution)/shard_map/ppermute | solution.py:29
  40.3 13.8 %collective-permute-start.11 = (bf16[512,256]{1,0:T(8,128)(2,1)S(1)}, bf16[512,256]{1,0:T(8,128)(2,1)S(1)}, u32[]{:S(2)}, u32[]{:S(2)}) collective-permute-start(bf16[512,256]{1,0:T(8,128)(2,1)S(1)} %add_convert_fusion.refs_0_), channel_id=1, source_target_pairs={{0,2},{1,3},{2,0},{3,1},{4,6},{5,7},{6,4},{7,5},{8,10},{9,11},{10,... | collective-permute-start | bytes 786440 | tf_op jit(solution)/shard_map/ppermute | solution.py:29
  50.8 8.4 %collective-permute-start.15 = (bf16[512,256]{1,0:T(8,128)(2,1)S(1)}, bf16[512,256]{1,0:T(8,128)(2,1)S(1)}, u32[]{:S(2)}, u32[]{:S(2)}) collective-permute-start(bf16[512,256]{1,0:T(8,128)(2,1)S(1)} %collective-permute-done.14.refs_4_), channel_id=1, source_target_pairs={{0,4},{1,5},{2,6},{3,7},{4,0},{5,1},{6,2},{7,3},{8,12},{9,13},{10,... | collective-permute-start | bytes 786440 | tf_op jit(solution)/shard_map/ppermute | solution.py:29
  53.3 8.7 %collective-permute-start.13 = (bf16[512,256]{1,0:T(8,128)(2,1)S(1)}, bf16[512,256]{1,0:T(8,128)(2,1)S(1)}, u32[]{:S(2)}, u32[]{:S(2)}) collective-permute-start(bf16[512,256]{1,0:T(8,128)(2,1)S(1)} %collective-permute-done.12.refs_2_), channel_id=1, source_target_pairs={{0,4},{1,5},{2,6},{3,7},{4,0},{5,1},{6,2},{7,3},{8,12},{9,13},{10,... | collective-permute-start | bytes 786440 | tf_op jit(solution)/shard_map/ppermute | solution.py:29
where the time goes:
time: 64.6 us; the launch traced here: 64.3 us
  waiting for transfers between devices  42.7 us (66%)
  starting transfers between devices  14.3 us (22%)
  Pallas kernels  4.92 us (8%)
  local copies, waits for them, and re-layouts  2.22 us (3%)
    ppermute x16, waiting for transfers between devices, permute(): return lax.ppermute(value, ('row', 'col'), pairs)  42.7 us
    ppermute x16, starting transfers between devices, permute(): return lax.ppermute(value, ('row', 'col'), pairs)  14.3 us
    pallas_call x1, Pallas kernels, exchange(): pl.pallas_call(functools.partial(half_kernel, kept_slots, nu_blocks, bloc...  2.58 us
    pallas_call x1, Pallas kernels, exchange(): pl.pallas_call(functools.partial(product_kernel, len(left), 1.0 / math.sq...  2.33 us
    unnamed x9, local copies, waits for them, and re-layouts  1.97 us
  transfers between devices with their start and end apart: 16, of which 11 were waited for; matrix products, arithmetic and copies ran while one was open for 1% of the time, Pallas kernels for 0%

commit v1 on v0

--- a/solution.py
+++ b/solution.py
@@ -32,12 +32,17 @@
         return self.permute(value, lambda z, y, w: (z ^ plane_bits, y ^ side_bits, w ^ col_bits))
 
 
-def share_kernel(own_ref, next_ref, out_ref):
-    part = out_ref.shape[2]
+def chip_half(ref, part):
     chip = lax.axis_index("col") >> 1 & 1
-    columns = pl.ds(pl.multiple_of(chip * part, part), part)
-    out_ref[0] = own_ref[:, columns]
-    out_ref[1] = next_ref[:, columns]
+    return ref[:, pl.ds(pl.multiple_of(chip * part, part), part)]
+
+
+def own_kernel(own_ref, out_ref):
+    out_ref[0] = chip_half(own_ref, out_ref.shape[2])
+
+
+def next_kernel(next_ref, held_ref, out_ref):
+    out_ref[1] = chip_half(next_ref, out_ref.shape[2])
 
 
 def half_kernel(kept_slots, nu_blocks, block, place_ref, own_table, next_table, own_ref, next_ref, *refs):
@@ -85,24 +90,31 @@
 
 
 def product_kernel(n_left, scale, place_ref, *refs):
-    left, right, (out_ref, left_rows, right_rows) = refs[:n_left], refs[n_left:-3], refs[-3:]
+    left, right = refs[:n_left], refs[n_left : 2 * n_left]
+    out_ref, left_rows, right_rows, tiles, sems = refs[-5:]
     rows = left[0].shape[0]
-    for index, piece in enumerate(left + right):
-        target = left_rows if index < n_left else right_rows
-        start = pl.multiple_of(place_ref[2 * index + 1], rows)
-        target[place_ref[2 * index], pl.ds(start, rows), :] = piece[...]
-    step = math.gcd(right_rows.shape[1], 256)
-    for start in range(0, right_rows.shape[1], step):
+    for index in range(n_left):
+        for base, pieces, held in ((1, left, left_rows), (1 + 2 * n_left, right, right_rows)):
+            start = pl.multiple_of(place_ref[base + 2 * index + 1], rows)
+            held[place_ref[base + 2 * index], pl.ds(start, rows), :] = pieces[index][...]
+    width = tiles.shape[2]
+    copies = []
+    for tile in range(tiles.shape[0]):
         value = sum(
             lax.dot_general(
                 left_rows[chip],
-                right_rows[chip, start : start + step, :],
+                right_rows[chip, tile * width : (tile + 1) * width, :],
                 (((1,), (1,)), ((), ())),
                 preferred_element_type=jnp.float32,
             )
             for chip in range(2)
         )
-        out_ref[:, start : start + step] = (value * scale).astype(out_ref.dtype)
+        tiles[tile] = (value * scale).astype(tiles.dtype)
+        first = pl.multiple_of(place_ref[0] + tile * width, width)
+        copies.append(pltpu.make_async_copy(tiles.at[tile], out_ref.at[:, pl.ds(first, width)], sems.at[tile]))
+        copies[-1].start()
+    for copy in copies:
+        copy.wait()
 
 
 def exchange(three_index, slot_pair, coeff, occ_mask):
@@ -122,12 +134,20 @@
     next_table = lay.shift(table, col_bits=2)
     next_blocks = lay.shift(blocks, col_bits=2)
     shared = pl.pallas_call(
-        share_kernel,
+        own_kernel,
+        out_shape=jax.ShapeDtypeStruct((2, nu_rows, part), coeff.dtype),
+        in_specs=[VMEM],
+        out_specs=VMEM,
+        compiler_params=PARAMS,
+    )(coeff)
+    shared = pl.pallas_call(
+        next_kernel,
         out_shape=jax.ShapeDtypeStruct((2, nu_rows, part), coeff.dtype),
         in_specs=[VMEM, VMEM],
         out_specs=VMEM,
+        input_output_aliases={1: 0},
         compiler_params=PARAMS,
-    )(coeff, next_coeff)
+    )(next_coeff, shared)
 
     pieces, places = [], []
     for d in range(n_col):
@@ -138,7 +158,7 @@
     partial = pl.pallas_call(
         functools.partial(half_kernel, kept_slots, nu_blocks, block),
         out_shape=jax.ShapeDtypeStruct((mu_rows, width // 2), jnp.float32),
-        in_specs=[SMEM] * 3 + [pl.BlockSpec(memory_space=pl.ANY)] + [VMEM] * (1 + len(pieces)),
+        in_specs=[SMEM] * 3 + [pl.BlockSpec(memory_space=pltpu.HBM)] + [VMEM] * (1 + len(pieces)),
         out_specs=VMEM,
         scratch_shapes=[
             pltpu.VMEM((2, nu_blocks * block, part), coeff.dtype),
@@ -157,27 +177,35 @@
             total = total + lay.shift(mine[e], col_bits=4 * e)
     final = total.astype(jnp.bfloat16)
 
-    left, right, places = [], [], []
-    for e in range(2 * groups):
+    pieces = 2 * groups
+    left, left_places = [], []
+    for e in range(pieces):
         left.append(lay.shift(final, col_bits=2 * e) if e else final)
-        places += [(col // 2 ^ e) % 2, (col // 2 ^ e) // 2 * rows]
-    for j in range(2 * groups):
-        here = lay.permute(final, lambda z, y, w: (w % 2 * 2 * groups + (w // 2 ^ j), y, z))
-        for t in range(ratio):
-            right.append(lay.shift(here, side_bits=t) if t else here)
-            source = plane % (2 * groups) ^ j
-            places += [source % 2, (side ^ t) * mu_rows + source // 2 * rows]
-    return pl.pallas_call(
-        functools.partial(product_kernel, len(left), 1.0 / math.sqrt(width)),
-        out_shape=jax.ShapeDtypeStruct((mu_rows, ratio * mu_rows), jnp.bfloat16),
-        in_specs=[SMEM] + [VMEM] * (len(left) + len(right)),
-        out_specs=VMEM,
-        scratch_shapes=[
-            pltpu.VMEM((2, mu_rows, width // 2), jnp.bfloat16),
-            pltpu.VMEM((2, ratio * mu_rows, width // 2), jnp.bfloat16),
-        ],
-        compiler_params=PARAMS,
-    )(jnp.stack(places), *left, *right)
+        left_places += [(col // 2 ^ e) % 2, (col // 2 ^ e) // 2 * rows]
+    sources = [lay.permute(final, lambda z, y, w: (w % 2 * pieces + (w // 2 ^ j), y, z)) for j in range(pieces)]
+    source_places = []
+    for j in range(pieces):
+        source_places += [(plane % pieces ^ j) % 2, (plane % pieces ^ j) // 2 * rows]
+
+    out = ()
+    columns = math.gcd(mu_rows, 256)
+    for t in range(ratio):
+        right = [lay.shift(piece, side_bits=t) if t else piece for piece in sources]
+        out = pl.pallas_call(
+            functools.partial(product_kernel, pieces, 1.0 / math.sqrt(width)),
+            out_shape=(jax.ShapeDtypeStruct((mu_rows, ratio * mu_rows), jnp.bfloat16),),
+            in_specs=[SMEM] + [VMEM] * (2 * pieces) + [pl.BlockSpec(memory_space=pltpu.HBM)] * len(out),
+            out_specs=(pl.BlockSpec(memory_space=pltpu.HBM),),
+            input_output_aliases={1 + 2 * pieces: 0} if out else {},
+            scratch_shapes=[
+                pltpu.VMEM((2, mu_rows, width // 2), jnp.bfloat16),
+                pltpu.VMEM((2, mu_rows, width // 2), jnp.bfloat16),
+                pltpu.VMEM((mu_rows // columns, mu_rows, columns), jnp.bfloat16),
+                pltpu.SemaphoreType.DMA((mu_rows // columns,)),
+            ],
+            compiler_params=PARAMS,
+        )(jnp.stack([(side ^ t) * mu_rows] + left_places + source_places), *left, *right, *out)
+    return out[0]
 
 
 def solution(mesh):

time: 64.6 us -> 62.8 us (0.972)
  waiting for transfers between devices: 42.7 us -> 39.2 us
  Pallas kernels: 4.92 us -> 6.31 us
  other arithmetic: 0.18 us -> 0.83 us
    ppermute x16, waiting for transfers between devices: 42.7 us -> 39.2 us  [permute(): return lax.ppermute(value, ('row', 'col'), pairs)]
    pallas_call x2 -> x4, Pallas kernels: 2.34 us -> 3.73 us  [the longest x2 3.72 us: exchange(): pl.pallas_call(functools.partial(product_kernel, pieces, 1.0 / math.sqrt(...]
    concatenate x1, other arithmetic: 0.07 us -> 0.73 us  [exchange(): jnp.concatenate([slot_pair.reshape(kept_slots), occ_mask.reshape(-1)])]
    unnamed x9 -> x5, local copies, waits for them, and re-layouts: 1.97 us -> 1.63 us
  transfers between devices with their start and end apart: 16 -> 16, of which waited for: 11 -> 11; matrix products, arithmetic and copies ran while one was open for 1% -> 3% of each run, Pallas kernels for 0% -> 3%
where the time goes in v1:
time: 62.8 us; the launch traced here: 62.6 us
  waiting for transfers between devices  39.2 us (62%)
  starting transfers between devices  14.2 us (23%)
  Pallas kernels  6.31 us (10%)
  local copies, waits for them, and re-layouts  1.96 us (3%)
  other arithmetic  0.83 us (1%)
    ppermute x16, waiting for transfers between devices, permute(): return lax.ppermute(value, ('row', 'col'), pairs)  39.2 us
    ppermute x16, starting transfers between devices, permute(): return lax.ppermute(value, ('row', 'col'), pairs)  14.2 us
    pallas_call x2, Pallas kernels, exchange(): pl.pallas_call(functools.partial(product_kernel, pieces, 1.0 / math.sqrt(...  3.72 us
    pallas_call x1, Pallas kernels, exchange(): pl.pallas_call(functools.partial(half_kernel, kept_slots, nu_blocks, bloc...  2.58 us
    unnamed x5, local copies, waits for them, and re-layouts  1.63 us
  transfers between devices with their start and end apart: 16, of which 11 were waited for; matrix products, arithmetic and copies ran while one was open for 3% of the time, Pallas kernels for 3%

profile of v1, /device:TPU:2, one launch (start us, length us, event | category | flops | bytes accessed | tf_op | source)
XLA Modules:
  0.0 62.6 jit_solution(16087778778720323517)
XLA Ops:
  0.0 0.0 copy-start
  0.0 0.0 collective-permute-start.1
  0.0 2.0 %collective-permute-start.2 = (bf16[128,256]{1,0:T(8,128)(2,1)}, bf16[128,256]{1,0:T(8,128)(2,1)S(1)}, u32[]{:S(2)}, u32[]{:S(2)}) collective-permute-start(bf16[128,256]{1,0:T(8,128)(2,1)} %own_ref.1), channel_id=1, source_target_pairs={{0,2},{1,3},{2,0},{3,1},{4,6},{5,7},{6,4},{7,5},{8,10},{9,11},{10,... | collective-permute-start | bytes 196616 | tf_op jit(solution)/shard_map/ppermute | solution.py:29
  2.0 0.0 copy-start.1
  2.0 0.9 %copy-done.1 = bf16[128,256]{1,0:T(8,128)(2,1)S(1)} copy-done((bf16[128,256]{1,0:T(8,128)(2,1)S(1)}, bf16[128,256]{1,0:T(8,128)(2,1)}, u32[]{:S(2)}) %copy-start.1) | copy-done | bytes 65560
  2.9 0.8 %copy.8 = s32[8,2]{1,0:T(8,128)S(1)} copy(s32[8,2]{0,1:T(2,128)} %param.7) | data formatting | bytes 128 | tf_op args[3]
  3.7 0.1 reshape.10
  3.7 11.5 %collective-permute-done.2.next_ref = bf16[128,256]{1,0:T(8,128)(2,1)S(1)} collective-permute-done((bf16[128,256]{1,0:T(8,128)(2,1)}, bf16[128,256]{1,0:T(8,128)(2,1)S(1)}, u32[]{:S(2)}, u32[]{:S(2)}) %collective-permute-start.2) | collective-permute-done | bytes 65568 | tf_op jit(solution)/shard_map/ppermute | solution.py:29
  15.3 3.6 %collective-permute-start.8 = (bf16[2,128,128]{2,1,0:T(8,128)(2,1)S(1)}, bf16[2,128,128]{2,1,0:T(8,128)(2,1)S(1)}, u32[]{:S(2)}, u32[]{:S(2)}) collective-permute-start(bf16[2,128,128]{2,1,0:T(8,128)(2,1)S(1)} %shard_map.47.refs_0_), channel_id=1, source_target_pairs={{0,24},{1,25},{2,26},{3,27},{4,28},{5,29},{6,30},{7,31},{8,16},{9,... | collective-permute-start | bytes 196616 | tf_op jit(solution)/shard_map/ppermute | solution.py:29
  18.9 0.0 collective-permute-start.6
  18.9 0.8 %collective-permute-start.4 = (bf16[2,128,128]{2,1,0:T(8,128)(2,1)S(1)}, bf16[2,128,128]{2,1,0:T(8,128)(2,1)S(1)}, u32[]{:S(2)}, u32[]{:S(2)}) collective-permute-start(bf16[2,128,128]{2,1,0:T(8,128)(2,1)S(1)} %shard_map.47.refs_0_), channel_id=1, source_target_pairs={{0,8},{1,9},{2,10},{3,11},{4,12},{5,13},{6,14},{7,15},{8,0},{9,1},... | collective-permute-start | bytes 196616 | tf_op jit(solution)/shard_map/ppermute | solution.py:29
  19.7 0.7 %pad_add_fusion.own_table = s32[24]{0:T(128)S(1)} fusion(s32[16]{0:T(128)S(1)} %reshape.10, s32[8]{0:T(128)} %bitcast.23), kind=kLoop, calls=%fused_computation.1 | loop fusion | flops 24 | bytes 192 | tf_op jit(solution)/shard_map/concatenate | solution.py:132
  20.4 0.4 collective-permute-start
  20.8 3.2 %collective-permute-done.next_table = s32[24]{0:T(128)S(1)} collective-permute-done((s32[24]{0:T(128)S(1)}, s32[24]{0:T(128)S(1)}, u32[]{:S(2)}, u32[]{:S(2)}) %collective-permute-start) | collective-permute-done | bytes 128 | tf_op jit(solution)/shard_map/ppermute | solution.py:29
  24.0 1.5 %collective-permute-start.3 = (bf16[2,128,128]{2,1,0:T(8,128)(2,1)S(1)}, bf16[2,128,128]{2,1,0:T(8,128)(2,1)S(1)}, u32[]{:S(2)}, u32[]{:S(2)}) collective-permute-start(bf16[2,128,128]{2,1,0:T(8,128)(2,1)S(1)} %shard_map.47.refs_0_), channel_id=1, source_target_pairs={{0,4},{1,5},{2,6},{3,7},{4,0},{5,1},{6,2},{7,3},{8,12},{9,13},{10,... | collective-permute-start | bytes 196616 | tf_op jit(solution)/shard_map/ppermute | solution.py:29
  25.5 0.0 collective-permute-done.8.refs_6_
  25.5 0.5 collective-permute-start.9
  26.0 0.0 collective-permute-done.6.refs_4_
  26.0 1.5 %collective-permute-start.7 = (bf16[2,128,128]{2,1,0:T(8,128)(2,1)S(1)}, bf16[2,128,128]{2,1,0:T(8,128)(2,1)S(1)}, u32[]{:S(2)}, u32[]{:S(2)}) collective-permute-start(bf16[2,128,128]{2,1,0:T(8,128)(2,1)S(1)} %collective-permute-done.6.refs_4_), channel_id=1, source_target_pairs={{0,4},{1,5},{2,6},{3,7},{4,0},{5,1},{6,2},{7,3},{8,12},{9,13},{10,... | collective-permute-start | bytes 196616 | tf_op jit(solution)/shard_map/ppermute | solution.py:29
  27.5 0.0 collective-permute-done.4.refs_2_
  27.5 0.5 collective-permute-start.5
  28.0 0.1 stack.93.place_ref
  28.1 0.1 collective-permute-done.3.refs_1_
  28.2 1.5 %collective-permute-done.9.refs_7_ = bf16[2,128,128]{2,1,0:T(8,128)(2,1)S(1)} collective-permute-done((bf16[2,128,128]{2,1,0:T(8,128)(2,1)S(1)}, bf16[2,128,128]{2,1,0:T(8,128)(2,1)S(1)}, u32[]{:S(2)}, u32[]{:S(2)}) %collective-permute-start.9) | collective-permute-done | bytes 65568 | tf_op jit(solution)/shard_map/ppermute | solution.py:29
  29.8 0.7 %collective-permute-done.7.refs_5_ = bf16[2,128,128]{2,1,0:T(8,128)(2,1)S(1)} collective-permute-done((bf16[2,128,128]{2,1,0:T(8,128)(2,1)S(1)}, bf16[2,128,128]{2,1,0:T(8,128)(2,1)S(1)}, u32[]{:S(2)}, u32[]{:S(2)}) %collective-permute-start.7) | collective-permute-done | bytes 65568 | tf_op jit(solution)/shard_map/ppermute | solution.py:29
  30.5 1.3 %collective-permute-done.5.refs_3_ = bf16[2,128,128]{2,1,0:T(8,128)(2,1)S(1)} collective-permute-done((bf16[2,128,128]{2,1,0:T(8,128)(2,1)S(1)}, bf16[2,128,128]{2,1,0:T(8,128)(2,1)S(1)}, u32[]{:S(2)}, u32[]{:S(2)}) %collective-permute-start.5) | collective-permute-done | bytes 65568 | tf_op jit(solution)/shard_map/ppermute | solution.py:29
  31.8 0.0 collective-permute-done.1.next_ref
  31.8 0.0 copy-done
  31.8 2.6 %shard_map.48 = f32[512,256]{1,0:T(8,128)S(1)} custom-call(s32[9]{0:T(128)S(1)} %stack.93.place_ref, s32[24]{0:T(128)S(1)} %pad_add_fusion.own_table, s32[24]{0:T(128)S(1)} %collective-permute-done.next_table, bf16[8,2,128,128]{3,2,1,0:T(8,128)(2,1)S(1)} %bitcast.22, bf16[8,2,128,128]{3,2,1,0:T(8,128)(2,1)S(1)} %collective-permute-done.1.next_ref, ...), custom_call_target="tpu_custom_call" | custom-call | tf_op jit(solution)/shard_map/pallas_call | solution.py:158
  34.4 0.1 collective-permute-start.10
  34.5 1.9 %collective-permute-done.10 = f32[512,256]{1,0:T(8,128)S(1)} collective-permute-done((f32[512,256]{1,0:T(8,128)S(1)}, f32[512,256]{1,0:T(8,128)S(1)}, u32[]{:S(2)}, u32[]{:S(2)}) %collective-permute-start.10) | collective-permute-done | bytes 524320 | tf_op jit(solution)/shard_map/ppermute | solution.py:29
  36.4 0.1 add_convert_fusion.refs_0_
  36.5 0.6 collective-permute-start.14
  37.1 1.9 %collective-permute-start.12 = (bf16[512,256]{1,0:T(8,128)(2,1)S(1)}, bf16[512,256]{1,0:T(8,128)(2,1)S(1)}, u32[]{:S(2)}, u32[]{:S(2)}) collective-permute-start(bf16[512,256]{1,0:T(8,128)(2,1)S(1)} %add_convert_fusion.refs_0_), channel_id=1, source_target_pairs={{0,0},{1,16},{2,8},{3,24},{4,4},{5,20},{6,12},{7,28},{8,1},{9,17},... | collective-permute-start | bytes 786440 | tf_op jit(solution)/shard_map/ppermute | solution.py:29
  39.0 0.1 collective-permute-start.11
  39.0 10.4 %collective-permute-done.14.refs_3_ = bf16[512,256]{1,0:T(8,128)(2,1)S(1)} collective-permute-done((bf16[512,256]{1,0:T(8,128)(2,1)S(1)}, bf16[512,256]{1,0:T(8,128)(2,1)S(1)}, u32[]{:S(2)}, u32[]{:S(2)}) %collective-permute-start.14) | collective-permute-done | bytes 262176 | tf_op jit(solution)/shard_map/ppermute | solution.py:29
  49.5 0.0 collective-permute-start.15
  49.5 2.5 %collective-permute-done.12.refs_2_ = bf16[512,256]{1,0:T(8,128)(2,1)S(1)} collective-permute-done((bf16[512,256]{1,0:T(8,128)(2,1)S(1)}, bf16[512,256]{1,0:T(8,128)(2,1)S(1)}, u32[]{:S(2)}, u32[]{:S(2)}) %collective-permute-start.12) | collective-permute-done | bytes 262176 | tf_op jit(solution)/shard_map/ppermute | solution.py:29
  52.0 0.7 %collective-permute-start.13 = (bf16[512,256]{1,0:T(8,128)(2,1)S(1)}, bf16[512,256]{1,0:T(8,128)(2,1)S(1)}, u32[]{:S(2)}, u32[]{:S(2)}) collective-permute-start(bf16[512,256]{1,0:T(8,128)(2,1)S(1)} %collective-permute-done.12.refs_2_), channel_id=1, source_target_pairs={{0,4},{1,5},{2,6},{3,7},{4,0},{5,1},{6,2},{7,3},{8,12},{9,13},{10,... | collective-permute-start | bytes 786440 | tf_op jit(solution)/shard_map/ppermute | solution.py:29
  52.7 0.1 stack.83.place_ref
  52.8 0.1 stack.95.place_ref
  52.8 0.0 collective-permute-done.11.refs_1_
  52.9 1.9 %shard_map.49.refs_4_ = bf16[512,1024]{1,0:T(8,128)(2,1)} custom-call(s32[9]{0:T(128)S(1)} %stack.95.place_ref, bf16[512,256]{1,0:T(8,128)(2,1)S(1)} %add_convert_fusion.refs_0_, bf16[512,256]{1,0:T(8,128)(2,1)S(1)} %collective-permute-done.11.refs_1_, bf16[512,256]{1,0:T(8,128)(2,1)S(1)} %collective-permute-done.12.refs_2_, ...), custom_call_target="tpu_custom_call" | custom-call | tf_op jit(solution)/shard_map/pallas_call | solution.py:194
  54.7 3.2 %collective-permute-done.15.refs_3_ = bf16[512,256]{1,0:T(8,128)(2,1)S(1)} collective-permute-done((bf16[512,256]{1,0:T(8,128)(2,1)S(1)}, bf16[512,256]{1,0:T(8,128)(2,1)S(1)}, u32[]{:S(2)}, u32[]{:S(2)}) %collective-permute-start.15) | collective-permute-done | bytes 262176 | tf_op jit(solution)/shard_map/ppermute | solution.py:29
  57.9 2.8 %collective-permute-done.13.refs_2_ = bf16[512,256]{1,0:T(8,128)(2,1)S(1)} collective-permute-done((bf16[512,256]{1,0:T(8,128)(2,1)S(1)}, bf16[512,256]{1,0:T(8,128)(2,1)S(1)}, u32[]{:S(2)}, u32[]{:S(2)}) %collective-permute-start.13) | collective-permute-done | bytes 262176 | tf_op jit(solution)/shard_map/ppermute | solution.py:29
  60.7 1.9 %shard_map.50 = bf16[512,1024]{1,0:T(8,128)(2,1)} custom-call(s32[9]{0:T(128)S(1)} %stack.83.place_ref, bf16[512,256]{1,0:T(8,128)(2,1)S(1)} %add_convert_fusion.refs_0_, bf16[512,256]{1,0:T(8,128)(2,1)S(1)} %collective-permute-done.11.refs_1_, bf16[512,256]{1,0:T(8,128)(2,1)S(1)} %collective-permute-done.13.refs_2_, ...), custom_call_target="tpu_custom_call", output_to_operand_aliasing={{}: (5, {})} | custom-call | tf_op jit(solution)/shard_map/pallas_call | solution.py:194
  (2 shorter events, 0.0 us)
Async XLA Ops:
  0.0 31.8 %copy-start = (bf16[1,1,8,2,128,128]{5,4,3,2,1,0:T(8,128)(2,1)S(1)}, bf16[1,1,8,2,128,128]{5,4,3,2,1,0:T(8,128)(2,1)}, u32[]{:S(2)}) copy-start(bf16[1,1,8,2,128,128]{5,4,3,2,1,0:T(8,128)(2,1)} %param.4) | copy-start | bytes 1572868
  0.0 31.8 %collective-permute-start.1 = (bf16[8,2,128,128]{3,2,1,0:T(8,128)(2,1)}, bf16[8,2,128,128]{3,2,1,0:T(8,128)(2,1)S(1)}, u32[]{:S(2)}, u32[]{:S(2)}) collective-permute-start(bf16[8,2,128,128]{3,2,1,0:T(8,128)(2,1)} %bitcast.21), channel_id=1, source_target_pairs={{0,2},{1,3},{2,0},{3,1},{4,6},{5,7},{6,4},{7,5},{8,10},{9,11},{10,... | collective-permute-start | bytes 1572872 | tf_op jit(solution)/shard_map/ppermute | solution.py:29
  0.0 15.3 %collective-permute-start.2 = (bf16[128,256]{1,0:T(8,128)(2,1)}, bf16[128,256]{1,0:T(8,128)(2,1)S(1)}, u32[]{:S(2)}, u32[]{:S(2)}) collective-permute-start(bf16[128,256]{1,0:T(8,128)(2,1)} %own_ref.1), channel_id=1, source_target_pairs={{0,2},{1,3},{2,0},{3,1},{4,6},{5,7},{6,4},{7,5},{8,10},{9,11},{10,... | collective-permute-start | bytes 196616 | tf_op jit(solution)/shard_map/ppermute | solution.py:29
  2.0 0.9 %copy-start.1 = (bf16[128,256]{1,0:T(8,128)(2,1)S(1)}, bf16[128,256]{1,0:T(8,128)(2,1)}, u32[]{:S(2)}) copy-start(bf16[128,256]{1,0:T(8,128)(2,1)} %own_ref.1) | copy-start | bytes 196612
  15.3 10.2 %collective-permute-start.8 = (bf16[2,128,128]{2,1,0:T(8,128)(2,1)S(1)}, bf16[2,128,128]{2,1,0:T(8,128)(2,1)S(1)}, u32[]{:S(2)}, u32[]{:S(2)}) collective-permute-start(bf16[2,128,128]{2,1,0:T(8,128)(2,1)S(1)} %shard_map.47.refs_0_), channel_id=1, source_target_pairs={{0,24},{1,25},{2,26},{3,27},{4,28},{5,29},{6,30},{7,31},{8,16},{9,... | collective-permute-start | bytes 196616 | tf_op jit(solution)/shard_map/ppermute | solution.py:29
  18.9 7.1 %collective-permute-start.6 = (bf16[2,128,128]{2,1,0:T(8,128)(2,1)S(1)}, bf16[2,128,128]{2,1,0:T(8,128)(2,1)S(1)}, u32[]{:S(2)}, u32[]{:S(2)}) collective-permute-start(bf16[2,128,128]{2,1,0:T(8,128)(2,1)S(1)} %shard_map.47.refs_0_), channel_id=1, source_target_pairs={{0,16},{1,17},{2,18},{3,19},{4,20},{5,21},{6,22},{7,23},{8,24},{9,... | collective-permute-start | bytes 196616 | tf_op jit(solution)/shard_map/ppermute | solution.py:29
  18.9 8.6 %collective-permute-start.4 = (bf16[2,128,128]{2,1,0:T(8,128)(2,1)S(1)}, bf16[2,128,128]{2,1,0:T(8,128)(2,1)S(1)}, u32[]{:S(2)}, u32[]{:S(2)}) collective-permute-start(bf16[2,128,128]{2,1,0:T(8,128)(2,1)S(1)} %shard_map.47.refs_0_), channel_id=1, source_target_pairs={{0,8},{1,9},{2,10},{3,11},{4,12},{5,13},{6,14},{7,15},{8,0},{9,1},... | collective-permute-start | bytes 196616 | tf_op jit(solution)/shard_map/ppermute | solution.py:29
  20.4 3.6 %collective-permute-start = (s32[24]{0:T(128)S(1)}, s32[24]{0:T(128)S(1)}, u32[]{:S(2)}, u32[]{:S(2)}) collective-permute-start(s32[24]{0:T(128)S(1)} %pad_add_fusion.own_table), channel_id=1, source_target_pairs={{0,2},{1,3},{2,0},{3,1},{4,6},{5,7},{6,4},{7,5},{8,10},{9,11},{10,... | collective-permute-start | bytes 296 | tf_op jit(solution)/shard_map/ppermute | solution.py:29
  24.0 4.3 %collective-permute-start.3 = (bf16[2,128,128]{2,1,0:T(8,128)(2,1)S(1)}, bf16[2,128,128]{2,1,0:T(8,128)(2,1)S(1)}, u32[]{:S(2)}, u32[]{:S(2)}) collective-permute-start(bf16[2,128,128]{2,1,0:T(8,128)(2,1)S(1)} %shard_map.47.refs_0_), channel_id=1, source_target_pairs={{0,4},{1,5},{2,6},{3,7},{4,0},{5,1},{6,2},{7,3},{8,12},{9,13},{10,... | collective-permute-start | bytes 196616 | tf_op jit(solution)/shard_map/ppermute | solution.py:29
  25.5 4.3 %collective-permute-start.9 = (bf16[2,128,128]{2,1,0:T(8,128)(2,1)S(1)}, bf16[2,128,128]{2,1,0:T(8,128)(2,1)S(1)}, u32[]{:S(2)}, u32[]{:S(2)}) collective-permute-start(bf16[2,128,128]{2,1,0:T(8,128)(2,1)S(1)} %collective-permute-done.8.refs_6_), channel_id=1, source_target_pairs={{0,4},{1,5},{2,6},{3,7},{4,0},{5,1},{6,2},{7,3},{8,12},{9,13},{10,... | collective-permute-start | bytes 196616 | tf_op jit(solution)/shard_map/ppermute | solution.py:29
  26.0 4.5 %collective-permute-start.7 = (bf16[2,128,128]{2,1,0:T(8,128)(2,1)S(1)}, bf16[2,128,128]{2,1,0:T(8,128)(2,1)S(1)}, u32[]{:S(2)}, u32[]{:S(2)}) collective-permute-start(bf16[2,128,128]{2,1,0:T(8,128)(2,1)S(1)} %collective-permute-done.6.refs_4_), channel_id=1, source_target_pairs={{0,4},{1,5},{2,6},{3,7},{4,0},{5,1},{6,2},{7,3},{8,12},{9,13},{10,... | collective-permute-start | bytes 196616 | tf_op jit(solution)/shard_map/ppermute | solution.py:29
  27.5 4.3 %collective-permute-start.5 = (bf16[2,128,128]{2,1,0:T(8,128)(2,1)S(1)}, bf16[2,128,128]{2,1,0:T(8,128)(2,1)S(1)}, u32[]{:S(2)}, u32[]{:S(2)}) collective-permute-start(bf16[2,128,128]{2,1,0:T(8,128)(2,1)S(1)} %collective-permute-done.4.refs_2_), channel_id=1, source_target_pairs={{0,4},{1,5},{2,6},{3,7},{4,0},{5,1},{6,2},{7,3},{8,12},{9,13},{10,... | collective-permute-start | bytes 196616 | tf_op jit(solution)/shard_map/ppermute | solution.py:29
  34.4 2.0 %collective-permute-start.10 = (f32[512,256]{1,0:T(8,128)S(1)}, f32[512,256]{1,0:T(8,128)S(1)}, u32[]{:S(2)}, u32[]{:S(2)}) collective-permute-start(f32[512,256]{1,0:T(8,128)S(1)} %shard_map.48), channel_id=1, source_target_pairs={{0,1},{1,0},{2,3},{3,2},{4,5},{5,4},{6,7},{7,6},{8,9},{9,8},{10,11... | collective-permute-start | bytes 1572872 | tf_op jit(solution)/shard_map/ppermute | solution.py:29
  36.5 13.0 %collective-permute-start.14 = (bf16[512,256]{1,0:T(8,128)(2,1)S(1)}, bf16[512,256]{1,0:T(8,128)(2,1)S(1)}, u32[]{:S(2)}, u32[]{:S(2)}) collective-permute-start(bf16[512,256]{1,0:T(8,128)(2,1)S(1)} %add_convert_fusion.refs_0_), channel_id=1, source_target_pairs={{0,8},{1,24},{2,0},{3,16},{4,12},{5,28},{6,4},{7,20},{8,9},{9,25},... | collective-permute-start | bytes 786440 | tf_op jit(solution)/shard_map/ppermute | solution.py:29
  37.1 14.9 %collective-permute-start.12 = (bf16[512,256]{1,0:T(8,128)(2,1)S(1)}, bf16[512,256]{1,0:T(8,128)(2,1)S(1)}, u32[]{:S(2)}, u32[]{:S(2)}) collective-permute-start(bf16[512,256]{1,0:T(8,128)(2,1)S(1)} %add_convert_fusion.refs_0_), channel_id=1, source_target_pairs={{0,0},{1,16},{2,8},{3,24},{4,4},{5,20},{6,12},{7,28},{8,1},{9,17},... | collective-permute-start | bytes 786440 | tf_op jit(solution)/shard_map/ppermute | solution.py:29
  39.0 13.9 %collective-permute-start.11 = (bf16[512,256]{1,0:T(8,128)(2,1)S(1)}, bf16[512,256]{1,0:T(8,128)(2,1)S(1)}, u32[]{:S(2)}, u32[]{:S(2)}) collective-permute-start(bf16[512,256]{1,0:T(8,128)(2,1)S(1)} %add_convert_fusion.refs_0_), channel_id=1, source_target_pairs={{0,2},{1,3},{2,0},{3,1},{4,6},{5,7},{6,4},{7,5},{8,10},{9,11},{10,... | collective-permute-start | bytes 786440 | tf_op jit(solution)/shard_map/ppermute | solution.py:29
  49.5 8.4 %collective-permute-start.15 = (bf16[512,256]{1,0:T(8,128)(2,1)S(1)}, bf16[512,256]{1,0:T(8,128)(2,1)S(1)}, u32[]{:S(2)}, u32[]{:S(2)}) collective-permute-start(bf16[512,256]{1,0:T(8,128)(2,1)S(1)} %collective-permute-done.14.refs_3_), channel_id=1, source_target_pairs={{0,4},{1,5},{2,6},{3,7},{4,0},{5,1},{6,2},{7,3},{8,12},{9,13},{10,... | collective-permute-start | bytes 786440 | tf_op jit(solution)/shard_map/ppermute | solution.py:29
  52.0 8.7 %collective-permute-start.13 = (bf16[512,256]{1,0:T(8,128)(2,1)S(1)}, bf16[512,256]{1,0:T(8,128)(2,1)S(1)}, u32[]{:S(2)}, u32[]{:S(2)}) collective-permute-start(bf16[512,256]{1,0:T(8,128)(2,1)S(1)} %collective-permute-done.12.refs_2_), channel_id=1, source_target_pairs={{0,4},{1,5},{2,6},{3,7},{4,0},{5,1},{6,2},{7,3},{8,12},{9,13},{10,... | collective-permute-start | bytes 786440 | tf_op jit(solution)/shard_map/ppermute | solution.py:29

commit v2 on v1

--- a/solution.py
+++ b/solution.py
@@ -10,6 +10,7 @@
 
 
 VMEM = pl.BlockSpec(memory_space=pltpu.VMEM)
+HBM = pl.BlockSpec(memory_space=pltpu.HBM)
 SMEM = pl.BlockSpec(memory_space=pltpu.SMEM)
 PARAMS = pltpu.CompilerParams(vmem_limit_bytes=16 << 20)
 
@@ -37,36 +38,43 @@
     return ref[:, pl.ds(pl.multiple_of(chip * part, part), part)]
 
 
-def own_kernel(own_ref, out_ref):
-    out_ref[0] = chip_half(own_ref, out_ref.shape[2])
+def own_kernel(coeff_ref, blocks_ref, out_ref, held_ref, coeff_held, sems):
+    copies = [
+        pltpu.make_async_copy(coeff_ref, coeff_held, sems.at[0]),
+        pltpu.make_async_copy(blocks_ref, held_ref, sems.at[1]),
+    ]
+    for copy in copies:
+        copy.start()
+    copies[0].wait()
+    out_ref[0] = chip_half(coeff_held, out_ref.shape[2])
+    copies[1].wait()
 
 
 def next_kernel(next_ref, held_ref, out_ref):
     out_ref[1] = chip_half(next_ref, out_ref.shape[2])
 
 
-def half_kernel(kept_slots, nu_blocks, block, place_ref, own_table, next_table, own_ref, next_ref, *refs):
-    pieces, (out_ref, rows_ref, held_ref, sem) = refs[:-4], refs[-4:]
+def half_kernel(
+    kept_slots, nu_blocks, block, place_ref, own_slots, next_slots, own_mask, next_mask, own_ref, next_ref, *refs
+):
+    pieces, (out_ref, rows_ref) = refs[:-2], refs[-2:]
     rows, part = pieces[0].shape[1:]
     aux = own_ref.shape[1]
-    copy = pltpu.make_async_copy(own_ref, held_ref, sem)
-    copy.start()
-    occ_blocks = 2 * part // block
     for index, piece in enumerate(pieces):
         start = pl.multiple_of(place_ref[1 + index] * rows, rows)
         for inner in range(0, rows, block):
             count = min(rows, block)
-            mask_row = kept_slots + (start + inner) // block * occ_blocks + place_ref[0]
+            nu_block = (start + inner) // block
             for first in range(0, part, block):
                 columns = slice(first, first + min(block, part))
-                for side, table in enumerate((own_table, next_table)):
+                for side, mask in enumerate((own_mask, next_mask)):
                     value = piece[side, inner : inner + count, columns]
-                    kept = jnp.where(table[mask_row + first // block] != 0, value, jnp.zeros_like(value))
+                    kept = jnp.where(mask[place_ref[0] + first // block, nu_block] != 0, value, jnp.zeros_like(value))
                     rows_ref[side, pl.ds(start + inner, count), columns] = kept
     out_ref[...] = jnp.zeros_like(out_ref)
 
-    def add(table, block_ref, side, slot):
-        pair = table[slot]
+    def add(slots, block_ref, side, slot):
+        pair = slots[slot]
 
         @pl.when(pair >= 0)
         def _():
@@ -80,13 +88,8 @@
 
     @pl.loop(0, kept_slots)
     def _(slot):
-        add(next_table, next_ref, 1, slot)
-
-    copy.wait()
-
-    @pl.loop(0, kept_slots)
-    def _(slot):
-        add(own_table, held_ref, 0, slot)
+        add(own_slots, own_ref, 0, slot)
+        add(next_slots, next_ref, 1, slot)
 
 
 def product_kernel(n_left, scale, place_ref, *refs):
@@ -129,17 +132,22 @@
     plane, side, group, chip = row // ratio, row % ratio, col // 4, col // 2 % 2
 
     blocks = three_index.reshape(kept_slots, aux, block, block)
-    table = jnp.concatenate([slot_pair.reshape(kept_slots), occ_mask.reshape(-1)])
+    slots, mask = slot_pair.reshape(kept_slots), occ_mask.T
     next_coeff = lay.shift(coeff, col_bits=2)
-    next_table = lay.shift(table, col_bits=2)
+    next_slots = lay.shift(slots, col_bits=2)
+    next_mask = lay.shift(mask, col_bits=2)
     next_blocks = lay.shift(blocks, col_bits=2)
-    shared = pl.pallas_call(
+    shared, blocks = pl.pallas_call(
         own_kernel,
-        out_shape=jax.ShapeDtypeStruct((2, nu_rows, part), coeff.dtype),
-        in_specs=[VMEM],
-        out_specs=VMEM,
+        out_shape=(
+            jax.ShapeDtypeStruct((2, nu_rows, part), coeff.dtype),
+            jax.ShapeDtypeStruct(blocks.shape, blocks.dtype),
+        ),
+        in_specs=[HBM, HBM],
+        out_specs=(VMEM, VMEM),
+        scratch_shapes=[pltpu.VMEM(coeff.shape, coeff.dtype), pltpu.SemaphoreType.DMA((2,))],
         compiler_params=PARAMS,
-    )(coeff)
+    )(coeff, blocks)
     shared = pl.pallas_call(
         next_kernel,
         out_shape=jax.ShapeDtypeStruct((2, nu_rows, part), coeff.dtype),
@@ -158,15 +166,11 @@
     partial = pl.pallas_call(
         functools.partial(half_kernel, kept_slots, nu_blocks, block),
         out_shape=jax.ShapeDtypeStruct((mu_rows, width // 2), jnp.float32),
-        in_specs=[SMEM] * 3 + [pl.BlockSpec(memory_space=pltpu.HBM)] + [VMEM] * (1 + len(pieces)),
+        in_specs=[SMEM] * 5 + [VMEM] * (2 + len(pieces)),
         out_specs=VMEM,
-        scratch_shapes=[
-            pltpu.VMEM((2, nu_blocks * block, part), coeff.dtype),
-            pltpu.VMEM(blocks.shape, blocks.dtype),
-            pltpu.SemaphoreType.DMA,
-        ],
+        scratch_shapes=[pltpu.VMEM((2, nu_blocks * block, part), coeff.dtype)],
         compiler_params=PARAMS,
-    )(jnp.stack([chip * part // block] + places), table, next_table, blocks, next_blocks, *pieces)
+    )(jnp.stack([chip * part // block] + places), slots, next_slots, mask, next_mask, blocks, next_blocks, *pieces)
 
     total = partial + lay.shift(partial, col_bits=1)
     rows = mu_rows // groups
@@ -194,8 +198,8 @@
         out = pl.pallas_call(
             functools.partial(product_kernel, pieces, 1.0 / math.sqrt(width)),
             out_shape=(jax.ShapeDtypeStruct((mu_rows, ratio * mu_rows), jnp.bfloat16),),
-            in_specs=[SMEM] + [VMEM] * (2 * pieces) + [pl.BlockSpec(memory_space=pltpu.HBM)] * len(out),
-            out_specs=(pl.BlockSpec(memory_space=pltpu.HBM),),
+            in_specs=[SMEM] + [VMEM] * (2 * pieces) + [HBM] * len(out),
+            out_specs=(HBM,),
             input_output_aliases={1 + 2 * pieces: 0} if out else {},
             scratch_shapes=[
                 pltpu.VMEM((2, mu_rows, width // 2), jnp.bfloat16),

time: 62.8 us -> 65.6 us (1.045)
  waiting for transfers between devices: 39.2 us -> 42.1 us
  other arithmetic: 0.83 us -> 0.07 us
    ppermute x16 -> x17, waiting for transfers between devices: 39.2 us -> 42.1 us  [permute(): return lax.ppermute(value, ('row', 'col'), pairs)]
    concatenate x1 -> x0, other arithmetic: 0.73 us -> none  [exchange(): jnp.concatenate([slot_pair.reshape(kept_slots), occ_mask.reshape(-1)])]
    ppermute x16 -> x17, starting transfers between devices: 14.2 us -> 14.7 us  [permute(): return lax.ppermute(value, ('row', 'col'), pairs)]
    unnamed x5 -> x8, local copies, waits for them, and re-layouts: 1.63 us -> 1.89 us
  transfers between devices with their start and end apart: 16 -> 17, of which waited for: 11 -> 12; matrix products, arithmetic and copies ran while one was open for 3% -> 0% of each run, Pallas kernels for 3% -> 3%
where the time goes in v2:
time: 65.6 us; the launch traced here: 65.4 us
  waiting for transfers between devices  42.1 us (64%)
  starting transfers between devices  14.7 us (22%)
  Pallas kernels  6.37 us (10%)
  local copies, waits for them, and re-layouts  2.14 us (3%)
    ppermute x17, waiting for transfers between devices, permute(): return lax.ppermute(value, ('row', 'col'), pairs)  42.1 us
    ppermute x17, starting transfers between devices, permute(): return lax.ppermute(value, ('row', 'col'), pairs)  14.7 us
    pallas_call x2, Pallas kernels, exchange(): pl.pallas_call(functools.partial(product_kernel, pieces, 1.0 / math.sqrt(...  3.72 us
    pallas_call x1, Pallas kernels, exchange(): pl.pallas_call(functools.partial(half_kernel, kept_slots, nu_blocks, bloc...  2.52 us
    unnamed x8, local copies, waits for them, and re-layouts  1.89 us
  transfers between devices with their start and end apart: 17, of which 12 were waited for; matrix products, arithmetic and copies ran while one was open for 0% of the time, Pallas kernels for 3%

profile of v2, /device:TPU:2, one launch (start us, length us, event | category | flops | bytes accessed | tf_op | source)
XLA Modules:
  0.0 65.4 jit_solution(15477907844341250901)
XLA Ops:
  0.0 0.0 collective-permute-start.2
  0.0 2.0 %collective-permute-start.3 = (bf16[128,256]{1,0:T(8,128)(2,1)}, bf16[128,256]{1,0:T(8,128)(2,1)S(1)}, u32[]{:S(2)}, u32[]{:S(2)}) collective-permute-start(bf16[128,256]{1,0:T(8,128)(2,1)} %coeff_ref.1), channel_id=1, source_target_pairs={{0,2},{1,3},{2,0},{3,1},{4,6},{5,7},{6,4},{7,5},{8,10},{9,11},{10,... | collective-permute-start | bytes 196616 | tf_op jit(solution)/shard_map/ppermute | solution.py:30
  2.0 0.0 copy-start
  2.0 1.0 %copy-done = bf16[1,1,8,2,128,128]{5,4,3,2,1,0:T(8,128)(2,1)S(1)} copy-done((bf16[1,1,8,2,128,128]{5,4,3,2,1,0:T(8,128)(2,1)S(1)}, bf16[1,1,8,2,128,128]{5,4,3,2,1,0:T(8,128)(2,1)}, u32[]{:S(2)}) %copy-start) | copy-done | bytes 524312
  3.1 0.0 copy-start.1
  3.1 0.8 %copy-done.1 = bf16[128,256]{1,0:T(8,128)(2,1)S(1)} copy-done((bf16[128,256]{1,0:T(8,128)(2,1)S(1)}, bf16[128,256]{1,0:T(8,128)(2,1)}, u32[]{:S(2)}) %copy-start.1) | copy-done | bytes 65560
  3.9 0.1 shard_map.46
  4.0 11.2 %collective-permute-done.3.next_ref = bf16[128,256]{1,0:T(8,128)(2,1)S(1)} collective-permute-done((bf16[128,256]{1,0:T(8,128)(2,1)}, bf16[128,256]{1,0:T(8,128)(2,1)S(1)}, u32[]{:S(2)}, u32[]{:S(2)}) %collective-permute-start.3) | collective-permute-done | bytes 65568 | tf_op jit(solution)/shard_map/ppermute | solution.py:30
  15.3 0.0 copy-start.3
  15.3 3.7 %collective-permute-start.9 = (bf16[2,128,128]{2,1,0:T(8,128)(2,1)S(1)}, bf16[2,128,128]{2,1,0:T(8,128)(2,1)S(1)}, u32[]{:S(2)}, u32[]{:S(2)}) collective-permute-start(bf16[2,128,128]{2,1,0:T(8,128)(2,1)S(1)} %shard_map.47.refs_0_), channel_id=1, source_target_pairs={{0,24},{1,25},{2,26},{3,27},{4,28},{5,29},{6,30},{7,31},{8,16},{9,... | collective-permute-start | bytes 196616 | tf_op jit(solution)/shard_map/ppermute | solution.py:30
  19.0 0.0 collective-permute-start.7
  19.0 0.8 %collective-permute-start.5 = (bf16[2,128,128]{2,1,0:T(8,128)(2,1)S(1)}, bf16[2,128,128]{2,1,0:T(8,128)(2,1)S(1)}, u32[]{:S(2)}, u32[]{:S(2)}) collective-permute-start(bf16[2,128,128]{2,1,0:T(8,128)(2,1)S(1)} %shard_map.47.refs_0_), channel_id=1, source_target_pairs={{0,8},{1,9},{2,10},{3,11},{4,12},{5,13},{6,14},{7,15},{8,0},{9,1},... | collective-permute-start | bytes 196616 | tf_op jit(solution)/shard_map/ppermute | solution.py:30
  19.7 0.0 copy-done.3
  19.8 0.0 copy-start.2
  19.8 0.4 collective-permute-start
  20.1 3.2 %collective-permute-done.next_slots = s32[8]{0:T(128)S(1)} collective-permute-done((s32[8]{0:T(128)S(1)}, s32[8]{0:T(128)S(1)}, u32[]{:S(2)}, u32[]{:S(2)}) %collective-permute-start) | collective-permute-done | bytes 64 | tf_op jit(solution)/shard_map/ppermute | solution.py:30
  23.3 0.0 copy-done.2
  23.3 0.4 collective-permute-start.1
  23.7 3.2 %collective-permute-done.1.next_mask = s32[2,8]{1,0:T(2,128)S(1)} collective-permute-done((s32[2,8]{1,0:T(2,128)S(1)}, s32[2,8]{1,0:T(2,128)S(1)}, u32[]{:S(2)}, u32[]{:S(2)}) %collective-permute-start.1) | collective-permute-done | bytes 96 | tf_op jit(solution)/shard_map/ppermute | solution.py:30
  26.9 1.5 %collective-permute-start.4 = (bf16[2,128,128]{2,1,0:T(8,128)(2,1)S(1)}, bf16[2,128,128]{2,1,0:T(8,128)(2,1)S(1)}, u32[]{:S(2)}, u32[]{:S(2)}) collective-permute-start(bf16[2,128,128]{2,1,0:T(8,128)(2,1)S(1)} %shard_map.47.refs_0_), channel_id=1, source_target_pairs={{0,4},{1,5},{2,6},{3,7},{4,0},{5,1},{6,2},{7,3},{8,12},{9,13},{10,... | collective-permute-start | bytes 196616 | tf_op jit(solution)/shard_map/ppermute | solution.py:30
  28.4 0.0 collective-permute-done.9.refs_6_
  28.4 0.5 collective-permute-start.10
  28.9 0.0 collective-permute-done.7.refs_4_
  28.9 1.5 %collective-permute-start.8 = (bf16[2,128,128]{2,1,0:T(8,128)(2,1)S(1)}, bf16[2,128,128]{2,1,0:T(8,128)(2,1)S(1)}, u32[]{:S(2)}, u32[]{:S(2)}) collective-permute-start(bf16[2,128,128]{2,1,0:T(8,128)(2,1)S(1)} %collective-permute-done.7.refs_4_), channel_id=1, source_target_pairs={{0,4},{1,5},{2,6},{3,7},{4,0},{5,1},{6,2},{7,3},{8,12},{9,13},{10,... | collective-permute-start | bytes 196616 | tf_op jit(solution)/shard_map/ppermute | solution.py:30
  30.5 0.0 collective-permute-done.5.refs_2_
  30.5 0.5 collective-permute-start.6
  31.0 0.1 stack.93.place_ref
  31.1 0.1 collective-permute-done.4.refs_1_
  31.2 1.5 %collective-permute-done.10.refs_7_ = bf16[2,128,128]{2,1,0:T(8,128)(2,1)S(1)} collective-permute-done((bf16[2,128,128]{2,1,0:T(8,128)(2,1)S(1)}, bf16[2,128,128]{2,1,0:T(8,128)(2,1)S(1)}, u32[]{:S(2)}, u32[]{:S(2)}) %collective-permute-start.10) | collective-permute-done | bytes 65568 | tf_op jit(solution)/shard_map/ppermute | solution.py:30
  32.7 0.7 %collective-permute-done.8.refs_5_ = bf16[2,128,128]{2,1,0:T(8,128)(2,1)S(1)} collective-permute-done((bf16[2,128,128]{2,1,0:T(8,128)(2,1)S(1)}, bf16[2,128,128]{2,1,0:T(8,128)(2,1)S(1)}, u32[]{:S(2)}, u32[]{:S(2)}) %collective-permute-start.8) | collective-permute-done | bytes 65568 | tf_op jit(solution)/shard_map/ppermute | solution.py:30
  33.4 1.3 %collective-permute-done.6.refs_3_ = bf16[2,128,128]{2,1,0:T(8,128)(2,1)S(1)} collective-permute-done((bf16[2,128,128]{2,1,0:T(8,128)(2,1)S(1)}, bf16[2,128,128]{2,1,0:T(8,128)(2,1)S(1)}, u32[]{:S(2)}, u32[]{:S(2)}) %collective-permute-start.6) | collective-permute-done | bytes 65568 | tf_op jit(solution)/shard_map/ppermute | solution.py:30
  34.7 0.0 collective-permute-done.2.next_ref
  34.7 2.5 %shard_map.48 = f32[512,256]{1,0:T(8,128)S(1)} custom-call(s32[9]{0:T(128)S(1)} %stack.93.place_ref, s32[8]{0:T(128)S(1)} %bitcast.27, s32[8]{0:T(128)S(1)} %collective-permute-done.next_slots, s32[2,8]{1,0:T(2,128)S(1)} %bitcast.25, s32[2,8]{1,0:T(2,128)S(1)} %collective-permute-done.1.next_mask, bf16[8,2,128,128]{3,2,1,0:T(8,128)(2,1)S(1)} %get-tuple-element.7.own_ref, ...), custom_call_target="tpu_custom_call" | custom-call | tf_op jit(solution)/shard_map/pallas_call | solution.py:166
  37.3 0.1 collective-permute-start.11
  37.3 1.9 %collective-permute-done.11 = f32[512,256]{1,0:T(8,128)S(1)} collective-permute-done((f32[512,256]{1,0:T(8,128)S(1)}, f32[512,256]{1,0:T(8,128)S(1)}, u32[]{:S(2)}, u32[]{:S(2)}) %collective-permute-start.11) | collective-permute-done | bytes 524320 | tf_op jit(solution)/shard_map/ppermute | solution.py:30
  39.2 0.1 add_convert_fusion.refs_0_
  39.3 0.6 collective-permute-start.15
  39.9 1.9 %collective-permute-start.13 = (bf16[512,256]{1,0:T(8,128)(2,1)S(1)}, bf16[512,256]{1,0:T(8,128)(2,1)S(1)}, u32[]{:S(2)}, u32[]{:S(2)}) collective-permute-start(bf16[512,256]{1,0:T(8,128)(2,1)S(1)} %add_convert_fusion.refs_0_), channel_id=1, source_target_pairs={{0,0},{1,16},{2,8},{3,24},{4,4},{5,20},{6,12},{7,28},{8,1},{9,17},... | collective-permute-start | bytes 786440 | tf_op jit(solution)/shard_map/ppermute | solution.py:30
  41.8 0.1 collective-permute-start.12
  41.9 10.4 %collective-permute-done.15.refs_3_ = bf16[512,256]{1,0:T(8,128)(2,1)S(1)} collective-permute-done((bf16[512,256]{1,0:T(8,128)(2,1)S(1)}, bf16[512,256]{1,0:T(8,128)(2,1)S(1)}, u32[]{:S(2)}, u32[]{:S(2)}) %collective-permute-start.15) | collective-permute-done | bytes 262176 | tf_op jit(solution)/shard_map/ppermute | solution.py:30
  52.3 0.0 collective-permute-start.16
  52.3 2.5 %collective-permute-done.13.refs_2_ = bf16[512,256]{1,0:T(8,128)(2,1)S(1)} collective-permute-done((bf16[512,256]{1,0:T(8,128)(2,1)S(1)}, bf16[512,256]{1,0:T(8,128)(2,1)S(1)}, u32[]{:S(2)}, u32[]{:S(2)}) %collective-permute-start.13) | collective-permute-done | bytes 262176 | tf_op jit(solution)/shard_map/ppermute | solution.py:30
  54.8 0.7 %collective-permute-start.14 = (bf16[512,256]{1,0:T(8,128)(2,1)S(1)}, bf16[512,256]{1,0:T(8,128)(2,1)S(1)}, u32[]{:S(2)}, u32[]{:S(2)}) collective-permute-start(bf16[512,256]{1,0:T(8,128)(2,1)S(1)} %collective-permute-done.13.refs_2_), channel_id=1, source_target_pairs={{0,4},{1,5},{2,6},{3,7},{4,0},{5,1},{6,2},{7,3},{8,12},{9,13},{10,... | collective-permute-start | bytes 786440 | tf_op jit(solution)/shard_map/ppermute | solution.py:30
  55.5 0.1 stack.83.place_ref
  55.6 0.1 stack.95.place_ref
  55.7 0.0 collective-permute-done.12.refs_1_
  55.7 1.9 %shard_map.49.refs_4_ = bf16[512,1024]{1,0:T(8,128)(2,1)} custom-call(s32[9]{0:T(128)S(1)} %stack.95.place_ref, bf16[512,256]{1,0:T(8,128)(2,1)S(1)} %add_convert_fusion.refs_0_, bf16[512,256]{1,0:T(8,128)(2,1)S(1)} %collective-permute-done.12.refs_1_, bf16[512,256]{1,0:T(8,128)(2,1)S(1)} %collective-permute-done.13.refs_2_, ...), custom_call_target="tpu_custom_call" | custom-call | tf_op jit(solution)/shard_map/pallas_call | solution.py:198
  57.6 3.2 %collective-permute-done.16.refs_3_ = bf16[512,256]{1,0:T(8,128)(2,1)S(1)} collective-permute-done((bf16[512,256]{1,0:T(8,128)(2,1)S(1)}, bf16[512,256]{1,0:T(8,128)(2,1)S(1)}, u32[]{:S(2)}, u32[]{:S(2)}) %collective-permute-start.16) | collective-permute-done | bytes 262176 | tf_op jit(solution)/shard_map/ppermute | solution.py:30
  60.7 2.8 %collective-permute-done.14.refs_2_ = bf16[512,256]{1,0:T(8,128)(2,1)S(1)} collective-permute-done((bf16[512,256]{1,0:T(8,128)(2,1)S(1)}, bf16[512,256]{1,0:T(8,128)(2,1)S(1)}, u32[]{:S(2)}, u32[]{:S(2)}) %collective-permute-start.14) | collective-permute-done | bytes 262176 | tf_op jit(solution)/shard_map/ppermute | solution.py:30
  63.6 1.9 %shard_map.50 = bf16[512,1024]{1,0:T(8,128)(2,1)} custom-call(s32[9]{0:T(128)S(1)} %stack.83.place_ref, bf16[512,256]{1,0:T(8,128)(2,1)S(1)} %add_convert_fusion.refs_0_, bf16[512,256]{1,0:T(8,128)(2,1)S(1)} %collective-permute-done.12.refs_1_, bf16[512,256]{1,0:T(8,128)(2,1)S(1)} %collective-permute-done.14.refs_2_, ...), custom_call_target="tpu_custom_call", output_to_operand_aliasing={{}: (5, {})} | custom-call | tf_op jit(solution)/shard_map/pallas_call | solution.py:198
  (1 shorter events, 0.0 us)
Async XLA Ops:
  0.0 34.7 %collective-permute-start.2 = (bf16[8,2,128,128]{3,2,1,0:T(8,128)(2,1)}, bf16[8,2,128,128]{3,2,1,0:T(8,128)(2,1)S(1)}, u32[]{:S(2)}, u32[]{:S(2)}) collective-permute-start(bf16[8,2,128,128]{3,2,1,0:T(8,128)(2,1)} %bitcast.22), channel_id=1, source_target_pairs={{0,2},{1,3},{2,0},{3,1},{4,6},{5,7},{6,4},{7,5},{8,10},{9,11},{10,... | collective-permute-start | bytes 1572872 | tf_op jit(solution)/shard_map/ppermute | solution.py:30
  0.0 15.3 %collective-permute-start.3 = (bf16[128,256]{1,0:T(8,128)(2,1)}, bf16[128,256]{1,0:T(8,128)(2,1)S(1)}, u32[]{:S(2)}, u32[]{:S(2)}) collective-permute-start(bf16[128,256]{1,0:T(8,128)(2,1)} %coeff_ref.1), channel_id=1, source_target_pairs={{0,2},{1,3},{2,0},{3,1},{4,6},{5,7},{6,4},{7,5},{8,10},{9,11},{10,... | collective-permute-start | bytes 196616 | tf_op jit(solution)/shard_map/ppermute | solution.py:30
  2.0 1.0 %copy-start = (bf16[1,1,8,2,128,128]{5,4,3,2,1,0:T(8,128)(2,1)S(1)}, bf16[1,1,8,2,128,128]{5,4,3,2,1,0:T(8,128)(2,1)}, u32[]{:S(2)}) copy-start(bf16[1,1,8,2,128,128]{5,4,3,2,1,0:T(8,128)(2,1)} %param.4) | copy-start | bytes 1572868
  3.1 0.8 %copy-start.1 = (bf16[128,256]{1,0:T(8,128)(2,1)S(1)}, bf16[128,256]{1,0:T(8,128)(2,1)}, u32[]{:S(2)}) copy-start(bf16[128,256]{1,0:T(8,128)(2,1)} %coeff_ref.1) | copy-start | bytes 196612
  15.3 4.5 %copy-start.3 = (s32[1,1,8]{2,1,0:T(1,128)S(1)}, s32[1,1,8]{2,1,0:T(1,128)}, u32[]{:S(2)}) copy-start(s32[1,1,8]{2,1,0:T(1,128)} %param.5) | copy-start | bytes 100
  15.3 13.1 %collective-permute-start.9 = (bf16[2,128,128]{2,1,0:T(8,128)(2,1)S(1)}, bf16[2,128,128]{2,1,0:T(8,128)(2,1)S(1)}, u32[]{:S(2)}, u32[]{:S(2)}) collective-permute-start(bf16[2,128,128]{2,1,0:T(8,128)(2,1)S(1)} %shard_map.47.refs_0_), channel_id=1, source_target_pairs={{0,24},{1,25},{2,26},{3,27},{4,28},{5,29},{6,30},{7,31},{8,16},{9,... | collective-permute-start | bytes 196616 | tf_op jit(solution)/shard_map/ppermute | solution.py:30
  19.0 10.0 %collective-permute-start.7 = (bf16[2,128,128]{2,1,0:T(8,128)(2,1)S(1)}, bf16[2,128,128]{2,1,0:T(8,128)(2,1)S(1)}, u32[]{:S(2)}, u32[]{:S(2)}) collective-permute-start(bf16[2,128,128]{2,1,0:T(8,128)(2,1)S(1)} %shard_map.47.refs_0_), channel_id=1, source_target_pairs={{0,16},{1,17},{2,18},{3,19},{4,20},{5,21},{6,22},{7,23},{8,24},{9,... | collective-permute-start | bytes 196616 | tf_op jit(solution)/shard_map/ppermute | solution.py:30
  19.0 11.5 %collective-permute-start.5 = (bf16[2,128,128]{2,1,0:T(8,128)(2,1)S(1)}, bf16[2,128,128]{2,1,0:T(8,128)(2,1)S(1)}, u32[]{:S(2)}, u32[]{:S(2)}) collective-permute-start(bf16[2,128,128]{2,1,0:T(8,128)(2,1)S(1)} %shard_map.47.refs_0_), channel_id=1, source_target_pairs={{0,8},{1,9},{2,10},{3,11},{4,12},{5,13},{6,14},{7,15},{8,0},{9,1},... | collective-permute-start | bytes 196616 | tf_op jit(solution)/shard_map/ppermute | solution.py:30
  19.8 3.6 %copy-start.2 = (s32[8,2]{0,1:T(2,128)S(1)}, s32[8,2]{0,1:T(2,128)}, u32[]{:S(2)}) copy-start(s32[8,2]{0,1:T(2,128)} %param.7) | copy-start | bytes 196
  19.8 3.6 %collective-permute-start = (s32[8]{0:T(128)S(1)}, s32[8]{0:T(128)S(1)}, u32[]{:S(2)}, u32[]{:S(2)}) collective-permute-start(s32[8]{0:T(128)S(1)} %bitcast.26), channel_id=1, source_target_pairs={{0,2},{1,3},{2,0},{3,1},{4,6},{5,7},{6,4},{7,5},{8,10},{9,11},{10,... | collective-permute-start | bytes 104 | tf_op jit(solution)/shard_map/ppermute | solution.py:30
  23.3 3.6 %collective-permute-start.1 = (s32[2,8]{1,0:T(2,128)S(1)}, s32[2,8]{1,0:T(2,128)S(1)}, u32[]{:S(2)}, u32[]{:S(2)}) collective-permute-start(s32[2,8]{1,0:T(2,128)S(1)} %bitcast.24), channel_id=1, source_target_pairs={{0,2},{1,3},{2,0},{3,1},{4,6},{5,7},{6,4},{7,5},{8,10},{9,11},{10,... | collective-permute-start | bytes 200 | tf_op jit(solution)/shard_map/ppermute | solution.py:30
  26.9 4.3 %collective-permute-start.4 = (bf16[2,128,128]{2,1,0:T(8,128)(2,1)S(1)}, bf16[2,128,128]{2,1,0:T(8,128)(2,1)S(1)}, u32[]{:S(2)}, u32[]{:S(2)}) collective-permute-start(bf16[2,128,128]{2,1,0:T(8,128)(2,1)S(1)} %shard_map.47.refs_0_), channel_id=1, source_target_pairs={{0,4},{1,5},{2,6},{3,7},{4,0},{5,1},{6,2},{7,3},{8,12},{9,13},{10,... | collective-permute-start | bytes 196616 | tf_op jit(solution)/shard_map/ppermute | solution.py:30
  28.4 4.3 %collective-permute-start.10 = (bf16[2,128,128]{2,1,0:T(8,128)(2,1)S(1)}, bf16[2,128,128]{2,1,0:T(8,128)(2,1)S(1)}, u32[]{:S(2)}, u32[]{:S(2)}) collective-permute-start(bf16[2,128,128]{2,1,0:T(8,128)(2,1)S(1)} %collective-permute-done.9.refs_6_), channel_id=1, source_target_pairs={{0,4},{1,5},{2,6},{3,7},{4,0},{5,1},{6,2},{7,3},{8,12},{9,13},{10,... | collective-permute-start | bytes 196616 | tf_op jit(solution)/shard_map/ppermute | solution.py:30
  28.9 4.5 %collective-permute-start.8 = (bf16[2,128,128]{2,1,0:T(8,128)(2,1)S(1)}, bf16[2,128,128]{2,1,0:T(8,128)(2,1)S(1)}, u32[]{:S(2)}, u32[]{:S(2)}) collective-permute-start(bf16[2,128,128]{2,1,0:T(8,128)(2,1)S(1)} %collective-permute-done.7.refs_4_), channel_id=1, source_target_pairs={{0,4},{1,5},{2,6},{3,7},{4,0},{5,1},{6,2},{7,3},{8,12},{9,13},{10,... | collective-permute-start | bytes 196616 | tf_op jit(solution)/shard_map/ppermute | solution.py:30
  30.5 4.3 %collective-permute-start.6 = (bf16[2,128,128]{2,1,0:T(8,128)(2,1)S(1)}, bf16[2,128,128]{2,1,0:T(8,128)(2,1)S(1)}, u32[]{:S(2)}, u32[]{:S(2)}) collective-permute-start(bf16[2,128,128]{2,1,0:T(8,128)(2,1)S(1)} %collective-permute-done.5.refs_2_), channel_id=1, source_target_pairs={{0,4},{1,5},{2,6},{3,7},{4,0},{5,1},{6,2},{7,3},{8,12},{9,13},{10,... | collective-permute-start | bytes 196616 | tf_op jit(solution)/shard_map/ppermute | solution.py:30
  37.3 2.0 %collective-permute-start.11 = (f32[512,256]{1,0:T(8,128)S(1)}, f32[512,256]{1,0:T(8,128)S(1)}, u32[]{:S(2)}, u32[]{:S(2)}) collective-permute-start(f32[512,256]{1,0:T(8,128)S(1)} %shard_map.48), channel_id=1, source_target_pairs={{0,1},{1,0},{2,3},{3,2},{4,5},{5,4},{6,7},{7,6},{8,9},{9,8},{10,11... | collective-permute-start | bytes 1572872 | tf_op jit(solution)/shard_map/ppermute | solution.py:30
  39.3 13.0 %collective-permute-start.15 = (bf16[512,256]{1,0:T(8,128)(2,1)S(1)}, bf16[512,256]{1,0:T(8,128)(2,1)S(1)}, u32[]{:S(2)}, u32[]{:S(2)}) collective-permute-start(bf16[512,256]{1,0:T(8,128)(2,1)S(1)} %add_convert_fusion.refs_0_), channel_id=1, source_target_pairs={{0,8},{1,24},{2,0},{3,16},{4,12},{5,28},{6,4},{7,20},{8,9},{9,25},... | collective-permute-start | bytes 786440 | tf_op jit(solution)/shard_map/ppermute | solution.py:30
  39.9 14.9 %collective-permute-start.13 = (bf16[512,256]{1,0:T(8,128)(2,1)S(1)}, bf16[512,256]{1,0:T(8,128)(2,1)S(1)}, u32[]{:S(2)}, u32[]{:S(2)}) collective-permute-start(bf16[512,256]{1,0:T(8,128)(2,1)S(1)} %add_convert_fusion.refs_0_), channel_id=1, source_target_pairs={{0,0},{1,16},{2,8},{3,24},{4,4},{5,20},{6,12},{7,28},{8,1},{9,17},... | collective-permute-start | bytes 786440 | tf_op jit(solution)/shard_map/ppermute | solution.py:30
  41.8 13.9 %collective-permute-start.12 = (bf16[512,256]{1,0:T(8,128)(2,1)S(1)}, bf16[512,256]{1,0:T(8,128)(2,1)S(1)}, u32[]{:S(2)}, u32[]{:S(2)}) collective-permute-start(bf16[512,256]{1,0:T(8,128)(2,1)S(1)} %add_convert_fusion.refs_0_), channel_id=1, source_target_pairs={{0,2},{1,3},{2,0},{3,1},{4,6},{5,7},{6,4},{7,5},{8,10},{9,11},{10,... | collective-permute-start | bytes 786440 | tf_op jit(solution)/shard_map/ppermute | solution.py:30
  52.3 8.4 %collective-permute-start.16 = (bf16[512,256]{1,0:T(8,128)(2,1)S(1)}, bf16[512,256]{1,0:T(8,128)(2,1)S(1)}, u32[]{:S(2)}, u32[]{:S(2)}) collective-permute-start(bf16[512,256]{1,0:T(8,128)(2,1)S(1)} %collective-permute-done.15.refs_3_), channel_id=1, source_target_pairs={{0,4},{1,5},{2,6},{3,7},{4,0},{5,1},{6,2},{7,3},{8,12},{9,13},{10,... | collective-permute-start | bytes 786440 | tf_op jit(solution)/shard_map/ppermute | solution.py:30
  54.8 8.7 %collective-permute-start.14 = (bf16[512,256]{1,0:T(8,128)(2,1)S(1)}, bf16[512,256]{1,0:T(8,128)(2,1)S(1)}, u32[]{:S(2)}, u32[]{:S(2)}) collective-permute-start(bf16[512,256]{1,0:T(8,128)(2,1)S(1)} %collective-permute-done.13.refs_2_), channel_id=1, source_target_pairs={{0,4},{1,5},{2,6},{3,7},{4,0},{5,1},{6,2},{7,3},{8,12},{9,13},{10,... | collective-permute-start | bytes 786440 | tf_op jit(solution)/shard_map/ppermute | solution.py:30

commit v3 on v2

--- a/solution.py
+++ b/solution.py
@@ -11,6 +11,7 @@
 
 VMEM = pl.BlockSpec(memory_space=pltpu.VMEM)
 HBM = pl.BlockSpec(memory_space=pltpu.HBM)
+TABLE = (8, 128)
 SMEM = pl.BlockSpec(memory_space=pltpu.SMEM)
 PARAMS = pltpu.CompilerParams(vmem_limit_bytes=16 << 20)
 
@@ -38,13 +39,22 @@
     return ref[:, pl.ds(pl.multiple_of(chip * part, part), part)]
 
 
-def own_kernel(coeff_ref, blocks_ref, out_ref, held_ref, coeff_held, sems):
+def own_kernel(slot_ref, mask_ref, coeff_ref, blocks_ref, out_ref, held_ref, table_ref, coeff_held, sems):
     copies = [
         pltpu.make_async_copy(coeff_ref, coeff_held, sems.at[0]),
         pltpu.make_async_copy(blocks_ref, held_ref, sems.at[1]),
     ]
     for copy in copies:
         copy.start()
+    line = lax.broadcasted_iota(jnp.int32, TABLE, 0)
+    lane = lax.broadcasted_iota(jnp.int32, TABLE, 1)
+    table = jnp.zeros(TABLE, jnp.int32)
+    for slot in range(slot_ref.shape[0]):
+        table = jnp.where((line == 0) & (lane == slot), slot_ref[slot], table)
+    for part in range(mask_ref.shape[0]):
+        for nu_block in range(mask_ref.shape[1]):
+            table = jnp.where((line == 1 + part) & (lane == nu_block), mask_ref[part, nu_block], table)
+    table_ref[...] = table
     copies[0].wait()
     out_ref[0] = chip_half(coeff_held, out_ref.shape[2])
     copies[1].wait()
@@ -55,7 +65,7 @@
 
 
 def half_kernel(
-    kept_slots, nu_blocks, block, place_ref, own_slots, next_slots, own_mask, next_mask, own_ref, next_ref, *refs
+    kept_slots, nu_blocks, block, place_ref, own_table, next_table, own_ref, next_ref, *refs
 ):
     pieces, (out_ref, rows_ref) = refs[:-2], refs[-2:]
     rows, part = pieces[0].shape[1:]
@@ -67,14 +77,14 @@
             nu_block = (start + inner) // block
             for first in range(0, part, block):
                 columns = slice(first, first + min(block, part))
-                for side, mask in enumerate((own_mask, next_mask)):
+                for side, table in enumerate((own_table, next_table)):
                     value = piece[side, inner : inner + count, columns]
-                    kept = jnp.where(mask[place_ref[0] + first // block, nu_block] != 0, value, jnp.zeros_like(value))
+                    kept = jnp.where(table[1 + place_ref[0] + first // block, nu_block] != 0, value, jnp.zeros_like(value))
                     rows_ref[side, pl.ds(start + inner, count), columns] = kept
     out_ref[...] = jnp.zeros_like(out_ref)
 
-    def add(slots, block_ref, side, slot):
-        pair = slots[slot]
+    def add(table, block_ref, side, slot):
+        pair = table[0, slot]
 
         @pl.when(pair >= 0)
         def _():
@@ -88,8 +98,8 @@
 
     @pl.loop(0, kept_slots)
     def _(slot):
-        add(own_slots, own_ref, 0, slot)
-        add(next_slots, next_ref, 1, slot)
+        add(own_table, own_ref, 0, slot)
+        add(next_table, next_ref, 1, slot)
 
 
 def product_kernel(n_left, scale, place_ref, *refs):
@@ -134,20 +144,20 @@
     blocks = three_index.reshape(kept_slots, aux, block, block)
     slots, mask = slot_pair.reshape(kept_slots), occ_mask.T
     next_coeff = lay.shift(coeff, col_bits=2)
-    next_slots = lay.shift(slots, col_bits=2)
-    next_mask = lay.shift(mask, col_bits=2)
-    next_blocks = lay.shift(blocks, col_bits=2)
-    shared, blocks = pl.pallas_call(
+    shared, blocks, table = pl.pallas_call(
         own_kernel,
         out_shape=(
             jax.ShapeDtypeStruct((2, nu_rows, part), coeff.dtype),
             jax.ShapeDtypeStruct(blocks.shape, blocks.dtype),
+            jax.ShapeDtypeStruct(TABLE, jnp.int32),
         ),
-        in_specs=[HBM, HBM],
-        out_specs=(VMEM, VMEM),
+        in_specs=[SMEM, SMEM, HBM, HBM],
+        out_specs=(VMEM, VMEM, VMEM),
         scratch_shapes=[pltpu.VMEM(coeff.shape, coeff.dtype), pltpu.SemaphoreType.DMA((2,))],
         compiler_params=PARAMS,
-    )(coeff, blocks)
+    )(slots, mask, coeff, blocks)
+    next_table = lay.shift(table, col_bits=2)
+    next_blocks = lay.shift(blocks, col_bits=2)
     shared = pl.pallas_call(
         next_kernel,
         out_shape=jax.ShapeDtypeStruct((2, nu_rows, part), coeff.dtype),
@@ -166,11 +176,11 @@
     partial = pl.pallas_call(
         functools.partial(half_kernel, kept_slots, nu_blocks, block),
         out_shape=jax.ShapeDtypeStruct((mu_rows, width // 2), jnp.float32),
-        in_specs=[SMEM] * 5 + [VMEM] * (2 + len(pieces)),
+        in_specs=[SMEM] * 3 + [VMEM] * (2 + len(pieces)),
         out_specs=VMEM,
         scratch_shapes=[pltpu.VMEM((2, nu_blocks * block, part), coeff.dtype)],
         compiler_params=PARAMS,
-    )(jnp.stack([chip * part // block] + places), slots, next_slots, mask, next_mask, blocks, next_blocks, *pieces)
+    )(jnp.stack([chip * part // block] + places), table, next_table, blocks, next_blocks, *pieces)
 
     total = partial + lay.shift(partial, col_bits=1)
     rows = mu_rows // groups

time: 65.6 us -> 65.3 us (level)
  waiting for transfers between devices: 42.1 us -> 40.7 us
  Pallas kernels: 6.37 us -> 7.07 us
  local copies, waits for them, and re-layouts: 2.14 us -> 2.83 us
    ppermute x17 -> x16, waiting for transfers between devices: 42.1 us -> 40.7 us  [permute(): return lax.ppermute(value, ('row', 'col'), pairs)]
    unnamed x8 -> x10, local copies, waits for them, and re-layouts: 1.89 us -> 2.58 us
    ppermute x17 -> x16, starting transfers between devices: 14.7 us -> 14.2 us  [permute(): return lax.ppermute(value, ('row', 'col'), pairs)]
  transfers between devices with their start and end apart: 17 -> 16, of which waited for: 12 -> 11; matrix products, arithmetic and copies ran while one was open for 0% -> 0% of each run, Pallas kernels for 3% -> 3%
where the time goes in v3:
time: 65.3 us; the launch traced here: 65.1 us
  waiting for transfers between devices  40.7 us (62%)
  starting transfers between devices  14.2 us (22%)
  Pallas kernels  7.07 us (11%)
  local copies, waits for them, and re-layouts  2.83 us (4%)
    ppermute x16, waiting for transfers between devices, permute(): return lax.ppermute(value, ('row', 'col'), pairs)  40.7 us
    ppermute x16, starting transfers between devices, permute(): return lax.ppermute(value, ('row', 'col'), pairs)  14.2 us
    pallas_call x2, Pallas kernels, exchange(): pl.pallas_call(functools.partial(product_kernel, pieces, 1.0 / math.sqrt(...  3.72 us
    pallas_call x1, Pallas kernels, exchange(): pl.pallas_call(functools.partial(half_kernel, kept_slots, nu_blocks, bloc...  2.61 us
    unnamed x10, local copies, waits for them, and re-layouts  2.58 us
  transfers between devices with their start and end apart: 16, of which 11 were waited for; matrix products, arithmetic and copies ran while one was open for 0% of the time, Pallas kernels for 3%

profile of v3, /device:TPU:2, one launch (start us, length us, event | category | flops | bytes accessed | tf_op | source)
XLA Modules:
  0.0 65.1 jit_solution(12917351712146066456)
XLA Ops:
  0.0 0.0 copy-start.3
  0.0 0.0 copy-start.4
  0.0 0.7 %copy-done.3 = s32[8,2]{0,1:T(2,128)S(1)} copy-done((s32[8,2]{0,1:T(2,128)S(1)}, s32[8,2]{0,1:T(2,128)}, u32[]{:S(2)}) %copy-start.3) | copy-done | bytes 88
  0.7 0.0 copy-done.4
  0.7 0.0 copy-start
  0.7 1.0 %copy-done = bf16[1,1,8,2,128,128]{5,4,3,2,1,0:T(8,128)(2,1)S(1)} copy-done((bf16[1,1,8,2,128,128]{5,4,3,2,1,0:T(8,128)(2,1)S(1)}, bf16[1,1,8,2,128,128]{5,4,3,2,1,0:T(8,128)(2,1)}, u32[]{:S(2)}) %copy-start) | copy-done | bytes 524312
  1.7 0.0 copy-start.1
  1.7 0.8 %copy-done.1 = bf16[128,256]{1,0:T(8,128)(2,1)S(1)} copy-done((bf16[128,256]{1,0:T(8,128)(2,1)S(1)}, bf16[128,256]{1,0:T(8,128)(2,1)}, u32[]{:S(2)}) %copy-start.1) | copy-done | bytes 65560
  2.6 0.0 copy-start.2
  2.6 0.7 %shard_map.46 = (bf16[2,128,128]{2,1,0:T(8,128)(2,1)S(1)}, bf16[8,2,128,128]{3,2,1,0:T(8,128)(2,1)S(1)}, s32[8,128]{1,0:T(8,128)S(1)}) custom-call(s32[8]{0:T(128)S(1)} %bitcast.24, s32[2,8]{1,0:T(2,128)S(1)} %bitcast.23, bf16[128,256]{1,0:T(8,128)(2,1)S(1)} %copy-done.1, bf16[8,2,128,128]{3,2,1,0:T(8,128)(2,1)S(1)} %bitcast.22), custom_call_target="tpu_custom_call" | custom-call | tf_op jit(solution)/shard_map/pallas_call | solution.py:147
  3.3 0.1 collective-permute-start.1
  3.4 0.0 copy-done.2
  3.4 2.0 %collective-permute-start.2 = (bf16[128,256]{1,0:T(8,128)(2,1)S(1)}, bf16[128,256]{1,0:T(8,128)(2,1)S(1)}, u32[]{:S(2)}, u32[]{:S(2)}) collective-permute-start(bf16[128,256]{1,0:T(8,128)(2,1)S(1)} %copy-done.2), channel_id=1, source_target_pairs={{0,2},{1,3},{2,0},{3,1},{4,6},{5,7},{6,4},{7,5},{8,10},{9,11},{10,... | collective-permute-start | bytes 196616 | tf_op jit(solution)/shard_map/ppermute | solution.py:31
  5.4 13.0 %collective-permute-done.2.next_ref = bf16[128,256]{1,0:T(8,128)(2,1)S(1)} collective-permute-done((bf16[128,256]{1,0:T(8,128)(2,1)S(1)}, bf16[128,256]{1,0:T(8,128)(2,1)S(1)}, u32[]{:S(2)}, u32[]{:S(2)}) %collective-permute-start.2) | collective-permute-done | bytes 65568 | tf_op jit(solution)/shard_map/ppermute | solution.py:31
  18.5 3.6 %collective-permute-start.8 = (bf16[2,128,128]{2,1,0:T(8,128)(2,1)S(1)}, bf16[2,128,128]{2,1,0:T(8,128)(2,1)S(1)}, u32[]{:S(2)}, u32[]{:S(2)}) collective-permute-start(bf16[2,128,128]{2,1,0:T(8,128)(2,1)S(1)} %shard_map.47.refs_0_), channel_id=1, source_target_pairs={{0,24},{1,25},{2,26},{3,27},{4,28},{5,29},{6,30},{7,31},{8,16},{9,... | collective-permute-start | bytes 196616 | tf_op jit(solution)/shard_map/ppermute | solution.py:31
  22.1 0.0 collective-permute-start.6
  22.1 0.8 %collective-permute-start.4 = (bf16[2,128,128]{2,1,0:T(8,128)(2,1)S(1)}, bf16[2,128,128]{2,1,0:T(8,128)(2,1)S(1)}, u32[]{:S(2)}, u32[]{:S(2)}) collective-permute-start(bf16[2,128,128]{2,1,0:T(8,128)(2,1)S(1)} %shard_map.47.refs_0_), channel_id=1, source_target_pairs={{0,8},{1,9},{2,10},{3,11},{4,12},{5,13},{6,14},{7,15},{8,0},{9,1},... | collective-permute-start | bytes 196616 | tf_op jit(solution)/shard_map/ppermute | solution.py:31
  22.8 0.4 collective-permute-start
  23.2 3.2 %collective-permute-done.next_table = s32[8,128]{1,0:T(8,128)S(1)} collective-permute-done((s32[8,128]{1,0:T(8,128)S(1)}, s32[8,128]{1,0:T(8,128)S(1)}, u32[]{:S(2)}, u32[]{:S(2)}) %collective-permute-start) | collective-permute-done | bytes 4128 | tf_op jit(solution)/shard_map/ppermute | solution.py:31
  26.4 1.5 %collective-permute-start.3 = (bf16[2,128,128]{2,1,0:T(8,128)(2,1)S(1)}, bf16[2,128,128]{2,1,0:T(8,128)(2,1)S(1)}, u32[]{:S(2)}, u32[]{:S(2)}) collective-permute-start(bf16[2,128,128]{2,1,0:T(8,128)(2,1)S(1)} %shard_map.47.refs_0_), channel_id=1, source_target_pairs={{0,4},{1,5},{2,6},{3,7},{4,0},{5,1},{6,2},{7,3},{8,12},{9,13},{10,... | collective-permute-start | bytes 196616 | tf_op jit(solution)/shard_map/ppermute | solution.py:31
  28.0 0.0 collective-permute-done.8.refs_6_
  28.0 0.5 collective-permute-start.9
  28.5 0.0 collective-permute-done.6.refs_4_
  28.5 1.5 %collective-permute-start.7 = (bf16[2,128,128]{2,1,0:T(8,128)(2,1)S(1)}, bf16[2,128,128]{2,1,0:T(8,128)(2,1)S(1)}, u32[]{:S(2)}, u32[]{:S(2)}) collective-permute-start(bf16[2,128,128]{2,1,0:T(8,128)(2,1)S(1)} %collective-permute-done.6.refs_4_), channel_id=1, source_target_pairs={{0,4},{1,5},{2,6},{3,7},{4,0},{5,1},{6,2},{7,3},{8,12},{9,13},{10,... | collective-permute-start | bytes 196616 | tf_op jit(solution)/shard_map/ppermute | solution.py:31
  30.0 0.0 collective-permute-done.4.refs_2_
  30.0 0.5 collective-permute-start.5
  30.5 0.1 stack.93.place_ref
  30.6 0.6 collective-permute-done.3.refs_1_
  31.2 1.0 %collective-permute-done.9.refs_7_ = bf16[2,128,128]{2,1,0:T(8,128)(2,1)S(1)} collective-permute-done((bf16[2,128,128]{2,1,0:T(8,128)(2,1)S(1)}, bf16[2,128,128]{2,1,0:T(8,128)(2,1)S(1)}, u32[]{:S(2)}, u32[]{:S(2)}) %collective-permute-start.9) | collective-permute-done | bytes 65568 | tf_op jit(solution)/shard_map/ppermute | solution.py:31
  32.2 0.7 %collective-permute-done.7.refs_5_ = bf16[2,128,128]{2,1,0:T(8,128)(2,1)S(1)} collective-permute-done((bf16[2,128,128]{2,1,0:T(8,128)(2,1)S(1)}, bf16[2,128,128]{2,1,0:T(8,128)(2,1)S(1)}, u32[]{:S(2)}, u32[]{:S(2)}) %collective-permute-start.7) | collective-permute-done | bytes 65568 | tf_op jit(solution)/shard_map/ppermute | solution.py:31
  32.9 1.3 %collective-permute-done.5.refs_3_ = bf16[2,128,128]{2,1,0:T(8,128)(2,1)S(1)} collective-permute-done((bf16[2,128,128]{2,1,0:T(8,128)(2,1)S(1)}, bf16[2,128,128]{2,1,0:T(8,128)(2,1)S(1)}, u32[]{:S(2)}, u32[]{:S(2)}) %collective-permute-start.5) | collective-permute-done | bytes 65568 | tf_op jit(solution)/shard_map/ppermute | solution.py:31
  34.3 0.0 collective-permute-done.1.next_ref
  34.3 2.6 %shard_map.48 = f32[512,256]{1,0:T(8,128)S(1)} custom-call(s32[9]{0:T(128)S(1)} %stack.93.place_ref, s32[8,128]{1,0:T(8,128)S(1)} %get-tuple-element.8.own_table, s32[8,128]{1,0:T(8,128)S(1)} %collective-permute-done.next_table, bf16[8,2,128,128]{3,2,1,0:T(8,128)(2,1)S(1)} %get-tuple-element.9.own_ref, ...), custom_call_target="tpu_custom_call" | custom-call | tf_op jit(solution)/shard_map/pallas_call | solution.py:176
  36.9 0.1 collective-permute-start.10
  37.0 1.9 %collective-permute-done.10 = f32[512,256]{1,0:T(8,128)S(1)} collective-permute-done((f32[512,256]{1,0:T(8,128)S(1)}, f32[512,256]{1,0:T(8,128)S(1)}, u32[]{:S(2)}, u32[]{:S(2)}) %collective-permute-start.10) | collective-permute-done | bytes 524320 | tf_op jit(solution)/shard_map/ppermute | solution.py:31
  38.9 0.1 add_convert_fusion.refs_0_
  39.0 0.6 collective-permute-start.14
  39.6 1.9 %collective-permute-start.12 = (bf16[512,256]{1,0:T(8,128)(2,1)S(1)}, bf16[512,256]{1,0:T(8,128)(2,1)S(1)}, u32[]{:S(2)}, u32[]{:S(2)}) collective-permute-start(bf16[512,256]{1,0:T(8,128)(2,1)S(1)} %add_convert_fusion.refs_0_), channel_id=1, source_target_pairs={{0,0},{1,16},{2,8},{3,24},{4,4},{5,20},{6,12},{7,28},{8,1},{9,17},... | collective-permute-start | bytes 786440 | tf_op jit(solution)/shard_map/ppermute | solution.py:31
  41.5 0.1 collective-permute-start.11
  41.6 10.4 %collective-permute-done.14.refs_3_ = bf16[512,256]{1,0:T(8,128)(2,1)S(1)} collective-permute-done((bf16[512,256]{1,0:T(8,128)(2,1)S(1)}, bf16[512,256]{1,0:T(8,128)(2,1)S(1)}, u32[]{:S(2)}, u32[]{:S(2)}) %collective-permute-start.14) | collective-permute-done | bytes 262176 | tf_op jit(solution)/shard_map/ppermute | solution.py:31
  52.0 0.0 collective-permute-start.15
  52.0 2.5 %collective-permute-done.12.refs_2_ = bf16[512,256]{1,0:T(8,128)(2,1)S(1)} collective-permute-done((bf16[512,256]{1,0:T(8,128)(2,1)S(1)}, bf16[512,256]{1,0:T(8,128)(2,1)S(1)}, u32[]{:S(2)}, u32[]{:S(2)}) %collective-permute-start.12) | collective-permute-done | bytes 262176 | tf_op jit(solution)/shard_map/ppermute | solution.py:31
  54.5 0.7 %collective-permute-start.13 = (bf16[512,256]{1,0:T(8,128)(2,1)S(1)}, bf16[512,256]{1,0:T(8,128)(2,1)S(1)}, u32[]{:S(2)}, u32[]{:S(2)}) collective-permute-start(bf16[512,256]{1,0:T(8,128)(2,1)S(1)} %collective-permute-done.12.refs_2_), channel_id=1, source_target_pairs={{0,4},{1,5},{2,6},{3,7},{4,0},{5,1},{6,2},{7,3},{8,12},{9,13},{10,... | collective-permute-start | bytes 786440 | tf_op jit(solution)/shard_map/ppermute | solution.py:31
  55.2 0.1 stack.83.place_ref
  55.3 0.1 stack.95.place_ref
  55.4 0.0 collective-permute-done.11.refs_1_
  55.4 1.9 %shard_map.49.refs_4_ = bf16[512,1024]{1,0:T(8,128)(2,1)} custom-call(s32[9]{0:T(128)S(1)} %stack.95.place_ref, bf16[512,256]{1,0:T(8,128)(2,1)S(1)} %add_convert_fusion.refs_0_, bf16[512,256]{1,0:T(8,128)(2,1)S(1)} %collective-permute-done.11.refs_1_, bf16[512,256]{1,0:T(8,128)(2,1)S(1)} %collective-permute-done.12.refs_2_, ...), custom_call_target="tpu_custom_call" | custom-call | tf_op jit(solution)/shard_map/pallas_call | solution.py:208
  57.2 3.2 %collective-permute-done.15.refs_3_ = bf16[512,256]{1,0:T(8,128)(2,1)S(1)} collective-permute-done((bf16[512,256]{1,0:T(8,128)(2,1)S(1)}, bf16[512,256]{1,0:T(8,128)(2,1)S(1)}, u32[]{:S(2)}, u32[]{:S(2)}) %collective-permute-start.15) | collective-permute-done | bytes 262176 | tf_op jit(solution)/shard_map/ppermute | solution.py:31
  60.4 2.8 %collective-permute-done.13.refs_2_ = bf16[512,256]{1,0:T(8,128)(2,1)S(1)} collective-permute-done((bf16[512,256]{1,0:T(8,128)(2,1)S(1)}, bf16[512,256]{1,0:T(8,128)(2,1)S(1)}, u32[]{:S(2)}, u32[]{:S(2)}) %collective-permute-start.13) | collective-permute-done | bytes 262176 | tf_op jit(solution)/shard_map/ppermute | solution.py:31
  63.2 1.9 %shard_map.50 = bf16[512,1024]{1,0:T(8,128)(2,1)} custom-call(s32[9]{0:T(128)S(1)} %stack.83.place_ref, bf16[512,256]{1,0:T(8,128)(2,1)S(1)} %add_convert_fusion.refs_0_, bf16[512,256]{1,0:T(8,128)(2,1)S(1)} %collective-permute-done.11.refs_1_, bf16[512,256]{1,0:T(8,128)(2,1)S(1)} %collective-permute-done.13.refs_2_, ...), custom_call_target="tpu_custom_call", output_to_operand_aliasing={{}: (5, {})} | custom-call | tf_op jit(solution)/shard_map/pallas_call | solution.py:208
  (1 shorter events, 0.0 us)
Async XLA Ops:
  0.0 0.7 %copy-start.3 = (s32[8,2]{0,1:T(2,128)S(1)}, s32[8,2]{0,1:T(2,128)}, u32[]{:S(2)}) copy-start(s32[8,2]{0,1:T(2,128)} %param.7) | copy-start | bytes 196
  0.0 0.7 %copy-start.4 = (s32[1,1,8]{2,1,0:T(1,128)S(1)}, s32[1,1,8]{2,1,0:T(1,128)}, u32[]{:S(2)}) copy-start(s32[1,1,8]{2,1,0:T(1,128)} %param.5) | copy-start | bytes 100
  0.7 1.0 %copy-start = (bf16[1,1,8,2,128,128]{5,4,3,2,1,0:T(8,128)(2,1)S(1)}, bf16[1,1,8,2,128,128]{5,4,3,2,1,0:T(8,128)(2,1)}, u32[]{:S(2)}) copy-start(bf16[1,1,8,2,128,128]{5,4,3,2,1,0:T(8,128)(2,1)} %param.4) | copy-start | bytes 1572868
  1.7 0.8 %copy-start.1 = (bf16[128,256]{1,0:T(8,128)(2,1)S(1)}, bf16[128,256]{1,0:T(8,128)(2,1)}, u32[]{:S(2)}) copy-start(bf16[128,256]{1,0:T(8,128)(2,1)} %coeff_ref.1) | copy-start | bytes 196612
  2.6 0.8 %copy-start.2 = (bf16[128,256]{1,0:T(8,128)(2,1)S(1)}, bf16[128,256]{1,0:T(8,128)(2,1)}, u32[]{:S(2)}) copy-start(bf16[128,256]{1,0:T(8,128)(2,1)} %coeff_ref.1) | copy-start | bytes 196612
  3.3 31.0 %collective-permute-start.1 = (bf16[8,2,128,128]{3,2,1,0:T(8,128)(2,1)S(1)}, bf16[8,2,128,128]{3,2,1,0:T(8,128)(2,1)S(1)}, u32[]{:S(2)}, u32[]{:S(2)}) collective-permute-start(bf16[8,2,128,128]{3,2,1,0:T(8,128)(2,1)S(1)} %get-tuple-element.9.own_ref), channel_id=1, source_target_pairs={{0,2},{1,3},{2,0},{3,1},{4,6},{5,7},{6,4},{7,5},{8,10},{9,11},{10,... | collective-permute-start | bytes 1572872 | tf_op jit(solution)/shard_map/ppermute | solution.py:31
  3.4 15.0 %collective-permute-start.2 = (bf16[128,256]{1,0:T(8,128)(2,1)S(1)}, bf16[128,256]{1,0:T(8,128)(2,1)S(1)}, u32[]{:S(2)}, u32[]{:S(2)}) collective-permute-start(bf16[128,256]{1,0:T(8,128)(2,1)S(1)} %copy-done.2), channel_id=1, source_target_pairs={{0,2},{1,3},{2,0},{3,1},{4,6},{5,7},{6,4},{7,5},{8,10},{9,11},{10,... | collective-permute-start | bytes 196616 | tf_op jit(solution)/shard_map/ppermute | solution.py:31
  18.5 9.5 %collective-permute-start.8 = (bf16[2,128,128]{2,1,0:T(8,128)(2,1)S(1)}, bf16[2,128,128]{2,1,0:T(8,128)(2,1)S(1)}, u32[]{:S(2)}, u32[]{:S(2)}) collective-permute-start(bf16[2,128,128]{2,1,0:T(8,128)(2,1)S(1)} %shard_map.47.refs_0_), channel_id=1, source_target_pairs={{0,24},{1,25},{2,26},{3,27},{4,28},{5,29},{6,30},{7,31},{8,16},{9,... | collective-permute-start | bytes 196616 | tf_op jit(solution)/shard_map/ppermute | solution.py:31
  22.1 6.4 %collective-permute-start.6 = (bf16[2,128,128]{2,1,0:T(8,128)(2,1)S(1)}, bf16[2,128,128]{2,1,0:T(8,128)(2,1)S(1)}, u32[]{:S(2)}, u32[]{:S(2)}) collective-permute-start(bf16[2,128,128]{2,1,0:T(8,128)(2,1)S(1)} %shard_map.47.refs_0_), channel_id=1, source_target_pairs={{0,16},{1,17},{2,18},{3,19},{4,20},{5,21},{6,22},{7,23},{8,24},{9,... | collective-permute-start | bytes 196616 | tf_op jit(solution)/shard_map/ppermute | solution.py:31
  22.1 7.9 %collective-permute-start.4 = (bf16[2,128,128]{2,1,0:T(8,128)(2,1)S(1)}, bf16[2,128,128]{2,1,0:T(8,128)(2,1)S(1)}, u32[]{:S(2)}, u32[]{:S(2)}) collective-permute-start(bf16[2,128,128]{2,1,0:T(8,128)(2,1)S(1)} %shard_map.47.refs_0_), channel_id=1, source_target_pairs={{0,8},{1,9},{2,10},{3,11},{4,12},{5,13},{6,14},{7,15},{8,0},{9,1},... | collective-permute-start | bytes 196616 | tf_op jit(solution)/shard_map/ppermute | solution.py:31
  22.8 3.6 %collective-permute-start = (s32[8,128]{1,0:T(8,128)S(1)}, s32[8,128]{1,0:T(8,128)S(1)}, u32[]{:S(2)}, u32[]{:S(2)}) collective-permute-start(s32[8,128]{1,0:T(8,128)S(1)} %get-tuple-element.8.own_table), channel_id=1, source_target_pairs={{0,2},{1,3},{2,0},{3,1},{4,6},{5,7},{6,4},{7,5},{8,10},{9,11},{10,... | collective-permute-start | bytes 12296 | tf_op jit(solution)/shard_map/ppermute | solution.py:31
  26.4 4.8 %collective-permute-start.3 = (bf16[2,128,128]{2,1,0:T(8,128)(2,1)S(1)}, bf16[2,128,128]{2,1,0:T(8,128)(2,1)S(1)}, u32[]{:S(2)}, u32[]{:S(2)}) collective-permute-start(bf16[2,128,128]{2,1,0:T(8,128)(2,1)S(1)} %shard_map.47.refs_0_), channel_id=1, source_target_pairs={{0,4},{1,5},{2,6},{3,7},{4,0},{5,1},{6,2},{7,3},{8,12},{9,13},{10,... | collective-permute-start | bytes 196616 | tf_op jit(solution)/shard_map/ppermute | solution.py:31
  28.0 4.3 %collective-permute-start.9 = (bf16[2,128,128]{2,1,0:T(8,128)(2,1)S(1)}, bf16[2,128,128]{2,1,0:T(8,128)(2,1)S(1)}, u32[]{:S(2)}, u32[]{:S(2)}) collective-permute-start(bf16[2,128,128]{2,1,0:T(8,128)(2,1)S(1)} %collective-permute-done.8.refs_6_), channel_id=1, source_target_pairs={{0,4},{1,5},{2,6},{3,7},{4,0},{5,1},{6,2},{7,3},{8,12},{9,13},{10,... | collective-permute-start | bytes 196616 | tf_op jit(solution)/shard_map/ppermute | solution.py:31
  28.5 4.5 %collective-permute-start.7 = (bf16[2,128,128]{2,1,0:T(8,128)(2,1)S(1)}, bf16[2,128,128]{2,1,0:T(8,128)(2,1)S(1)}, u32[]{:S(2)}, u32[]{:S(2)}) collective-permute-start(bf16[2,128,128]{2,1,0:T(8,128)(2,1)S(1)} %collective-permute-done.6.refs_4_), channel_id=1, source_target_pairs={{0,4},{1,5},{2,6},{3,7},{4,0},{5,1},{6,2},{7,3},{8,12},{9,13},{10,... | collective-permute-start | bytes 196616 | tf_op jit(solution)/shard_map/ppermute | solution.py:31
  30.0 4.3 %collective-permute-start.5 = (bf16[2,128,128]{2,1,0:T(8,128)(2,1)S(1)}, bf16[2,128,128]{2,1,0:T(8,128)(2,1)S(1)}, u32[]{:S(2)}, u32[]{:S(2)}) collective-permute-start(bf16[2,128,128]{2,1,0:T(8,128)(2,1)S(1)} %collective-permute-done.4.refs_2_), channel_id=1, source_target_pairs={{0,4},{1,5},{2,6},{3,7},{4,0},{5,1},{6,2},{7,3},{8,12},{9,13},{10,... | collective-permute-start | bytes 196616 | tf_op jit(solution)/shard_map/ppermute | solution.py:31
  36.9 2.0 %collective-permute-start.10 = (f32[512,256]{1,0:T(8,128)S(1)}, f32[512,256]{1,0:T(8,128)S(1)}, u32[]{:S(2)}, u32[]{:S(2)}) collective-permute-start(f32[512,256]{1,0:T(8,128)S(1)} %shard_map.48), channel_id=1, source_target_pairs={{0,1},{1,0},{2,3},{3,2},{4,5},{5,4},{6,7},{7,6},{8,9},{9,8},{10,11... | collective-permute-start | bytes 1572872 | tf_op jit(solution)/shard_map/ppermute | solution.py:31
  39.0 13.0 %collective-permute-start.14 = (bf16[512,256]{1,0:T(8,128)(2,1)S(1)}, bf16[512,256]{1,0:T(8,128)(2,1)S(1)}, u32[]{:S(2)}, u32[]{:S(2)}) collective-permute-start(bf16[512,256]{1,0:T(8,128)(2,1)S(1)} %add_convert_fusion.refs_0_), channel_id=1, source_target_pairs={{0,8},{1,24},{2,0},{3,16},{4,12},{5,28},{6,4},{7,20},{8,9},{9,25},... | collective-permute-start | bytes 786440 | tf_op jit(solution)/shard_map/ppermute | solution.py:31
  39.6 14.9 %collective-permute-start.12 = (bf16[512,256]{1,0:T(8,128)(2,1)S(1)}, bf16[512,256]{1,0:T(8,128)(2,1)S(1)}, u32[]{:S(2)}, u32[]{:S(2)}) collective-permute-start(bf16[512,256]{1,0:T(8,128)(2,1)S(1)} %add_convert_fusion.refs_0_), channel_id=1, source_target_pairs={{0,0},{1,16},{2,8},{3,24},{4,4},{5,20},{6,12},{7,28},{8,1},{9,17},... | collective-permute-start | bytes 786440 | tf_op jit(solution)/shard_map/ppermute | solution.py:31
  41.5 13.9 %collective-permute-start.11 = (bf16[512,256]{1,0:T(8,128)(2,1)S(1)}, bf16[512,256]{1,0:T(8,128)(2,1)S(1)}, u32[]{:S(2)}, u32[]{:S(2)}) collective-permute-start(bf16[512,256]{1,0:T(8,128)(2,1)S(1)} %add_convert_fusion.refs_0_), channel_id=1, source_target_pairs={{0,2},{1,3},{2,0},{3,1},{4,6},{5,7},{6,4},{7,5},{8,10},{9,11},{10,... | collective-permute-start | bytes 786440 | tf_op jit(solution)/shard_map/ppermute | solution.py:31
  52.0 8.4 %collective-permute-start.15 = (bf16[512,256]{1,0:T(8,128)(2,1)S(1)}, bf16[512,256]{1,0:T(8,128)(2,1)S(1)}, u32[]{:S(2)}, u32[]{:S(2)}) collective-permute-start(bf16[512,256]{1,0:T(8,128)(2,1)S(1)} %collective-permute-done.14.refs_3_), channel_id=1, source_target_pairs={{0,4},{1,5},{2,6},{3,7},{4,0},{5,1},{6,2},{7,3},{8,12},{9,13},{10,... | collective-permute-start | bytes 786440 | tf_op jit(solution)/shard_map/ppermute | solution.py:31
  54.5 8.7 %collective-permute-start.13 = (bf16[512,256]{1,0:T(8,128)(2,1)S(1)}, bf16[512,256]{1,0:T(8,128)(2,1)S(1)}, u32[]{:S(2)}, u32[]{:S(2)}) collective-permute-start(bf16[512,256]{1,0:T(8,128)(2,1)S(1)} %collective-permute-done.12.refs_2_), channel_id=1, source_target_pairs={{0,4},{1,5},{2,6},{3,7},{4,0},{5,1},{6,2},{7,3},{8,12},{9,13},{10,... | collective-permute-start | bytes 786440 | tf_op jit(solution)/shard_map/ppermute | solution.py:31

commit v4 on v3

--- a/solution.py
+++ b/solution.py
@@ -169,9 +169,14 @@
 
     pieces, places = [], []
     for d in range(n_col):
-        here = lay.shift(shared, plane_bits=d) if d else shared
+        held = lay.shift(shared, plane_bits=d) if d else shared
         for t in range(ratio):
-            pieces.append(lay.shift(here, side_bits=t) if t else here)
+            here = held
+            if t and d == 1:
+                here = lay.shift(shared, plane_bits=d, side_bits=t)
+            elif t:
+                here = lay.shift(held, side_bits=t)
+            pieces.append(here)
             places.append((plane ^ d) * ratio + (side ^ t))
     partial = pl.pallas_call(
         functools.partial(half_kernel, kept_slots, nu_blocks, block),

time: 65.3 us -> 66.2 us (1.014)
  waiting for transfers between devices: 40.7 us -> 41.4 us
    ppermute x16, waiting for transfers between devices: 40.7 us -> 41.4 us  [permute(): return lax.ppermute(value, ('row', 'col'), pairs)]
where the time goes in v4:
time: 66.2 us; the launch traced here: 65.9 us
  waiting for transfers between devices  41.4 us (63%)
  starting transfers between devices  14.4 us (22%)
  Pallas kernels  7.07 us (11%)
  local copies, waits for them, and re-layouts  2.83 us (4%)
    ppermute x16, waiting for transfers between devices, permute(): return lax.ppermute(value, ('row', 'col'), pairs)  41.4 us
    ppermute x16, starting transfers between devices, permute(): return lax.ppermute(value, ('row', 'col'), pairs)  14.4 us
    pallas_call x2, Pallas kernels, exchange(): pl.pallas_call(functools.partial(product_kernel, pieces, 1.0 / math.sqrt(...  3.72 us
    pallas_call x1, Pallas kernels, exchange(): pl.pallas_call(functools.partial(half_kernel, kept_slots, nu_blocks, bloc...  2.61 us
    unnamed x10, local copies, waits for them, and re-layouts  2.58 us
  transfers between devices with their start and end apart: 16, of which 11 were waited for; matrix products, arithmetic and copies ran while one was open for 0% of the time, Pallas kernels for 3%

profile of v4, /device:TPU:2, one launch (start us, length us, event | category | flops | bytes accessed | tf_op | source)
XLA Modules:
  0.0 65.9 jit_solution(4727159862408544542)
XLA Ops:
  0.0 0.0 copy-start.3
  0.0 0.0 copy-start.4
  0.0 0.7 %copy-done.3 = s32[8,2]{0,1:T(2,128)S(1)} copy-done((s32[8,2]{0,1:T(2,128)S(1)}, s32[8,2]{0,1:T(2,128)}, u32[]{:S(2)}) %copy-start.3) | copy-done | bytes 88
  0.7 0.0 copy-done.4
  0.7 0.0 copy-start
  0.7 1.0 %copy-done = bf16[1,1,8,2,128,128]{5,4,3,2,1,0:T(8,128)(2,1)S(1)} copy-done((bf16[1,1,8,2,128,128]{5,4,3,2,1,0:T(8,128)(2,1)S(1)}, bf16[1,1,8,2,128,128]{5,4,3,2,1,0:T(8,128)(2,1)}, u32[]{:S(2)}) %copy-start) | copy-done | bytes 524312
  1.7 0.0 copy-start.1
  1.7 0.8 %copy-done.1 = bf16[128,256]{1,0:T(8,128)(2,1)S(1)} copy-done((bf16[128,256]{1,0:T(8,128)(2,1)S(1)}, bf16[128,256]{1,0:T(8,128)(2,1)}, u32[]{:S(2)}) %copy-start.1) | copy-done | bytes 65560
  2.6 0.0 copy-start.2
  2.6 0.7 %shard_map.46 = (bf16[2,128,128]{2,1,0:T(8,128)(2,1)S(1)}, bf16[8,2,128,128]{3,2,1,0:T(8,128)(2,1)S(1)}, s32[8,128]{1,0:T(8,128)S(1)}) custom-call(s32[8]{0:T(128)S(1)} %bitcast.24, s32[2,8]{1,0:T(2,128)S(1)} %bitcast.23, bf16[128,256]{1,0:T(8,128)(2,1)S(1)} %copy-done.1, bf16[8,2,128,128]{3,2,1,0:T(8,128)(2,1)S(1)} %bitcast.22), custom_call_target="tpu_custom_call" | custom-call | tf_op jit(solution)/shard_map/pallas_call | solution.py:147
  3.3 0.1 collective-permute-start.1
  3.4 0.0 copy-done.2
  3.4 2.0 %collective-permute-start.2 = (bf16[128,256]{1,0:T(8,128)(2,1)S(1)}, bf16[128,256]{1,0:T(8,128)(2,1)S(1)}, u32[]{:S(2)}, u32[]{:S(2)}) collective-permute-start(bf16[128,256]{1,0:T(8,128)(2,1)S(1)} %copy-done.2), channel_id=1, source_target_pairs={{0,2},{1,3},{2,0},{3,1},{4,6},{5,7},{6,4},{7,5},{8,10},{9,11},{10,... | collective-permute-start | bytes 196616 | tf_op jit(solution)/shard_map/ppermute | solution.py:31
  5.4 13.0 %collective-permute-done.2.next_ref = bf16[128,256]{1,0:T(8,128)(2,1)S(1)} collective-permute-done((bf16[128,256]{1,0:T(8,128)(2,1)S(1)}, bf16[128,256]{1,0:T(8,128)(2,1)S(1)}, u32[]{:S(2)}, u32[]{:S(2)}) %collective-permute-start.2) | collective-permute-done | bytes 65568 | tf_op jit(solution)/shard_map/ppermute | solution.py:31
  18.5 3.6 %collective-permute-start.8 = (bf16[2,128,128]{2,1,0:T(8,128)(2,1)S(1)}, bf16[2,128,128]{2,1,0:T(8,128)(2,1)S(1)}, u32[]{:S(2)}, u32[]{:S(2)}) collective-permute-start(bf16[2,128,128]{2,1,0:T(8,128)(2,1)S(1)} %shard_map.47.refs_0_), channel_id=1, source_target_pairs={{0,24},{1,25},{2,26},{3,27},{4,28},{5,29},{6,30},{7,31},{8,16},{9,... | collective-permute-start | bytes 196616 | tf_op jit(solution)/shard_map/ppermute | solution.py:31
  22.1 0.0 collective-permute-start.6
  22.1 1.7 %collective-permute-start.5 = (bf16[2,128,128]{2,1,0:T(8,128)(2,1)S(1)}, bf16[2,128,128]{2,1,0:T(8,128)(2,1)S(1)}, u32[]{:S(2)}, u32[]{:S(2)}) collective-permute-start(bf16[2,128,128]{2,1,0:T(8,128)(2,1)S(1)} %shard_map.47.refs_0_), channel_id=1, source_target_pairs={{0,12},{1,13},{2,14},{3,15},{4,8},{5,9},{6,10},{7,11},{8,4},{9,5},... | collective-permute-start | bytes 196616 | tf_op jit(solution)/shard_map/ppermute | solution.py:31
  23.8 0.5 collective-permute-start
  24.3 3.1 %collective-permute-done.next_table = s32[8,128]{1,0:T(8,128)S(1)} collective-permute-done((s32[8,128]{1,0:T(8,128)S(1)}, s32[8,128]{1,0:T(8,128)S(1)}, u32[]{:S(2)}, u32[]{:S(2)}) %collective-permute-start) | collective-permute-done | bytes 4128 | tf_op jit(solution)/shard_map/ppermute | solution.py:31
  27.4 1.2 %collective-permute-start.4 = (bf16[2,128,128]{2,1,0:T(8,128)(2,1)S(1)}, bf16[2,128,128]{2,1,0:T(8,128)(2,1)S(1)}, u32[]{:S(2)}, u32[]{:S(2)}) collective-permute-start(bf16[2,128,128]{2,1,0:T(8,128)(2,1)S(1)} %shard_map.47.refs_0_), channel_id=1, source_target_pairs={{0,8},{1,9},{2,10},{3,11},{4,12},{5,13},{6,14},{7,15},{8,0},{9,1},... | collective-permute-start | bytes 196616 | tf_op jit(solution)/shard_map/ppermute | solution.py:31
  28.6 0.0 collective-permute-done.8.refs_6_
  28.6 0.5 collective-permute-start.3
  29.2 0.0 collective-permute-done.6.refs_4_
  29.2 1.5 %collective-permute-start.9 = (bf16[2,128,128]{2,1,0:T(8,128)(2,1)S(1)}, bf16[2,128,128]{2,1,0:T(8,128)(2,1)S(1)}, u32[]{:S(2)}, u32[]{:S(2)}) collective-permute-start(bf16[2,128,128]{2,1,0:T(8,128)(2,1)S(1)} %collective-permute-done.8.refs_6_), channel_id=1, source_target_pairs={{0,4},{1,5},{2,6},{3,7},{4,0},{5,1},{6,2},{7,3},{8,12},{9,13},{10,... | collective-permute-start | bytes 196616 | tf_op jit(solution)/shard_map/ppermute | solution.py:31
  30.7 0.0 collective-permute-done.5.refs_3_
  30.7 0.5 collective-permute-start.7
  31.2 0.1 stack.93.place_ref
  31.3 0.4 collective-permute-done.4.refs_2_
  31.7 1.2 %collective-permute-done.3.refs_1_ = bf16[2,128,128]{2,1,0:T(8,128)(2,1)S(1)} collective-permute-done((bf16[2,128,128]{2,1,0:T(8,128)(2,1)S(1)}, bf16[2,128,128]{2,1,0:T(8,128)(2,1)S(1)}, u32[]{:S(2)}, u32[]{:S(2)}) %collective-permute-start.3) | collective-permute-done | bytes 65568 | tf_op jit(solution)/shard_map/ppermute | solution.py:31
  32.9 0.7 %collective-permute-done.9.refs_7_ = bf16[2,128,128]{2,1,0:T(8,128)(2,1)S(1)} collective-permute-done((bf16[2,128,128]{2,1,0:T(8,128)(2,1)S(1)}, bf16[2,128,128]{2,1,0:T(8,128)(2,1)S(1)}, u32[]{:S(2)}, u32[]{:S(2)}) %collective-permute-start.9) | collective-permute-done | bytes 65568 | tf_op jit(solution)/shard_map/ppermute | solution.py:31
  33.6 1.3 %collective-permute-done.7.refs_5_ = bf16[2,128,128]{2,1,0:T(8,128)(2,1)S(1)} collective-permute-done((bf16[2,128,128]{2,1,0:T(8,128)(2,1)S(1)}, bf16[2,128,128]{2,1,0:T(8,128)(2,1)S(1)}, u32[]{:S(2)}, u32[]{:S(2)}) %collective-permute-start.7) | collective-permute-done | bytes 65568 | tf_op jit(solution)/shard_map/ppermute | solution.py:31
  35.0 0.0 collective-permute-done.1.next_ref
  35.0 2.6 %shard_map.48 = f32[512,256]{1,0:T(8,128)S(1)} custom-call(s32[9]{0:T(128)S(1)} %stack.93.place_ref, s32[8,128]{1,0:T(8,128)S(1)} %get-tuple-element.8.own_table, s32[8,128]{1,0:T(8,128)S(1)} %collective-permute-done.next_table, bf16[8,2,128,128]{3,2,1,0:T(8,128)(2,1)S(1)} %get-tuple-element.9.own_ref, ...), custom_call_target="tpu_custom_call" | custom-call | tf_op jit(solution)/shard_map/pallas_call | solution.py:181
  37.6 0.1 collective-permute-start.10
  37.7 1.9 %collective-permute-done.10 = f32[512,256]{1,0:T(8,128)S(1)} collective-permute-done((f32[512,256]{1,0:T(8,128)S(1)}, f32[512,256]{1,0:T(8,128)S(1)}, u32[]{:S(2)}, u32[]{:S(2)}) %collective-permute-start.10) | collective-permute-done | bytes 524320 | tf_op jit(solution)/shard_map/ppermute | solution.py:31
  39.5 0.1 add_convert_fusion.refs_0_
  39.6 0.6 collective-permute-start.14
  40.2 1.9 %collective-permute-start.12 = (bf16[512,256]{1,0:T(8,128)(2,1)S(1)}, bf16[512,256]{1,0:T(8,128)(2,1)S(1)}, u32[]{:S(2)}, u32[]{:S(2)}) collective-permute-start(bf16[512,256]{1,0:T(8,128)(2,1)S(1)} %add_convert_fusion.refs_0_), channel_id=1, source_target_pairs={{0,0},{1,16},{2,8},{3,24},{4,4},{5,20},{6,12},{7,28},{8,1},{9,17},... | collective-permute-start | bytes 786440 | tf_op jit(solution)/shard_map/ppermute | solution.py:31
  42.2 0.1 collective-permute-start.11
  42.2 7.1 %collective-permute-done.14.refs_3_ = bf16[512,256]{1,0:T(8,128)(2,1)S(1)} collective-permute-done((bf16[512,256]{1,0:T(8,128)(2,1)S(1)}, bf16[512,256]{1,0:T(8,128)(2,1)S(1)}, u32[]{:S(2)}, u32[]{:S(2)}) %collective-permute-start.14) | collective-permute-done | bytes 262176 | tf_op jit(solution)/shard_map/ppermute | solution.py:31
  49.3 0.0 collective-permute-start.15
  49.3 6.1 %collective-permute-done.12.refs_2_ = bf16[512,256]{1,0:T(8,128)(2,1)S(1)} collective-permute-done((bf16[512,256]{1,0:T(8,128)(2,1)S(1)}, bf16[512,256]{1,0:T(8,128)(2,1)S(1)}, u32[]{:S(2)}, u32[]{:S(2)}) %collective-permute-start.12) | collective-permute-done | bytes 262176 | tf_op jit(solution)/shard_map/ppermute | solution.py:31
  55.4 0.1 collective-permute-start.13
  55.4 0.1 stack.83.place_ref
  55.5 0.1 stack.95.place_ref
  55.6 0.0 collective-permute-done.11.refs_1_
  55.7 1.9 %shard_map.49.refs_4_ = bf16[512,1024]{1,0:T(8,128)(2,1)} custom-call(s32[9]{0:T(128)S(1)} %stack.95.place_ref, bf16[512,256]{1,0:T(8,128)(2,1)S(1)} %add_convert_fusion.refs_0_, bf16[512,256]{1,0:T(8,128)(2,1)S(1)} %collective-permute-done.11.refs_1_, bf16[512,256]{1,0:T(8,128)(2,1)S(1)} %collective-permute-done.12.refs_2_, ...), custom_call_target="tpu_custom_call" | custom-call | tf_op jit(solution)/shard_map/pallas_call | solution.py:213
  57.5 0.8 %collective-permute-done.15.refs_3_ = bf16[512,256]{1,0:T(8,128)(2,1)S(1)} collective-permute-done((bf16[512,256]{1,0:T(8,128)(2,1)S(1)}, bf16[512,256]{1,0:T(8,128)(2,1)S(1)}, u32[]{:S(2)}, u32[]{:S(2)}) %collective-permute-start.15) | collective-permute-done | bytes 262176 | tf_op jit(solution)/shard_map/ppermute | solution.py:31
  58.3 5.7 %collective-permute-done.13.refs_2_ = bf16[512,256]{1,0:T(8,128)(2,1)S(1)} collective-permute-done((bf16[512,256]{1,0:T(8,128)(2,1)S(1)}, bf16[512,256]{1,0:T(8,128)(2,1)S(1)}, u32[]{:S(2)}, u32[]{:S(2)}) %collective-permute-start.13) | collective-permute-done | bytes 262176 | tf_op jit(solution)/shard_map/ppermute | solution.py:31
  64.1 1.9 %shard_map.50 = bf16[512,1024]{1,0:T(8,128)(2,1)} custom-call(s32[9]{0:T(128)S(1)} %stack.83.place_ref, bf16[512,256]{1,0:T(8,128)(2,1)S(1)} %add_convert_fusion.refs_0_, bf16[512,256]{1,0:T(8,128)(2,1)S(1)} %collective-permute-done.11.refs_1_, bf16[512,256]{1,0:T(8,128)(2,1)S(1)} %collective-permute-done.13.refs_2_, ...), custom_call_target="tpu_custom_call", output_to_operand_aliasing={{}: (5, {})} | custom-call | tf_op jit(solution)/shard_map/pallas_call | solution.py:213
  (1 shorter events, 0.0 us)
Async XLA Ops:
  0.0 0.7 %copy-start.3 = (s32[8,2]{0,1:T(2,128)S(1)}, s32[8,2]{0,1:T(2,128)}, u32[]{:S(2)}) copy-start(s32[8,2]{0,1:T(2,128)} %param.7) | copy-start | bytes 196
  0.0 0.7 %copy-start.4 = (s32[1,1,8]{2,1,0:T(1,128)S(1)}, s32[1,1,8]{2,1,0:T(1,128)}, u32[]{:S(2)}) copy-start(s32[1,1,8]{2,1,0:T(1,128)} %param.5) | copy-start | bytes 100
  0.7 1.0 %copy-start = (bf16[1,1,8,2,128,128]{5,4,3,2,1,0:T(8,128)(2,1)S(1)}, bf16[1,1,8,2,128,128]{5,4,3,2,1,0:T(8,128)(2,1)}, u32[]{:S(2)}) copy-start(bf16[1,1,8,2,128,128]{5,4,3,2,1,0:T(8,128)(2,1)} %param.4) | copy-start | bytes 1572868
  1.7 0.8 %copy-start.1 = (bf16[128,256]{1,0:T(8,128)(2,1)S(1)}, bf16[128,256]{1,0:T(8,128)(2,1)}, u32[]{:S(2)}) copy-start(bf16[128,256]{1,0:T(8,128)(2,1)} %coeff_ref.1) | copy-start | bytes 196612
  2.6 0.8 %copy-start.2 = (bf16[128,256]{1,0:T(8,128)(2,1)S(1)}, bf16[128,256]{1,0:T(8,128)(2,1)}, u32[]{:S(2)}) copy-start(bf16[128,256]{1,0:T(8,128)(2,1)} %coeff_ref.1) | copy-start | bytes 196612
  3.3 31.6 %collective-permute-start.1 = (bf16[8,2,128,128]{3,2,1,0:T(8,128)(2,1)S(1)}, bf16[8,2,128,128]{3,2,1,0:T(8,128)(2,1)S(1)}, u32[]{:S(2)}, u32[]{:S(2)}) collective-permute-start(bf16[8,2,128,128]{3,2,1,0:T(8,128)(2,1)S(1)} %get-tuple-element.9.own_ref), channel_id=1, source_target_pairs={{0,2},{1,3},{2,0},{3,1},{4,6},{5,7},{6,4},{7,5},{8,10},{9,11},{10,... | collective-permute-start | bytes 1572872 | tf_op jit(solution)/shard_map/ppermute | solution.py:31
  3.4 15.0 %collective-permute-start.2 = (bf16[128,256]{1,0:T(8,128)(2,1)S(1)}, bf16[128,256]{1,0:T(8,128)(2,1)S(1)}, u32[]{:S(2)}, u32[]{:S(2)}) collective-permute-start(bf16[128,256]{1,0:T(8,128)(2,1)S(1)} %copy-done.2), channel_id=1, source_target_pairs={{0,2},{1,3},{2,0},{3,1},{4,6},{5,7},{6,4},{7,5},{8,10},{9,11},{10,... | collective-permute-start | bytes 196616 | tf_op jit(solution)/shard_map/ppermute | solution.py:31
  18.5 10.2 %collective-permute-start.8 = (bf16[2,128,128]{2,1,0:T(8,128)(2,1)S(1)}, bf16[2,128,128]{2,1,0:T(8,128)(2,1)S(1)}, u32[]{:S(2)}, u32[]{:S(2)}) collective-permute-start(bf16[2,128,128]{2,1,0:T(8,128)(2,1)S(1)} %shard_map.47.refs_0_), channel_id=1, source_target_pairs={{0,24},{1,25},{2,26},{3,27},{4,28},{5,29},{6,30},{7,31},{8,16},{9,... | collective-permute-start | bytes 196616 | tf_op jit(solution)/shard_map/ppermute | solution.py:31
  22.1 7.1 %collective-permute-start.6 = (bf16[2,128,128]{2,1,0:T(8,128)(2,1)S(1)}, bf16[2,128,128]{2,1,0:T(8,128)(2,1)S(1)}, u32[]{:S(2)}, u32[]{:S(2)}) collective-permute-start(bf16[2,128,128]{2,1,0:T(8,128)(2,1)S(1)} %shard_map.47.refs_0_), channel_id=1, source_target_pairs={{0,16},{1,17},{2,18},{3,19},{4,20},{5,21},{6,22},{7,23},{8,24},{9,... | collective-permute-start | bytes 196616 | tf_op jit(solution)/shard_map/ppermute | solution.py:31
  22.1 8.6 %collective-permute-start.5 = (bf16[2,128,128]{2,1,0:T(8,128)(2,1)S(1)}, bf16[2,128,128]{2,1,0:T(8,128)(2,1)S(1)}, u32[]{:S(2)}, u32[]{:S(2)}) collective-permute-start(bf16[2,128,128]{2,1,0:T(8,128)(2,1)S(1)} %shard_map.47.refs_0_), channel_id=1, source_target_pairs={{0,12},{1,13},{2,14},{3,15},{4,8},{5,9},{6,10},{7,11},{8,4},{9,5},... | collective-permute-start | bytes 196616 | tf_op jit(solution)/shard_map/ppermute | solution.py:31
  23.8 3.6 %collective-permute-start = (s32[8,128]{1,0:T(8,128)S(1)}, s32[8,128]{1,0:T(8,128)S(1)}, u32[]{:S(2)}, u32[]{:S(2)}) collective-permute-start(s32[8,128]{1,0:T(8,128)S(1)} %get-tuple-element.8.own_table), channel_id=1, source_target_pairs={{0,2},{1,3},{2,0},{3,1},{4,6},{5,7},{6,4},{7,5},{8,10},{9,11},{10,... | collective-permute-start | bytes 12296 | tf_op jit(solution)/shard_map/ppermute | solution.py:31
  27.4 4.3 %collective-permute-start.4 = (bf16[2,128,128]{2,1,0:T(8,128)(2,1)S(1)}, bf16[2,128,128]{2,1,0:T(8,128)(2,1)S(1)}, u32[]{:S(2)}, u32[]{:S(2)}) collective-permute-start(bf16[2,128,128]{2,1,0:T(8,128)(2,1)S(1)} %shard_map.47.refs_0_), channel_id=1, source_target_pairs={{0,8},{1,9},{2,10},{3,11},{4,12},{5,13},{6,14},{7,15},{8,0},{9,1},... | collective-permute-start | bytes 196616 | tf_op jit(solution)/shard_map/ppermute | solution.py:31
  28.6 4.3 %collective-permute-start.3 = (bf16[2,128,128]{2,1,0:T(8,128)(2,1)S(1)}, bf16[2,128,128]{2,1,0:T(8,128)(2,1)S(1)}, u32[]{:S(2)}, u32[]{:S(2)}) collective-permute-start(bf16[2,128,128]{2,1,0:T(8,128)(2,1)S(1)} %shard_map.47.refs_0_), channel_id=1, source_target_pairs={{0,4},{1,5},{2,6},{3,7},{4,0},{5,1},{6,2},{7,3},{8,12},{9,13},{10,... | collective-permute-start | bytes 196616 | tf_op jit(solution)/shard_map/ppermute | solution.py:31
  29.2 4.5 %collective-permute-start.9 = (bf16[2,128,128]{2,1,0:T(8,128)(2,1)S(1)}, bf16[2,128,128]{2,1,0:T(8,128)(2,1)S(1)}, u32[]{:S(2)}, u32[]{:S(2)}) collective-permute-start(bf16[2,128,128]{2,1,0:T(8,128)(2,1)S(1)} %collective-permute-done.8.refs_6_), channel_id=1, source_target_pairs={{0,4},{1,5},{2,6},{3,7},{4,0},{5,1},{6,2},{7,3},{8,12},{9,13},{10,... | collective-permute-start | bytes 196616 | tf_op jit(solution)/shard_map/ppermute | solution.py:31
  30.7 4.3 %collective-permute-start.7 = (bf16[2,128,128]{2,1,0:T(8,128)(2,1)S(1)}, bf16[2,128,128]{2,1,0:T(8,128)(2,1)S(1)}, u32[]{:S(2)}, u32[]{:S(2)}) collective-permute-start(bf16[2,128,128]{2,1,0:T(8,128)(2,1)S(1)} %collective-permute-done.6.refs_4_), channel_id=1, source_target_pairs={{0,4},{1,5},{2,6},{3,7},{4,0},{5,1},{6,2},{7,3},{8,12},{9,13},{10,... | collective-permute-start | bytes 196616 | tf_op jit(solution)/shard_map/ppermute | solution.py:31
  37.6 2.0 %collective-permute-start.10 = (f32[512,256]{1,0:T(8,128)S(1)}, f32[512,256]{1,0:T(8,128)S(1)}, u32[]{:S(2)}, u32[]{:S(2)}) collective-permute-start(f32[512,256]{1,0:T(8,128)S(1)} %shard_map.48), channel_id=1, source_target_pairs={{0,1},{1,0},{2,3},{3,2},{4,5},{5,4},{6,7},{7,6},{8,9},{9,8},{10,11... | collective-permute-start | bytes 1572872 | tf_op jit(solution)/shard_map/ppermute | solution.py:31
  39.6 9.6 %collective-permute-start.14 = (bf16[512,256]{1,0:T(8,128)(2,1)S(1)}, bf16[512,256]{1,0:T(8,128)(2,1)S(1)}, u32[]{:S(2)}, u32[]{:S(2)}) collective-permute-start(bf16[512,256]{1,0:T(8,128)(2,1)S(1)} %add_convert_fusion.refs_0_), channel_id=1, source_target_pairs={{0,8},{1,24},{2,0},{3,16},{4,12},{5,28},{6,4},{7,20},{8,9},{9,25},... | collective-permute-start | bytes 786440 | tf_op jit(solution)/shard_map/ppermute | solution.py:31
  40.2 15.1 %collective-permute-start.12 = (bf16[512,256]{1,0:T(8,128)(2,1)S(1)}, bf16[512,256]{1,0:T(8,128)(2,1)S(1)}, u32[]{:S(2)}, u32[]{:S(2)}) collective-permute-start(bf16[512,256]{1,0:T(8,128)(2,1)S(1)} %add_convert_fusion.refs_0_), channel_id=1, source_target_pairs={{0,0},{1,16},{2,8},{3,24},{4,4},{5,20},{6,12},{7,28},{8,1},{9,17},... | collective-permute-start | bytes 786440 | tf_op jit(solution)/shard_map/ppermute | solution.py:31
  42.2 13.5 %collective-permute-start.11 = (bf16[512,256]{1,0:T(8,128)(2,1)S(1)}, bf16[512,256]{1,0:T(8,128)(2,1)S(1)}, u32[]{:S(2)}, u32[]{:S(2)}) collective-permute-start(bf16[512,256]{1,0:T(8,128)(2,1)S(1)} %add_convert_fusion.refs_0_), channel_id=1, source_target_pairs={{0,2},{1,3},{2,0},{3,1},{4,6},{5,7},{6,4},{7,5},{8,10},{9,11},{10,... | collective-permute-start | bytes 786440 | tf_op jit(solution)/shard_map/ppermute | solution.py:31
  49.3 9.1 %collective-permute-start.15 = (bf16[512,256]{1,0:T(8,128)(2,1)S(1)}, bf16[512,256]{1,0:T(8,128)(2,1)S(1)}, u32[]{:S(2)}, u32[]{:S(2)}) collective-permute-start(bf16[512,256]{1,0:T(8,128)(2,1)S(1)} %collective-permute-done.14.refs_3_), channel_id=1, source_target_pairs={{0,4},{1,5},{2,6},{3,7},{4,0},{5,1},{6,2},{7,3},{8,12},{9,13},{10,... | collective-permute-start | bytes 786440 | tf_op jit(solution)/shard_map/ppermute | solution.py:31
  55.4 8.7 %collective-permute-start.13 = (bf16[512,256]{1,0:T(8,128)(2,1)S(1)}, bf16[512,256]{1,0:T(8,128)(2,1)S(1)}, u32[]{:S(2)}, u32[]{:S(2)}) collective-permute-start(bf16[512,256]{1,0:T(8,128)(2,1)S(1)} %collective-permute-done.12.refs_2_), channel_id=1, source_target_pairs={{0,4},{1,5},{2,6},{3,7},{4,0},{5,1},{6,2},{7,3},{8,12},{9,13},{10,... | collective-permute-start | bytes 786440 | tf_op jit(solution)/shard_map/ppermute | solution.py:31

commit v5 on v4

--- a/solution.py
+++ b/solution.py
@@ -65,8 +65,9 @@
 
 
 def half_kernel(
-    kept_slots, nu_blocks, block, place_ref, own_table, next_table, own_ref, next_ref, *refs
+    kept_slots, nu_blocks, block, places, own_table, next_table, own_ref, next_ref, *refs
 ):
+    place_ref = places()
     pieces, (out_ref, rows_ref) = refs[:-2], refs[-2:]
     rows, part = pieces[0].shape[1:]
     aux = own_ref.shape[1]
@@ -102,7 +103,8 @@
         add(next_table, next_ref, 1, slot)
 
 
-def product_kernel(n_left, scale, place_ref, *refs):
+def product_kernel(n_left, scale, places, *refs):
+    place_ref = places()
     left, right = refs[:n_left], refs[n_left : 2 * n_left]
     out_ref, left_rows, right_rows, tiles, sems = refs[-5:]
     rows = left[0].shape[0]
@@ -138,8 +140,8 @@
     ratio, groups = lay.ratio, lay.groups
     mu_rows, width, part = nu_rows * n_col, aux * occ, occ // 2
     nu_blocks = nu_rows * n_row // block
-    row, col = lax.axis_index("row"), lax.axis_index("col")
-    plane, side, group, chip = row // ratio, row % ratio, col // 4, col // 2 % 2
+    col = lax.axis_index("col")
+    group = col // 4
 
     blocks = three_index.reshape(kept_slots, aux, block, block)
     slots, mask = slot_pair.reshape(kept_slots), occ_mask.T
@@ -167,7 +169,13 @@
         compiler_params=PARAMS,
     )(next_coeff, shared)
 
-    pieces, places = [], []
+    def gather_places():
+        row, col = lax.axis_index("row"), lax.axis_index("col")
+        plane, side = row // ratio, row % ratio
+        starts = [(plane ^ d) * ratio + (side ^ t) for d in range(n_col) for t in range(ratio)]
+        return [(col >> 1 & 1) * part // block] + starts
+
+    pieces = []
     for d in range(n_col):
         held = lay.shift(shared, plane_bits=d) if d else shared
         for t in range(ratio):
@@ -177,15 +185,14 @@
             elif t:
                 here = lay.shift(held, side_bits=t)
             pieces.append(here)
-            places.append((plane ^ d) * ratio + (side ^ t))
     partial = pl.pallas_call(
-        functools.partial(half_kernel, kept_slots, nu_blocks, block),
+        functools.partial(half_kernel, kept_slots, nu_blocks, block, gather_places),
         out_shape=jax.ShapeDtypeStruct((mu_rows, width // 2), jnp.float32),
-        in_specs=[SMEM] * 3 + [VMEM] * (2 + len(pieces)),
+        in_specs=[SMEM] * 2 + [VMEM] * (2 + len(pieces)),
         out_specs=VMEM,
         scratch_shapes=[pltpu.VMEM((2, nu_blocks * block, part), coeff.dtype)],
         compiler_params=PARAMS,
-    )(jnp.stack([chip * part // block] + places), table, next_table, blocks, next_blocks, *pieces)
+    )(table, next_table, blocks, next_blocks, *pieces)
 
     total = partial + lay.shift(partial, col_bits=1)
     rows = mu_rows // groups
@@ -197,25 +204,32 @@
     final = total.astype(jnp.bfloat16)
 
     pieces = 2 * groups
-    left, left_places = [], []
+    left = []
     for e in range(pieces):
         left.append(lay.shift(final, col_bits=2 * e) if e else final)
-        left_places += [(col // 2 ^ e) % 2, (col // 2 ^ e) // 2 * rows]
     sources = [lay.permute(final, lambda z, y, w: (w % 2 * pieces + (w // 2 ^ j), y, z)) for j in range(pieces)]
-    source_places = []
-    for j in range(pieces):
-        source_places += [(plane % pieces ^ j) % 2, (plane % pieces ^ j) // 2 * rows]
+
+    def product_places(t):
+        row, col = lax.axis_index("row"), lax.axis_index("col")
+        plane, side, chips = row // ratio, row % ratio, col >> 1
+        starts = [(side ^ t) * mu_rows]
+        for e in range(pieces):
+            starts += [(chips ^ e) & 1, ((chips ^ e) >> 1) * rows]
+        for j in range(pieces):
+            source = plane % pieces ^ j
+            starts += [source & 1, (source >> 1) * rows]
+        return starts
 
     out = ()
     columns = math.gcd(mu_rows, 256)
     for t in range(ratio):
         right = [lay.shift(piece, side_bits=t) if t else piece for piece in sources]
         out = pl.pallas_call(
-            functools.partial(product_kernel, pieces, 1.0 / math.sqrt(width)),
+            functools.partial(product_kernel, pieces, 1.0 / math.sqrt(width), functools.partial(product_places, t)),
             out_shape=(jax.ShapeDtypeStruct((mu_rows, ratio * mu_rows), jnp.bfloat16),),
-            in_specs=[SMEM] + [VMEM] * (2 * pieces) + [HBM] * len(out),
+            in_specs=[VMEM] * (2 * pieces) + [HBM] * len(out),
             out_specs=(HBM,),
-            input_output_aliases={1 + 2 * pieces: 0} if out else {},
+            input_output_aliases={2 * pieces: 0} if out else {},
             scratch_shapes=[
                 pltpu.VMEM((2, mu_rows, width // 2), jnp.bfloat16),
                 pltpu.VMEM((2, mu_rows, width // 2), jnp.bfloat16),
@@ -223,7 +237,7 @@
                 pltpu.SemaphoreType.DMA((mu_rows // columns,)),
             ],
             compiler_params=PARAMS,
-        )(jnp.stack([(side ^ t) * mu_rows] + left_places + source_places), *left, *right, *out)
+        )(*left, *right, *out)
     return out[0]
 
 

time: 66.2 us -> 65.7 us (level)
  Pallas kernels: 7.07 us -> 6.05 us
  waiting for transfers between devices: 41.4 us -> 42.2 us
    pallas_call x2, Pallas kernels: 3.72 us -> 2.68 us  [exchange(): pl.pallas_call(functools.partial(product_kernel, pieces, 1.0 / math.sqrt(...]
    ppermute x16, waiting for transfers between devices: 41.4 us -> 42.2 us  [permute(): return lax.ppermute(value, ('row', 'col'), pairs)]
  transfers between devices with their start and end apart: 16 -> 16, of which waited for: 11 -> 12; matrix products, arithmetic and copies ran while one was open for 0% -> 0% of each run, Pallas kernels for 3% -> 2%
where the time goes in v5:
time: 65.7 us; the launch traced here: 65.4 us
  waiting for transfers between devices  42.2 us (64%)
  starting transfers between devices  14.4 us (22%)
  Pallas kernels  6.05 us (9%)
  local copies, waits for them, and re-layouts  2.58 us (4%)
    ppermute x16, waiting for transfers between devices, permute(): return lax.ppermute(value, ('row', 'col'), pairs)  42.2 us
    ppermute x16, starting transfers between devices, permute(): return lax.ppermute(value, ('row', 'col'), pairs)  14.4 us
    pallas_call x2, Pallas kernels, exchange(): pl.pallas_call(functools.partial(product_kernel, pieces, 1.0 / math.sqrt(...  2.68 us
    pallas_call x1, Pallas kernels, exchange(): pl.pallas_call(functools.partial(half_kernel, kept_slots, nu_blocks, bloc...  2.63 us
    unnamed x10, local copies, waits for them, and re-layouts  2.58 us
  transfers between devices with their start and end apart: 16, of which 12 were waited for; matrix products, arithmetic and copies ran while one was open for 0% of the time, Pallas kernels for 2%

profile of v5, /device:TPU:2, one launch (start us, length us, event | category | flops | bytes accessed | tf_op | source)
XLA Modules:
  0.0 65.4 jit_solution(3160037255971340059)
XLA Ops:
  0.0 0.0 copy-start.3
  0.0 0.0 copy-start.4
  0.0 0.7 %copy-done.3 = s32[8,2]{0,1:T(2,128)S(1)} copy-done((s32[8,2]{0,1:T(2,128)S(1)}, s32[8,2]{0,1:T(2,128)}, u32[]{:S(2)}) %copy-start.3) | copy-done | bytes 88
  0.7 0.0 copy-done.4
  0.7 0.0 copy-start
  0.7 1.0 %copy-done = bf16[1,1,8,2,128,128]{5,4,3,2,1,0:T(8,128)(2,1)S(1)} copy-done((bf16[1,1,8,2,128,128]{5,4,3,2,1,0:T(8,128)(2,1)S(1)}, bf16[1,1,8,2,128,128]{5,4,3,2,1,0:T(8,128)(2,1)}, u32[]{:S(2)}) %copy-start) | copy-done | bytes 524312
  1.7 0.0 copy-start.1
  1.7 0.8 %copy-done.1 = bf16[128,256]{1,0:T(8,128)(2,1)S(1)} copy-done((bf16[128,256]{1,0:T(8,128)(2,1)S(1)}, bf16[128,256]{1,0:T(8,128)(2,1)}, u32[]{:S(2)}) %copy-start.1) | copy-done | bytes 65560
  2.6 0.0 copy-start.2
  2.6 0.7 %shard_map.46 = (bf16[2,128,128]{2,1,0:T(8,128)(2,1)S(1)}, bf16[8,2,128,128]{3,2,1,0:T(8,128)(2,1)S(1)}, s32[8,128]{1,0:T(8,128)S(1)}) custom-call(s32[8]{0:T(128)S(1)} %bitcast.5, s32[2,8]{1,0:T(2,128)S(1)} %bitcast.4, bf16[128,256]{1,0:T(8,128)(2,1)S(1)} %copy-done.1, bf16[8,2,128,128]{3,2,1,0:T(8,128)(2,1)S(1)} %bitcast.3), custom_call_target="tpu_custom_call" | custom-call | tf_op jit(solution)/shard_map/pallas_call | solution.py:149
  3.3 0.1 collective-permute-start.1
  3.4 0.0 copy-done.2
  3.4 2.0 %collective-permute-start.2 = (bf16[128,256]{1,0:T(8,128)(2,1)S(1)}, bf16[128,256]{1,0:T(8,128)(2,1)S(1)}, u32[]{:S(2)}, u32[]{:S(2)}) collective-permute-start(bf16[128,256]{1,0:T(8,128)(2,1)S(1)} %copy-done.2), channel_id=1, source_target_pairs={{0,2},{1,3},{2,0},{3,1},{4,6},{5,7},{6,4},{7,5},{8,10},{9,11},{10,... | collective-permute-start | bytes 196616 | tf_op jit(solution)/shard_map/ppermute | solution.py:31
  5.4 13.0 %collective-permute-done.2.next_ref = bf16[128,256]{1,0:T(8,128)(2,1)S(1)} collective-permute-done((bf16[128,256]{1,0:T(8,128)(2,1)S(1)}, bf16[128,256]{1,0:T(8,128)(2,1)S(1)}, u32[]{:S(2)}, u32[]{:S(2)}) %collective-permute-start.2) | collective-permute-done | bytes 65568 | tf_op jit(solution)/shard_map/ppermute | solution.py:31
  18.5 3.6 %collective-permute-start.8 = (bf16[2,128,128]{2,1,0:T(8,128)(2,1)S(1)}, bf16[2,128,128]{2,1,0:T(8,128)(2,1)S(1)}, u32[]{:S(2)}, u32[]{:S(2)}) collective-permute-start(bf16[2,128,128]{2,1,0:T(8,128)(2,1)S(1)} %shard_map.47.refs_0_), channel_id=1, source_target_pairs={{0,24},{1,25},{2,26},{3,27},{4,28},{5,29},{6,30},{7,31},{8,16},{9,... | collective-permute-start | bytes 196616 | tf_op jit(solution)/shard_map/ppermute | solution.py:31
  22.1 0.0 collective-permute-start.6
  22.1 1.7 %collective-permute-start.5 = (bf16[2,128,128]{2,1,0:T(8,128)(2,1)S(1)}, bf16[2,128,128]{2,1,0:T(8,128)(2,1)S(1)}, u32[]{:S(2)}, u32[]{:S(2)}) collective-permute-start(bf16[2,128,128]{2,1,0:T(8,128)(2,1)S(1)} %shard_map.47.refs_0_), channel_id=1, source_target_pairs={{0,12},{1,13},{2,14},{3,15},{4,8},{5,9},{6,10},{7,11},{8,4},{9,5},... | collective-permute-start | bytes 196616 | tf_op jit(solution)/shard_map/ppermute | solution.py:31
  23.8 0.5 collective-permute-start
  24.3 3.1 %collective-permute-done.next_table = s32[8,128]{1,0:T(8,128)S(1)} collective-permute-done((s32[8,128]{1,0:T(8,128)S(1)}, s32[8,128]{1,0:T(8,128)S(1)}, u32[]{:S(2)}, u32[]{:S(2)}) %collective-permute-start) | collective-permute-done | bytes 4128 | tf_op jit(solution)/shard_map/ppermute | solution.py:31
  27.4 1.2 %collective-permute-start.4 = (bf16[2,128,128]{2,1,0:T(8,128)(2,1)S(1)}, bf16[2,128,128]{2,1,0:T(8,128)(2,1)S(1)}, u32[]{:S(2)}, u32[]{:S(2)}) collective-permute-start(bf16[2,128,128]{2,1,0:T(8,128)(2,1)S(1)} %shard_map.47.refs_0_), channel_id=1, source_target_pairs={{0,8},{1,9},{2,10},{3,11},{4,12},{5,13},{6,14},{7,15},{8,0},{9,1},... | collective-permute-start | bytes 196616 | tf_op jit(solution)/shard_map/ppermute | solution.py:31
  28.6 0.0 collective-permute-done.8.refs_6_
  28.6 0.5 collective-permute-start.3
  29.2 0.0 collective-permute-done.6.refs_4_
  29.2 1.5 %collective-permute-start.9 = (bf16[2,128,128]{2,1,0:T(8,128)(2,1)S(1)}, bf16[2,128,128]{2,1,0:T(8,128)(2,1)S(1)}, u32[]{:S(2)}, u32[]{:S(2)}) collective-permute-start(bf16[2,128,128]{2,1,0:T(8,128)(2,1)S(1)} %collective-permute-done.8.refs_6_), channel_id=1, source_target_pairs={{0,4},{1,5},{2,6},{3,7},{4,0},{5,1},{6,2},{7,3},{8,12},{9,13},{10,... | collective-permute-start | bytes 196616 | tf_op jit(solution)/shard_map/ppermute | solution.py:31
  30.7 0.0 collective-permute-done.5.refs_3_
  30.7 0.5 collective-permute-start.7
  31.2 0.5 collective-permute-done.4.refs_2_
  31.7 1.2 %collective-permute-done.3.refs_1_ = bf16[2,128,128]{2,1,0:T(8,128)(2,1)S(1)} collective-permute-done((bf16[2,128,128]{2,1,0:T(8,128)(2,1)S(1)}, bf16[2,128,128]{2,1,0:T(8,128)(2,1)S(1)}, u32[]{:S(2)}, u32[]{:S(2)}) %collective-permute-start.3) | collective-permute-done | bytes 65568 | tf_op jit(solution)/shard_map/ppermute | solution.py:31
  32.9 0.7 %collective-permute-done.9.refs_7_ = bf16[2,128,128]{2,1,0:T(8,128)(2,1)S(1)} collective-permute-done((bf16[2,128,128]{2,1,0:T(8,128)(2,1)S(1)}, bf16[2,128,128]{2,1,0:T(8,128)(2,1)S(1)}, u32[]{:S(2)}, u32[]{:S(2)}) %collective-permute-start.9) | collective-permute-done | bytes 65568 | tf_op jit(solution)/shard_map/ppermute | solution.py:31
  33.6 1.3 %collective-permute-done.7.refs_5_ = bf16[2,128,128]{2,1,0:T(8,128)(2,1)S(1)} collective-permute-done((bf16[2,128,128]{2,1,0:T(8,128)(2,1)S(1)}, bf16[2,128,128]{2,1,0:T(8,128)(2,1)S(1)}, u32[]{:S(2)}, u32[]{:S(2)}) %collective-permute-start.7) | collective-permute-done | bytes 65568 | tf_op jit(solution)/shard_map/ppermute | solution.py:31
  35.0 0.0 collective-permute-done.1.next_ref
  35.0 2.6 %shard_map.48 = f32[512,256]{1,0:T(8,128)S(1)} custom-call(s32[8,128]{1,0:T(8,128)S(1)} %get-tuple-element.8.own_table, s32[8,128]{1,0:T(8,128)S(1)} %collective-permute-done.next_table, bf16[8,2,128,128]{3,2,1,0:T(8,128)(2,1)S(1)} %get-tuple-element.9.own_ref, bf16[8,2,128,128]{3,2,1,0:T(8,128)(2,1)S(1)} %collective-permute-done.1.next_ref, ...), custom_call_target="tpu_custom_call" | custom-call | tf_op jit(solution)/shard_map/pallas_call | solution.py:188
  37.6 0.1 collective-permute-start.10
  37.7 1.9 %collective-permute-done.10 = f32[512,256]{1,0:T(8,128)S(1)} collective-permute-done((f32[512,256]{1,0:T(8,128)S(1)}, f32[512,256]{1,0:T(8,128)S(1)}, u32[]{:S(2)}, u32[]{:S(2)}) %collective-permute-start.10) | collective-permute-done | bytes 524320 | tf_op jit(solution)/shard_map/ppermute | solution.py:31
  39.6 0.1 add_convert_fusion.refs_0_
  39.6 0.6 collective-permute-start.14
  40.2 1.9 %collective-permute-start.12 = (bf16[512,256]{1,0:T(8,128)(2,1)S(1)}, bf16[512,256]{1,0:T(8,128)(2,1)S(1)}, u32[]{:S(2)}, u32[]{:S(2)}) collective-permute-start(bf16[512,256]{1,0:T(8,128)(2,1)S(1)} %add_convert_fusion.refs_0_), channel_id=1, source_target_pairs={{0,0},{1,16},{2,8},{3,24},{4,4},{5,20},{6,12},{7,28},{8,1},{9,17},... | collective-permute-start | bytes 786440 | tf_op jit(solution)/shard_map/ppermute | solution.py:31
  42.2 0.1 collective-permute-start.11
  42.2 7.1 %collective-permute-done.14.refs_3_ = bf16[512,256]{1,0:T(8,128)(2,1)S(1)} collective-permute-done((bf16[512,256]{1,0:T(8,128)(2,1)S(1)}, bf16[512,256]{1,0:T(8,128)(2,1)S(1)}, u32[]{:S(2)}, u32[]{:S(2)}) %collective-permute-start.14) | collective-permute-done | bytes 262176 | tf_op jit(solution)/shard_map/ppermute | solution.py:31
  49.3 0.0 collective-permute-start.15
  49.3 6.1 %collective-permute-done.12.refs_2_ = bf16[512,256]{1,0:T(8,128)(2,1)S(1)} collective-permute-done((bf16[512,256]{1,0:T(8,128)(2,1)S(1)}, bf16[512,256]{1,0:T(8,128)(2,1)S(1)}, u32[]{:S(2)}, u32[]{:S(2)}) %collective-permute-start.12) | collective-permute-done | bytes 262176 | tf_op jit(solution)/shard_map/ppermute | solution.py:31
  55.4 0.1 collective-permute-start.13
  55.4 0.2 collective-permute-done.11.refs_1_
  55.7 1.3 %shard_map.49.refs_4_ = bf16[512,1024]{1,0:T(8,128)(2,1)} custom-call(bf16[512,256]{1,0:T(8,128)(2,1)S(1)} %add_convert_fusion.refs_0_, bf16[512,256]{1,0:T(8,128)(2,1)S(1)} %collective-permute-done.11.refs_1_, bf16[512,256]{1,0:T(8,128)(2,1)S(1)} %collective-permute-done.12.refs_2_, bf16[512,256]{1,0:T(8,128)(2,1)S(1)} %collective-permute-done.14.refs_3_), custom_call_target="tpu_custom_call" | custom-call | tf_op jit(solution)/shard_map/pallas_call | solution.py:227
  57.0 1.3 %collective-permute-done.15.refs_3_ = bf16[512,256]{1,0:T(8,128)(2,1)S(1)} collective-permute-done((bf16[512,256]{1,0:T(8,128)(2,1)S(1)}, bf16[512,256]{1,0:T(8,128)(2,1)S(1)}, u32[]{:S(2)}, u32[]{:S(2)}) %collective-permute-start.15) | collective-permute-done | bytes 262176 | tf_op jit(solution)/shard_map/ppermute | solution.py:31
  58.4 5.7 %collective-permute-done.13.refs_2_ = bf16[512,256]{1,0:T(8,128)(2,1)S(1)} collective-permute-done((bf16[512,256]{1,0:T(8,128)(2,1)S(1)}, bf16[512,256]{1,0:T(8,128)(2,1)S(1)}, u32[]{:S(2)}, u32[]{:S(2)}) %collective-permute-start.13) | collective-permute-done | bytes 262176 | tf_op jit(solution)/shard_map/ppermute | solution.py:31
  64.1 1.3 %shard_map.50 = bf16[512,1024]{1,0:T(8,128)(2,1)} custom-call(bf16[512,256]{1,0:T(8,128)(2,1)S(1)} %add_convert_fusion.refs_0_, bf16[512,256]{1,0:T(8,128)(2,1)S(1)} %collective-permute-done.11.refs_1_, bf16[512,256]{1,0:T(8,128)(2,1)S(1)} %collective-permute-done.13.refs_2_, ...), custom_call_target="tpu_custom_call", output_to_operand_aliasing={{}: (4, {})} | custom-call | tf_op jit(solution)/shard_map/pallas_call | solution.py:227
  (1 shorter events, 0.0 us)
Async XLA Ops:
  0.0 0.7 %copy-start.3 = (s32[8,2]{0,1:T(2,128)S(1)}, s32[8,2]{0,1:T(2,128)}, u32[]{:S(2)}) copy-start(s32[8,2]{0,1:T(2,128)} %param.7) | copy-start | bytes 196
  0.0 0.7 %copy-start.4 = (s32[1,1,8]{2,1,0:T(1,128)S(1)}, s32[1,1,8]{2,1,0:T(1,128)}, u32[]{:S(2)}) copy-start(s32[1,1,8]{2,1,0:T(1,128)} %param.5) | copy-start | bytes 100
  0.7 1.0 %copy-start = (bf16[1,1,8,2,128,128]{5,4,3,2,1,0:T(8,128)(2,1)S(1)}, bf16[1,1,8,2,128,128]{5,4,3,2,1,0:T(8,128)(2,1)}, u32[]{:S(2)}) copy-start(bf16[1,1,8,2,128,128]{5,4,3,2,1,0:T(8,128)(2,1)} %param.4) | copy-start | bytes 1572868
  1.7 0.8 %copy-start.1 = (bf16[128,256]{1,0:T(8,128)(2,1)S(1)}, bf16[128,256]{1,0:T(8,128)(2,1)}, u32[]{:S(2)}) copy-start(bf16[128,256]{1,0:T(8,128)(2,1)} %coeff_ref.1) | copy-start | bytes 196612
  2.6 0.8 %copy-start.2 = (bf16[128,256]{1,0:T(8,128)(2,1)S(1)}, bf16[128,256]{1,0:T(8,128)(2,1)}, u32[]{:S(2)}) copy-start(bf16[128,256]{1,0:T(8,128)(2,1)} %coeff_ref.1) | copy-start | bytes 196612
  3.3 31.6 %collective-permute-start.1 = (bf16[8,2,128,128]{3,2,1,0:T(8,128)(2,1)S(1)}, bf16[8,2,128,128]{3,2,1,0:T(8,128)(2,1)S(1)}, u32[]{:S(2)}, u32[]{:S(2)}) collective-permute-start(bf16[8,2,128,128]{3,2,1,0:T(8,128)(2,1)S(1)} %get-tuple-element.9.own_ref), channel_id=1, source_target_pairs={{0,2},{1,3},{2,0},{3,1},{4,6},{5,7},{6,4},{7,5},{8,10},{9,11},{10,... | collective-permute-start | bytes 1572872 | tf_op jit(solution)/shard_map/ppermute | solution.py:31
  3.4 15.0 %collective-permute-start.2 = (bf16[128,256]{1,0:T(8,128)(2,1)S(1)}, bf16[128,256]{1,0:T(8,128)(2,1)S(1)}, u32[]{:S(2)}, u32[]{:S(2)}) collective-permute-start(bf16[128,256]{1,0:T(8,128)(2,1)S(1)} %copy-done.2), channel_id=1, source_target_pairs={{0,2},{1,3},{2,0},{3,1},{4,6},{5,7},{6,4},{7,5},{8,10},{9,11},{10,... | collective-permute-start | bytes 196616 | tf_op jit(solution)/shard_map/ppermute | solution.py:31
  18.5 10.2 %collective-permute-start.8 = (bf16[2,128,128]{2,1,0:T(8,128)(2,1)S(1)}, bf16[2,128,128]{2,1,0:T(8,128)(2,1)S(1)}, u32[]{:S(2)}, u32[]{:S(2)}) collective-permute-start(bf16[2,128,128]{2,1,0:T(8,128)(2,1)S(1)} %shard_map.47.refs_0_), channel_id=1, source_target_pairs={{0,24},{1,25},{2,26},{3,27},{4,28},{5,29},{6,30},{7,31},{8,16},{9,... | collective-permute-start | bytes 196616 | tf_op jit(solution)/shard_map/ppermute | solution.py:31
  22.1 7.1 %collective-permute-start.6 = (bf16[2,128,128]{2,1,0:T(8,128)(2,1)S(1)}, bf16[2,128,128]{2,1,0:T(8,128)(2,1)S(1)}, u32[]{:S(2)}, u32[]{:S(2)}) collective-permute-start(bf16[2,128,128]{2,1,0:T(8,128)(2,1)S(1)} %shard_map.47.refs_0_), channel_id=1, source_target_pairs={{0,16},{1,17},{2,18},{3,19},{4,20},{5,21},{6,22},{7,23},{8,24},{9,... | collective-permute-start | bytes 196616 | tf_op jit(solution)/shard_map/ppermute | solution.py:31
  22.1 8.6 %collective-permute-start.5 = (bf16[2,128,128]{2,1,0:T(8,128)(2,1)S(1)}, bf16[2,128,128]{2,1,0:T(8,128)(2,1)S(1)}, u32[]{:S(2)}, u32[]{:S(2)}) collective-permute-start(bf16[2,128,128]{2,1,0:T(8,128)(2,1)S(1)} %shard_map.47.refs_0_), channel_id=1, source_target_pairs={{0,12},{1,13},{2,14},{3,15},{4,8},{5,9},{6,10},{7,11},{8,4},{9,5},... | collective-permute-start | bytes 196616 | tf_op jit(solution)/shard_map/ppermute | solution.py:31
  23.8 3.6 %collective-permute-start = (s32[8,128]{1,0:T(8,128)S(1)}, s32[8,128]{1,0:T(8,128)S(1)}, u32[]{:S(2)}, u32[]{:S(2)}) collective-permute-start(s32[8,128]{1,0:T(8,128)S(1)} %get-tuple-element.8.own_table), channel_id=1, source_target_pairs={{0,2},{1,3},{2,0},{3,1},{4,6},{5,7},{6,4},{7,5},{8,10},{9,11},{10,... | collective-permute-start | bytes 12296 | tf_op jit(solution)/shard_map/ppermute | solution.py:31
  27.4 4.3 %collective-permute-start.4 = (bf16[2,128,128]{2,1,0:T(8,128)(2,1)S(1)}, bf16[2,128,128]{2,1,0:T(8,128)(2,1)S(1)}, u32[]{:S(2)}, u32[]{:S(2)}) collective-permute-start(bf16[2,128,128]{2,1,0:T(8,128)(2,1)S(1)} %shard_map.47.refs_0_), channel_id=1, source_target_pairs={{0,8},{1,9},{2,10},{3,11},{4,12},{5,13},{6,14},{7,15},{8,0},{9,1},... | collective-permute-start | bytes 196616 | tf_op jit(solution)/shard_map/ppermute | solution.py:31
  28.6 4.3 %collective-permute-start.3 = (bf16[2,128,128]{2,1,0:T(8,128)(2,1)S(1)}, bf16[2,128,128]{2,1,0:T(8,128)(2,1)S(1)}, u32[]{:S(2)}, u32[]{:S(2)}) collective-permute-start(bf16[2,128,128]{2,1,0:T(8,128)(2,1)S(1)} %shard_map.47.refs_0_), channel_id=1, source_target_pairs={{0,4},{1,5},{2,6},{3,7},{4,0},{5,1},{6,2},{7,3},{8,12},{9,13},{10,... | collective-permute-start | bytes 196616 | tf_op jit(solution)/shard_map/ppermute | solution.py:31
  29.2 4.5 %collective-permute-start.9 = (bf16[2,128,128]{2,1,0:T(8,128)(2,1)S(1)}, bf16[2,128,128]{2,1,0:T(8,128)(2,1)S(1)}, u32[]{:S(2)}, u32[]{:S(2)}) collective-permute-start(bf16[2,128,128]{2,1,0:T(8,128)(2,1)S(1)} %collective-permute-done.8.refs_6_), channel_id=1, source_target_pairs={{0,4},{1,5},{2,6},{3,7},{4,0},{5,1},{6,2},{7,3},{8,12},{9,13},{10,... | collective-permute-start | bytes 196616 | tf_op jit(solution)/shard_map/ppermute | solution.py:31
  30.7 4.3 %collective-permute-start.7 = (bf16[2,128,128]{2,1,0:T(8,128)(2,1)S(1)}, bf16[2,128,128]{2,1,0:T(8,128)(2,1)S(1)}, u32[]{:S(2)}, u32[]{:S(2)}) collective-permute-start(bf16[2,128,128]{2,1,0:T(8,128)(2,1)S(1)} %collective-permute-done.6.refs_4_), channel_id=1, source_target_pairs={{0,4},{1,5},{2,6},{3,7},{4,0},{5,1},{6,2},{7,3},{8,12},{9,13},{10,... | collective-permute-start | bytes 196616 | tf_op jit(solution)/shard_map/ppermute | solution.py:31
  37.6 2.0 %collective-permute-start.10 = (f32[512,256]{1,0:T(8,128)S(1)}, f32[512,256]{1,0:T(8,128)S(1)}, u32[]{:S(2)}, u32[]{:S(2)}) collective-permute-start(f32[512,256]{1,0:T(8,128)S(1)} %shard_map.48), channel_id=1, source_target_pairs={{0,1},{1,0},{2,3},{3,2},{4,5},{5,4},{6,7},{7,6},{8,9},{9,8},{10,11... | collective-permute-start | bytes 1572872 | tf_op jit(solution)/shard_map/ppermute | solution.py:31
  39.6 9.6 %collective-permute-start.14 = (bf16[512,256]{1,0:T(8,128)(2,1)S(1)}, bf16[512,256]{1,0:T(8,128)(2,1)S(1)}, u32[]{:S(2)}, u32[]{:S(2)}) collective-permute-start(bf16[512,256]{1,0:T(8,128)(2,1)S(1)} %add_convert_fusion.refs_0_), channel_id=1, source_target_pairs={{0,8},{1,24},{2,0},{3,16},{4,12},{5,28},{6,4},{7,20},{8,9},{9,25},... | collective-permute-start | bytes 786440 | tf_op jit(solution)/shard_map/ppermute | solution.py:31
  40.2 15.1 %collective-permute-start.12 = (bf16[512,256]{1,0:T(8,128)(2,1)S(1)}, bf16[512,256]{1,0:T(8,128)(2,1)S(1)}, u32[]{:S(2)}, u32[]{:S(2)}) collective-permute-start(bf16[512,256]{1,0:T(8,128)(2,1)S(1)} %add_convert_fusion.refs_0_), channel_id=1, source_target_pairs={{0,0},{1,16},{2,8},{3,24},{4,4},{5,20},{6,12},{7,28},{8,1},{9,17},... | collective-permute-start | bytes 786440 | tf_op jit(solution)/shard_map/ppermute | solution.py:31
  42.2 13.5 %collective-permute-start.11 = (bf16[512,256]{1,0:T(8,128)(2,1)S(1)}, bf16[512,256]{1,0:T(8,128)(2,1)S(1)}, u32[]{:S(2)}, u32[]{:S(2)}) collective-permute-start(bf16[512,256]{1,0:T(8,128)(2,1)S(1)} %add_convert_fusion.refs_0_), channel_id=1, source_target_pairs={{0,2},{1,3},{2,0},{3,1},{4,6},{5,7},{6,4},{7,5},{8,10},{9,11},{10,... | collective-permute-start | bytes 786440 | tf_op jit(solution)/shard_map/ppermute | solution.py:31
  49.3 9.1 %collective-permute-start.15 = (bf16[512,256]{1,0:T(8,128)(2,1)S(1)}, bf16[512,256]{1,0:T(8,128)(2,1)S(1)}, u32[]{:S(2)}, u32[]{:S(2)}) collective-permute-start(bf16[512,256]{1,0:T(8,128)(2,1)S(1)} %collective-permute-done.14.refs_3_), channel_id=1, source_target_pairs={{0,4},{1,5},{2,6},{3,7},{4,0},{5,1},{6,2},{7,3},{8,12},{9,13},{10,... | collective-permute-start | bytes 786440 | tf_op jit(solution)/shard_map/ppermute | solution.py:31
  55.4 8.7 %collective-permute-start.13 = (bf16[512,256]{1,0:T(8,128)(2,1)S(1)}, bf16[512,256]{1,0:T(8,128)(2,1)S(1)}, u32[]{:S(2)}, u32[]{:S(2)}) collective-permute-start(bf16[512,256]{1,0:T(8,128)(2,1)S(1)} %collective-permute-done.12.refs_2_), channel_id=1, source_target_pairs={{0,4},{1,5},{2,6},{3,7},{4,0},{5,1},{6,2},{7,3},{8,12},{9,13},{10,... | collective-permute-start | bytes 786440 | tf_op jit(solution)/shard_map/ppermute | solution.py:31
